TPU v7x, 32 devices: a whole 2x2x4 slice. The times are simulated.
32 devices in a mesh: row: 8 (over z, x), col: 4 (over y, core).
Axes of the slice: x: 2, y: 2, z: 4, core: 2. Of those that a mesh axis runs over, the one named last changes fastest.
Arguments:
- start_vector: float32 [12288, 12288], P('row', 'col'), may hold values from -6 to 6, as said below
- ham_blocks: bfloat16 [384, 128, 128], P('row'), may hold values from -0.1875 to 0.1875
- diagonal: float32 [12288], replicated, may hold values from -1 to 1
- pair_lists: int32 [3, 8, 64], replicated, may hold values from 0 to 47, as said below
- pair_counts: int32 [8], replicated, may hold values from 16 to 64, as said below
- hot_blocks: int32 [8, 2], replicated, may hold values from 0 to 11, as said below
- selection: int32 [8, 8], replicated, may hold values from 0 to 1
Outputs:
- first_iterate: float32 [12288, 12288], P('row', 'col')
- second_iterate: float32 [12288, 12288], P('row', 'col')
Inputs may be any that keep to these rules, and one draw needn't show every extreme that they name: start_vector is symmetric: entry (a, b) equals entry (b, a). `pair_lists`: component 0 is a tile (0 to 7), component 1 a block of a tile (0 to 11), component 2 a block id (0 to 47); slot k < 8 of every list has source tile k. `pair_counts`: some tile has all 64 slots live. `hot_blocks`: the 2 blocks of a tile are distinct.
All inputs are finite; a program needn't handle non-finite values.
Results may differ from a plain program's by a relative error of at most 0.0023.
Values may be sent and summed in bfloat16 or wider, within the bound.
A program may use at most 320 MiB of HBM per device.

v0:
```python
import functools

import jax
import jax.numpy as jnp
from jax import lax
from jax.experimental import pallas as pl
from jax.experimental.pallas import tpu as pltpu
from jax.sharding import PartitionSpec as P

center = 0.25
half_width = 2.5
VMEM_LIMIT = 60 * 1024 * 1024


def dense_kernel(transposed, tiles, pairs, counts, ham_ref, out_ref, acc):
    tile = tiles[pl.program_id(0)]
    tile_count = counts.shape[0]
    slots = pairs.shape[0] // (3 * tile_count)
    size = ham_ref.shape[-1]
    acc[...] = jnp.zeros_like(acc)

    def add(slot, carry):
        at = tile * slots + slot
        source = pl.multiple_of(pairs[at] * size, size)
        target = pl.multiple_of(pairs[tile_count * slots + at] * size, size)
        block = ham_ref[0, pairs[2 * tile_count * slots + at]].astype(jnp.float32)
        if transposed:
            acc[pl.ds(source, size), pl.ds(target, size)] += block.T
        else:
            acc[pl.ds(target, size), pl.ds(source, size)] += block
        return carry

    lax.fori_loop(0, counts[tile], add, 0)
    out_ref[0] = acc[...].astype(out_ref.dtype)


def dense(hams, tiles, pairs, counts, shape, transposed):
    grid_spec = pltpu.PrefetchScalarGridSpec(
        num_scalar_prefetch=3,
        grid=(hams.shape[0],),
        in_specs=[pl.BlockSpec((1,) + hams.shape[1:], lambda i, *_: (i, 0, 0, 0))],
        out_specs=pl.BlockSpec((1,) + shape, lambda i, *_: (i, 0, 0)),
        scratch_shapes=[pltpu.VMEM(shape, jnp.float32)],
    )
    return pl.pallas_call(
        functools.partial(dense_kernel, transposed),
        out_shape=jax.ShapeDtypeStruct((hams.shape[0],) + shape, jnp.bfloat16),
        grid_spec=grid_spec,
        compiler_params=pltpu.CompilerParams(vmem_limit_bytes=VMEM_LIMIT),
    )(tiles, pairs, counts, hams)


def round_kernel(place, hot, sel, x_ref, out_ref):
    out_ref[0] = x_ref[...].astype(out_ref.dtype)


def gather_rows(x, place, hot, sel, row_count, size):
    width = x.shape[1]
    hot_count = hot.shape[0] // row_count

    def pick(p, place, hot, sel):
        p = jnp.minimum(p, row_count - 1)
        return (hot[place[0] * hot_count + sel[p * row_count + place[0]]], 0)

    grid_spec = pltpu.PrefetchScalarGridSpec(
        num_scalar_prefetch=3,
        grid=(row_count,),
        in_specs=[pl.BlockSpec((size, width), pick)],
        out_specs=pl.BlockSpec((1, size, width), lambda p, *_: (p, 0, 0)),
    )
    return pl.pallas_call(
        round_kernel,
        out_shape=jax.ShapeDtypeStruct((row_count, size, width), jnp.bfloat16),
        grid_spec=grid_spec,
    )(place, hot, sel, x)


def gather_cols(x, place, hot, sel, row_count, ratio, size):
    height = x.shape[0]
    hot_count = hot.shape[0] // row_count
    blocks = x.shape[1] // (ratio * size)

    def pick(n, place, hot, sel):
        n = jnp.minimum(n, ratio * hot_count - 1)
        tile, which = n // hot_count, n % hot_count
        return (0, tile * blocks + hot[(place[1] * ratio + tile) * hot_count + which])

    grid_spec = pltpu.PrefetchScalarGridSpec(
        num_scalar_prefetch=3,
        grid=(ratio * hot_count,),
        in_specs=[pl.BlockSpec((height, size), pick)],
        out_specs=pl.BlockSpec((1, height, size), lambda n, *_: (n, 0, 0)),
    )
    return pl.pallas_call(
        round_kernel,
        out_shape=jax.ShapeDtypeStruct((ratio * hot_count, height, size), jnp.bfloat16),
        grid_spec=grid_spec,
    )(place, hot, sel, x)


def spread_hams(ham, row_n, col_n):
    ratio = row_n // col_n
    side = lax.rem(lax.axis_index("row"), ratio)
    group = lax.axis_index("row") // ratio
    dist = lax.rem(group - lax.axis_index("col") + col_n, col_n)
    bwd = (col_n - 1) // 2
    fwd = col_n - 1 - bwd

    def device(group, side, col):
        return ((group % col_n) * ratio + side) * col_n + col

    held = ham
    for way, count in ((1, fwd), (-1, bwd)):
        moving = ham
        for step in range(count):
            links = [(device(col + way * step, s, col), device(col + way * (step + 1), s, col))
                     for col in range(col_n) for s in range(ratio)]
            moving = lax.ppermute(moving, ("row", "col"), links)
            held = jnp.where(dist == (way * (step + 1)) % col_n, moving, held)
    pieces = [held]
    for m in range(1, ratio):
        links = [(device(g, s, col), device(g, (s + m) % ratio, col))
                 for g in range(col_n) for col in range(col_n) for s in range(ratio)]
        pieces.append(lax.ppermute(held, ("row", "col"), links))
    order = lax.rem(side - jnp.arange(ratio) + ratio, ratio)
    return jnp.take(jnp.stack(pieces), order, axis=0)


def exchange(rows_in, cols_in):
    rows = lax.all_to_all(rows_in, "row", split_axis=0, concat_axis=0, tiled=True)
    return rows, lax.all_gather(cols_in, "col")


def filter_kernel(source_count, row_chunk, last, place, sel, wa_ref, s_ref, wb_ref, rd_ref, cd_ref, *refs):
    b_refs = refs[:source_count]
    rest = refs[source_count:]
    if last:
        x_ref, start_ref, out_ref = rest
    else:
        x_ref, out_ref = rest

    def chunk(i, carry):
        rows = pl.ds(pl.multiple_of(i * row_chunk, row_chunk), row_chunk)
        beta = jnp.concatenate([b[0, rows, :] for b in b_refs], axis=1)
        acc = jnp.dot(wa_ref[rows, :], s_ref[...], preferred_element_type=jnp.float32)
        acc = acc + jnp.dot(beta, wb_ref[0], preferred_element_type=jnp.float32)
        x = x_ref[rows, :]
        acc = acc + (rd_ref[rows, :] + cd_ref[...] - center) * x
        if last:
            out_ref[rows, :] = acc * (2.0 / half_width) - start_ref[rows, :]
        else:
            out_ref[rows, :] = acc * (1.0 / half_width)
        return carry

    lax.fori_loop(0, x_ref.shape[0] // row_chunk, chunk, 0)


def filter_step(place, sel, wa, s, wb, rd, cd, cols, x, start, row_n, ratio):
    height, width = x.shape
    size = cols.shape[-1]
    hot_count = cols.shape[0] // row_n
    tile_width = width // ratio
    stripe = 256 if tile_width % 256 == 0 else size
    per_tile = tile_width // stripe
    row_chunk = height // 3 if height % 384 == 0 else size
    last = start is not None

    def b_spec(q):
        return pl.BlockSpec(
            (1, height, size),
            lambda n, place, sel: (q * hot_count + sel[(place[1] * ratio + jnp.minimum(n // per_tile, ratio - 1)) * row_n + q], 0, 0))

    striped = pl.BlockSpec((height, stripe), lambda n, *_: (0, n))
    in_specs = [
        pl.BlockSpec(wa.shape, lambda n, *_: (0, 0)),
        pl.BlockSpec((s.shape[0], stripe), lambda n, *_: (0, n)),
        pl.BlockSpec((1, wb.shape[1], stripe), lambda n, *_: (n // per_tile, 0, n % per_tile)),
        pl.BlockSpec((height, 1), lambda n, *_: (0, 0)),
        pl.BlockSpec((1, stripe), lambda n, *_: (0, n)),
    ] + [b_spec(q) for q in range(row_n)] + [striped] * (2 if last else 1)
    args = [wa, s, wb, rd, cd] + [cols] * row_n + [x] + ([start] if last else [])
    grid_spec = pltpu.PrefetchScalarGridSpec(
        num_scalar_prefetch=2, grid=(width // stripe,), in_specs=in_specs, out_specs=striped)
    return pl.pallas_call(
        functools.partial(filter_kernel, row_n, row_chunk, last),
        out_shape=jax.ShapeDtypeStruct(x.shape, jnp.float32),
        grid_spec=grid_spec,
        compiler_params=pltpu.CompilerParams(vmem_limit_bytes=VMEM_LIMIT),
    )(place, sel, *args)


def body(start_vector, ham_blocks, diagonal, pair_lists, pair_counts, hot_blocks, selection):
    row_n = lax.axis_size("row")
    col_n = lax.axis_size("col")
    ratio = row_n // col_n
    height, width = start_vector.shape
    size = ham_blocks.shape[1]
    row_index = lax.axis_index("row")
    col_index = lax.axis_index("col")
    place = jnp.stack([row_index, col_index]).astype(jnp.int32)
    pairs = pair_lists.reshape(-1)
    hot = hot_blocks.reshape(-1)
    sel = selection.reshape(-1)
    rd = lax.dynamic_slice_in_dim(diagonal, row_index * height, height)[:, None]
    cd = lax.dynamic_slice_in_dim(diagonal, col_index * width, width)[None, :]
    depth = row_n * size

    def sources(x):
        rows = gather_rows(x, place, hot, sel, row_n, size)
        cols = gather_cols(x, place, hot, sel, row_n, ratio, size)
        return rows, cols

    def joined(rows, cols):
        return rows.reshape(depth, width), cols.reshape((-1,) + cols.shape[2:])

    rows, cols = exchange(*sources(start_vector))
    hams = spread_hams(ham_blocks, row_n, col_n)
    wa = dense(ham_blocks[None], place[:1], pairs, pair_counts, (height, depth), False)[0]
    mirrors = (col_index * ratio + jnp.arange(ratio)).astype(jnp.int32)
    wb = dense(hams, mirrors, pairs, pair_counts, (depth, width // ratio), True)
    s, b = joined(rows, cols)
    first = filter_step(place, sel, wa, s, wb, rd, cd, b, start_vector, None, row_n, ratio)
    s, b = joined(*exchange(*sources(first)))
    second = filter_step(place, sel, wa, s, wb, rd, cd, b, first, start_vector, row_n, ratio)
    return (first, second)


def solution(mesh):
    in_specs = (P("row", "col"), P("row", None, None), P(), P(), P(), P(), P())
    out_specs = (P("row", "col"), P("row", "col"))
    return jax.shard_map(body, mesh=mesh, in_specs=in_specs, out_specs=out_specs, check_vma=False)
```

profile of v0, /device:TPU:24, one launch (start us, length us, event | category | flops | bytes accessed | tf_op | source)
XLA Modules:
  0.0 497.0 jit_solution(4224378967195216840)
XLA Ops:
  7.2 1.3 reshape.67.sel
  8.5 0.8 copy.13
  9.3 0.7 reshape.69.hot
  9.9 0.6 pad_add_fusion.place
  10.6 9.9 %shard_map.87 = bf16[8,128,3072]{2,1,0:T(8,128)(2,1)} custom-call(s32[2]{0:T(128)} %pad_add_fusion.place, s32[16]{0:T(128)} %reshape.69.hot, s32[64]{0:T(128)} %reshape.67.sel, f32[1536,3072]{1,0:T(8,128)} %refs_9_.1), custom_call_target="tpu_custom_call" | custom-call | tf_op jit(solution)/shard_map/pallas_call | solution.py:71
  20.4 6.1 %all-to-all-start = ((bf16[8,128,3072]{2,1,0:T(8,128)(2,1)}), bf16[8,128,3072]{2,1,0:T(8,128)(2,1)}, u32[]{:S(2)}, u32[]{:S(2)}) async-start(bf16[8,128,3072]{2,1,0:T(8,128)(2,1)} %shard_map.87), calls=%async_computation | async-start | bytes 12582912 | tf_op jit(solution)/shard_map/all_to_all | solution.py:130
  26.6 0.0 copy-start
  26.6 0.0 all-gather.5.cloned.1.call-start
  26.6 4.8 shard_map.89
  31.4 0.0 all-gather.5.cloned.1.call-update
  31.4 0.0 copy-done
  31.4 0.8 collective-permute-start.1
  32.2 1.3 collective-permute-start
  33.5 0.0 collective-permute-done.1
  33.5 0.0 copy-start.2
  33.5 1.8 collective-permute-start.2
  35.3 0.0 copy-start.4
  35.3 128.0 %collective-permute-done = bf16[48,128,128]{2,1,0:T(8,128)(2,1)} collective-permute-done((bf16[48,128,128]{2,1,0:T(8,128)(2,1)S(1)}, bf16[48,128,128]{2,1,0:T(8,128)(2,1)}, u32[]{:S(2)}, u32[]{:S(2)}) %collective-permute-start) | collective-permute-done | bytes 1572896 | tf_op jit(solution)/shard_map/ppermute | solution.py:118
  163.3 0.0 copy-done.2
  163.3 0.0 collective-permute-done.2
  163.3 1.7 select_select_fusion
  165.0 0.0 copy-start.1
  165.0 1.3 collective-permute-start.3
  166.3 0.0 copy-done.4
  166.3 0.7 reshape.68.pairs
  167.0 0.8 dynamic_slice.6
  167.8 1.3 dynamic_slice.7
  169.1 1.1 broadcast_in_dim.24.rd_ref
  170.2 4.8 shard_map.86
  175.1 0.6 iota_add_fusion.tiles
  175.7 9.8 %collective-permute-done.3 = bf16[48,128,128]{2,1,0:T(8,128)(2,1)S(1)} collective-permute-done((bf16[48,128,128]{2,1,0:T(8,128)(2,1)S(1)}, bf16[48,128,128]{2,1,0:T(8,128)(2,1)S(1)}, u32[]{:S(2)}, u32[]{:S(2)}) %collective-permute-start.3) | collective-permute-done | bytes 1572896 | tf_op jit(solution)/shard_map/ppermute | solution.py:124
  185.5 0.0 copy-start.3
  185.5 0.0 copy-done.1
  185.5 1.1 copy-done.3
  186.7 2.2 pad_maximum_fusion
  188.8 2.6 gather_fusion
  191.5 3.9 broadcast_select_fusion.ham_ref
  195.4 9.2 %shard_map.88.wb_ref = bf16[2,1024,1536]{2,1,0:T(8,128)(2,1)} custom-call(s32[2]{0:T(128)} %iota_add_fusion.tiles, s32[1536]{0:T(1024)} %reshape.68.pairs, s32[8]{0:T(128)} %counts.3, bf16[2,48,128,128]{3,2,1,0:T(8,128)(2,1)} %broadcast_select_fusion.ham_ref), custom_call_target="tpu_custom_call" | custom-call | tf_op jit(solution)/shard_map/pallas_call | solution.py:45
  204.5 0.0 all-gather.5.cloned.1.call-done.refs_0_.refs_1_.refs_2_.refs_3_.refs_4_.refs_5_.refs_6_.refs_7_
  204.5 0.0 all-to-all-done
  204.5 34.5 %shard_map.90.x_ref.refs_8_ = f32[1536,3072]{1,0:T(8,128)} custom-call(s32[2]{0:T(128)} %pad_add_fusion.place, s32[64]{0:T(128)} %reshape.67.sel, bf16[1536,1024]{1,0:T(8,128)(2,1)} %bitcast.11, bf16[1024,3072]{1,0:T(8,128)(2,1)} %bitcast.4.s_ref, bf16[2,1024,1536]{2,1,0:T(8,128)(2,1)} %shard_map.88.wb_ref, f32[1536,1]{1,0:T(8,128)} %broadcast_in_dim.24.rd_ref, ...), custom_call_target="tpu_custom_call" | custom-call | tf_op jit(solution)/shard_map/pallas_call | solution.py:184
  239.0 9.9 %shard_map.91 = bf16[8,128,3072]{2,1,0:T(8,128)(2,1)} custom-call(s32[2]{0:T(128)} %pad_add_fusion.place, s32[16]{0:T(128)} %reshape.69.hot, s32[64]{0:T(128)} %reshape.67.sel, f32[1536,3072]{1,0:T(8,128)} %shard_map.90.x_ref.refs_8_), custom_call_target="tpu_custom_call" | custom-call | tf_op jit(solution)/shard_map/pallas_call | solution.py:71
  248.9 66.8 %all-to-all-start.1 = ((bf16[8,128,3072]{2,1,0:T(8,128)(2,1)}), bf16[8,128,3072]{2,1,0:T(8,128)(2,1)}, u32[]{:S(2)}, u32[]{:S(2)}) async-start(bf16[8,128,3072]{2,1,0:T(8,128)(2,1)} %shard_map.91), calls=%async_computation.1 | async-start | bytes 12582912 | tf_op jit(solution)/shard_map/all_to_all | solution.py:130
  315.7 0.0 all-gather.7.cloned.1.call-start
  315.7 4.7 shard_map.92
  320.4 0.0 all-gather.7.cloned.1.call-update
  320.4 52.3 %all-gather.7.cloned.1.call-done.refs_0_.refs_1_.refs_2_.refs_3_.refs_4_.refs_5_.refs_6_.refs_7_ = bf16[16,1536,128]{2,1,0:T(8,128)(2,1)} async-done(((bf16[4,1536,128]{2,1,0:T(8,128)(2,1)}), bf16[16,1536,128]{2,1,0:T(8,128)(2,1)}) %all-gather.7.cloned.1.call-update) | async-done | bytes 6291472 | tf_op jit(solution)/shard_map/all_gather | solution.py:131
  372.7 81.0 %all-to-all-done.1 = bf16[8,128,3072]{2,1,0:T(8,128)(2,1)} async-done(((bf16[8,128,3072]{2,1,0:T(8,128)(2,1)}), bf16[8,128,3072]{2,1,0:T(8,128)(2,1)}, u32[]{:S(2)}, u32[]{:S(2)}) %all-to-all-start.1) | async-done | bytes 6291488 | tf_op jit(solution)/shard_map/all_to_all | solution.py:130
  453.8 36.4 %shard_map.93 = f32[1536,3072]{1,0:T(8,128)} custom-call(s32[2]{0:T(128)} %pad_add_fusion.place, s32[64]{0:T(128)} %reshape.67.sel, bf16[1536,1024]{1,0:T(8,128)(2,1)} %bitcast.12, bf16[1024,3072]{1,0:T(8,128)(2,1)} %bitcast.9.s_ref, bf16[2,1024,1536]{2,1,0:T(8,128)(2,1)} %shard_map.88.wb_ref, f32[1536,1]{1,0:T(8,128)} %broadcast_in_dim.24.rd_ref, ...), custom_call_target="tpu_custom_call" | custom-call | tf_op jit(solution)/shard_map/pallas_call | solution.py:184
  (3 shorter events, 0.0 us)
Async XLA Ops:
  20.4 184.1 %all-to-all-start = ((bf16[8,128,3072]{2,1,0:T(8,128)(2,1)}), bf16[8,128,3072]{2,1,0:T(8,128)(2,1)}, u32[]{:S(2)}, u32[]{:S(2)}) async-start(bf16[8,128,3072]{2,1,0:T(8,128)(2,1)} %shard_map.87), calls=%async_computation | async-start | bytes 12582912 | tf_op jit(solution)/shard_map/all_to_all | solution.py:130
  26.6 4.8 copy-start
  26.6 178.0 %all-gather.5.cloned.1.call-start = ((), (), s32[]{:S(2)}) async-start(), calls=%async_computation.2 | async-start | bytes 7864320 | tf_op jit(solution)/shard_map/all_gather | solution.py:131
  31.4 2.1 collective-permute-start.1
  32.2 131.2 %collective-permute-start = (bf16[48,128,128]{2,1,0:T(8,128)(2,1)S(1)}, bf16[48,128,128]{2,1,0:T(8,128)(2,1)}, u32[]{:S(2)}, u32[]{:S(2)}) collective-permute-start(bf16[48,128,128]{2,1,0:T(8,128)(2,1)S(1)} %copy-done), channel_id=1, source_target_pairs={{0,24},{4,28},{9,1},{13,5},{18,10},{22,14},{27,19},{31,23}} | collective-permute-start | bytes 4718600 | tf_op jit(solution)/shard_map/ppermute | solution.py:118
  33.5 129.9 %copy-start.2 = (bf16[48,128,128]{2,1,0:T(8,128)(2,1)}, bf16[48,128,128]{2,1,0:T(8,128)(2,1)S(1)}, u32[]{:S(2)}) copy-start(bf16[48,128,128]{2,1,0:T(8,128)(2,1)S(1)} %collective-permute-done.1) | copy-start | bytes 4718596
  33.5 129.9 %collective-permute-start.2 = (bf16[48,128,128]{2,1,0:T(8,128)(2,1)S(1)}, bf16[48,128,128]{2,1,0:T(8,128)(2,1)}, u32[]{:S(2)}, u32[]{:S(2)}) collective-permute-start(bf16[48,128,128]{2,1,0:T(8,128)(2,1)S(1)} %collective-permute-done.1), channel_id=1, source_target_pairs={{8,16},{12,20},{17,25},{21,29},{26,2},{30,6},{3,11},{7,15}} | collective-permute-start | bytes 4718600 | tf_op jit(solution)/shard_map/ppermute | solution.py:118
  35.3 131.0 %copy-start.4 = (s32[3,8,64]{2,1,0:T(8,128)S(1)}, s32[3,8,64]{2,1,0:T(8,128)}, u32[]{:S(2)}) copy-start(s32[3,8,64]{2,1,0:T(8,128)} %param.10) | copy-start | bytes 18436
  165.0 20.5 %copy-start.1 = (bf16[48,128,128]{2,1,0:T(8,128)(2,1)}, bf16[48,128,128]{2,1,0:T(8,128)(2,1)S(1)}, u32[]{:S(2)}) copy-start(bf16[48,128,128]{2,1,0:T(8,128)(2,1)S(1)} %select_select_fusion) | copy-start | bytes 4718596
  165.0 20.5 %collective-permute-start.3 = (bf16[48,128,128]{2,1,0:T(8,128)(2,1)S(1)}, bf16[48,128,128]{2,1,0:T(8,128)(2,1)S(1)}, u32[]{:S(2)}, u32[]{:S(2)}) collective-permute-start(bf16[48,128,128]{2,1,0:T(8,128)(2,1)S(1)} %select_select_fusion), channel_id=1, source_target_pairs={{0,4},{4,0},{1,5},{5,1},{2,6},{6,2},{3,7},{7,3},{8,12},{12,8},{9,1... | collective-permute-start | bytes 4718600 | tf_op jit(solution)/shard_map/ppermute | solution.py:124
  185.5 1.1 copy-start.3
  248.9 204.9 %all-to-all-start.1 = ((bf16[8,128,3072]{2,1,0:T(8,128)(2,1)}), bf16[8,128,3072]{2,1,0:T(8,128)(2,1)}, u32[]{:S(2)}, u32[]{:S(2)}) async-start(bf16[8,128,3072]{2,1,0:T(8,128)(2,1)} %shard_map.91), calls=%async_computation.1 | async-start | bytes 12582912 | tf_op jit(solution)/shard_map/all_to_all | solution.py:130
  315.7 57.0 %all-gather.7.cloned.1.call-start = ((), (), s32[]{:S(2)}) async-start(), calls=%async_computation.3 | async-start | bytes 7864320 | tf_op jit(solution)/shard_map/all_gather | solution.py:131
Sparse Core Ops, SparseCore 0:
  31.5 47.2 all-gather.4
  320.5 52.1 all-gather.6
where the time goes:
time: 500 us; the launch traced here: 497 us
  waiting for transfers between devices  271 us (54%)
  Pallas kernels  114 us (23%)
  starting transfers between devices  78.1 us (16%)
  between operations  14.1 us (3%)
  local copies, waits for them, and re-layouts  10.4 us (2%)
  other arithmetic  9.03 us (2%)
    ppermute x3, waiting for transfers between devices, spread_hams(): moving = lax.ppermute(moving, ('row', 'col'), links)  128 us
    all_to_all x2, waiting for transfers between devices, exchange(): lax.all_to_all(rows_in, 'row', split_axis=0, concat_axis=0, tiled=True)  81.1 us
    all_to_all x2, starting transfers between devices, exchange(): lax.all_to_all(rows_in, 'row', split_axis=0, concat_axis=0, tiled=True)  72.9 us
    pallas_call x2, Pallas kernels, filter_step(): pl.pallas_call(functools.partial(filter_kernel, row_n, row_chunk, last),...  70.9 us
    all_gather x2, waiting for transfers between devices, exchange(): return (rows, lax.all_gather(cols_in, 'col'))  52.3 us
    pallas_call x2, Pallas kernels, gather_rows(): pl.pallas_call(round_kernel, out_shape=jax.ShapeDtypeStruct((row_count, s...  19.7 us
    pallas_call x2, Pallas kernels, dense(): pl.pallas_call(functools.partial(dense_kernel, transposed), out_shape=jax...  14 us
  transfers between devices with their start and end apart: 8, of which 4 were waited for; matrix products, arithmetic and copies ran while one was open for 3% of the time, Pallas kernels for 5%

commit v1 on v0

--- a/solution.py
+++ b/solution.py
@@ -10,6 +10,7 @@
 center = 0.25
 half_width = 2.5
 VMEM_LIMIT = 60 * 1024 * 1024
+MESH = pl.DeviceIdType.MESH
 
 
 def dense_kernel(transposed, tiles, pairs, counts, ham_ref, out_ref, acc):
@@ -50,85 +51,390 @@
     )(tiles, pairs, counts, hams)
 
 
-def round_kernel(place, hot, sel, x_ref, out_ref):
-    out_ref[0] = x_ref[...].astype(out_ref.dtype)
-
-
-def gather_rows(x, place, hot, sel, row_count, size):
-    width = x.shape[1]
+def pack_kernel(place, hot, xr_ref, xc_ref, rows_ref, cols_ref):
+    rows_ref[0] = xr_ref[...].astype(rows_ref.dtype)
+    cols_ref[0] = xc_ref[...].astype(cols_ref.dtype)
+
+
+def pack(x, place, hot, row_count, ratio, size):
+    height, width = x.shape
     hot_count = hot.shape[0] // row_count
-
-    def pick(p, place, hot, sel):
-        p = jnp.minimum(p, row_count - 1)
-        return (hot[place[0] * hot_count + sel[p * row_count + place[0]]], 0)
-
-    grid_spec = pltpu.PrefetchScalarGridSpec(
-        num_scalar_prefetch=3,
-        grid=(row_count,),
-        in_specs=[pl.BlockSpec((size, width), pick)],
-        out_specs=pl.BlockSpec((1, size, width), lambda p, *_: (p, 0, 0)),
-    )
-    return pl.pallas_call(
-        round_kernel,
-        out_shape=jax.ShapeDtypeStruct((row_count, size, width), jnp.bfloat16),
-        grid_spec=grid_spec,
-    )(place, hot, sel, x)
-
-
-def gather_cols(x, place, hot, sel, row_count, ratio, size):
-    height = x.shape[0]
-    hot_count = hot.shape[0] // row_count
-    blocks = x.shape[1] // (ratio * size)
-
-    def pick(n, place, hot, sel):
+    blocks = width // (ratio * size)
+    part = width // ratio
+
+    def row_block(n, place, hot):
+        n = jnp.minimum(n, ratio * hot_count - 1)
+        return (hot[place[0] * hot_count + n // ratio], n % ratio)
+
+    def col_block(n, place, hot):
         n = jnp.minimum(n, ratio * hot_count - 1)
         tile, which = n // hot_count, n % hot_count
         return (0, tile * blocks + hot[(place[1] * ratio + tile) * hot_count + which])
 
     grid_spec = pltpu.PrefetchScalarGridSpec(
-        num_scalar_prefetch=3,
+        num_scalar_prefetch=2,
         grid=(ratio * hot_count,),
-        in_specs=[pl.BlockSpec((height, size), pick)],
-        out_specs=pl.BlockSpec((1, height, size), lambda n, *_: (n, 0, 0)),
+        in_specs=[pl.BlockSpec((size, part), row_block), pl.BlockSpec((height, size), col_block)],
+        out_specs=[
+            pl.BlockSpec((1, size, part), lambda n, *_: (n // ratio, 0, n % ratio)),
+            pl.BlockSpec((1, height, size), lambda n, *_: (n, 0, 0)),
+        ],
     )
     return pl.pallas_call(
-        round_kernel,
-        out_shape=jax.ShapeDtypeStruct((ratio * hot_count, height, size), jnp.bfloat16),
+        pack_kernel,
+        out_shape=[
+            jax.ShapeDtypeStruct((hot_count, size, width), jnp.bfloat16),
+            jax.ShapeDtypeStruct((ratio * hot_count, height, size), jnp.bfloat16),
+        ],
         grid_spec=grid_spec,
-    )(place, hot, sel, x)
-
-
-def spread_hams(ham, row_n, col_n):
+    )(place, hot, x, x)
+
+
+class Grid:
+    def __init__(self, row_n, col_n):
+        line = 1
+        while 4 * line * line <= 2 * row_n:
+            line *= 2
+        self.line, self.lanes = line, row_n // line
+        self.cores = 2 if col_n % 2 == 0 else 1
+        self.chips = col_n // self.cores
+        self.row_n, self.col_n = row_n, col_n
+        row, col = lax.axis_index("row"), lax.axis_index("col")
+        self.row, self.col = row, col
+        self.at, self.lane = row // self.lanes, lax.rem(row, self.lanes)
+        self.chip, self.core = col // self.cores, lax.rem(col, self.cores)
+
+    def on_line(self, at):
+        return (at * self.lanes + self.lane, self.col)
+
+    def other_lane(self, step):
+        return (self.at * self.lanes + lax.rem(self.lane + step, self.lanes), self.col)
+
+    def other_chip(self, step):
+        return (self.row, lax.rem(self.chip + step, self.chips) * self.cores + self.core)
+
+    def other_core(self):
+        return (self.row, self.chip * self.cores + lax.rem(self.core + 1, self.cores))
+
+
+def remote(src, dst, send, recv, device):
+    return pltpu.make_async_remote_copy(
+        src_ref=src, dst_ref=dst, send_sem=send, recv_sem=recv, device_id=device, device_id_type=MESH)
+
+
+def greet(g):
+    barrier = pltpu.get_barrier_semaphore()
+    up, down = g.at + 1 < g.line, g.at > 0
+
+    def hello(device):
+        pl.semaphore_signal(barrier, inc=1, device_id=device, device_id_type=MESH)
+
+    @pl.when(up)
+    def _():
+        hello(g.on_line(g.at + 1))
+
+    @pl.when(down)
+    def _():
+        hello(g.on_line(g.at - 1))
+
+    for step in range(1, g.lanes):
+        hello(g.other_lane(step))
+    for step in range(1, g.chips):
+        hello(g.other_chip(step))
+    fixed = g.lanes - 1 + g.chips - 1
+    if g.cores == 2:
+        hello(g.other_core())
+        fixed += 1
+    pl.semaphore_wait(barrier, fixed + up.astype(jnp.int32) + down.astype(jnp.int32))
+
+
+def exchange_kernel(row_n, col_n, pieces, with_ham, sel, rows_ref, cols_ref, *refs):
+    g = Grid(row_n, col_n)
+    if with_ham:
+        ham_ref, s_out, c_out, h_out = refs[:4]
+        refs = refs[4:]
+    else:
+        s_out, c_out = refs[:2]
+        refs = refs[2:]
+    held, lane_buf, own_buf, col_buf, own_sem, line_recv, up_send, down_send, lane_send, lane_recv = refs[:10]
+    chip_send, chip_recv, core_send, core_recv = refs[10:14]
+    if with_ham:
+        ham_buf, ham_sem, ham_recv, ham_up, ham_down, ham_lane = refs[14:]
+        ratio = row_n // col_n
+        ham_rows = ham_ref.shape[0] // pieces
+    hot_count, size = rows_ref.shape[0], rows_ref.shape[1]
+    piece = size // pieces
+    block_n = cols_ref.shape[0]
+    line, lanes, at = g.line, g.lanes, g.at
+
+    take = pltpu.make_async_copy(rows_ref, held.at[at], own_sem.at[0])
+    take_cols = pltpu.make_async_copy(cols_ref, col_buf, own_sem.at[1])
+    take.start()
+    take_cols.start()
+    if with_ham:
+        take_ham = pltpu.make_async_copy(ham_ref, ham_buf, ham_sem.at[0])
+        take_ham.start()
+    greet(g)
+
+    def chip_copy(step, b):
+        slot = g.col * block_n + b
+        return remote(cols_ref.at[b], c_out.at[slot], chip_send.at[step - 1, b], chip_recv.at[step - 1, b], g.other_chip(step))
+
+    def chip_slot(step):
+        return (lax.rem(g.chip - step + g.chips, g.chips) * g.cores + g.core) * block_n
+
+    def core_copy(step, b):
+        if step == 0:
+            src, slot = cols_ref.at[b], g.col * block_n + b
+        else:
+            slot = chip_slot(step) + b
+            src = c_out.at[slot]
+        return remote(src, c_out.at[slot], core_send.at[step, b], core_recv.at[step, b], g.other_core())
+
+    for b in range(block_n):
+        for step in range(1, g.chips):
+            chip_copy(step, b).start()
+    if g.cores == 2:
+        for b in range(block_n):
+            core_copy(0, b).start()
+    take.wait()
+    take_cols.wait()
+    put_cols = pltpu.make_async_copy(col_buf, c_out.at[pl.ds(g.col * block_n, block_n)], own_sem.at[1])
+    put_cols.start()
+
+    def part(slot, p):
+        return held.at[slot, :, pl.ds(pl.multiple_of(p * piece, piece), piece), :]
+
+    def up_copy(slot, p):
+        return remote(part(slot, p), part(slot, p), up_send.at[slot, p], line_recv.at[slot, p], g.on_line(at + 1))
+
+    def down_copy(slot, p):
+        return remote(part(slot, p), part(slot, p), down_send.at[slot, p], line_recv.at[slot, p], g.on_line(at - 1))
+
+    def lane_copy(step, slot, p):
+        rows = pl.ds(pl.multiple_of(p * piece, piece), piece)
+        return remote(
+            lane_buf.at[step - 1, slot, rows, :], s_out.at[slot * lanes + g.lane, rows, :],
+            lane_send.at[step - 1, slot, p], lane_recv.at[step - 1, slot, p], g.other_lane(step))
+
+    def choose(target, source, slot, p, out):
+        rows = pl.ds(pl.multiple_of(p * piece, piece), piece)
+        which = sel[target * row_n + source]
+        value = held[slot, 0, rows, :]
+        for h in range(1, hot_count):
+            value = jnp.where(which == h, held[slot, h, rows, :], value)
+        out[slot, rows, :] = value
+
+    def select(slot, p):
+        source = slot * lanes + g.lane
+        for step in range(1, lanes):
+            choose(at * lanes + lax.rem(g.lane + step, lanes), source, slot, p, lane_buf.at[step - 1])
+            lane_copy(step, slot, p).start()
+        choose(g.row, source, slot, p, own_buf)
+
+    if with_ham:
+        def ham_part(ref, p):
+            return ref.at[pl.ds(pl.multiple_of(p * ham_rows, ham_rows), ham_rows)]
+
+        def ham_copies(i, p):
+            part_of = ham_part(h_out.at[i], p)
+            up = remote(part_of, part_of, ham_up.at[i, p], ham_recv.at[i, p], g.on_line(at + 1))
+            down = remote(part_of, part_of, ham_down.at[i, p], ham_recv.at[i, p], g.on_line(at - 1))
+            over = [remote(part_of, part_of, ham_lane.at[i, step - 1, p], ham_recv.at[i, p], g.other_lane(step))
+                    for step in range(1, lanes)]
+            return up, down, over
+
+        def ham_place(i):
+            tile = g.col * ratio + i
+            return tile // lanes, lax.rem(tile, lanes)
+
+        take_ham.wait()
+        for i in range(ratio):
+            home, home_lane = ham_place(i)
+
+            @pl.when((home == at) & (home_lane == g.lane))
+            def _():
+                put = pltpu.make_async_copy(ham_buf, h_out.at[i], ham_sem.at[0])
+                put.start()
+                put.wait()
+
+        def ham_sends(i, p, act):
+            home, home_lane = ham_place(i)
+            up, down, over = ham_copies(i, p)
+
+            @pl.when(home_lane == g.lane)
+            def _():
+                @pl.when((at >= home) & (at + 1 < line))
+                def _():
+                    act(up)
+
+                @pl.when((at <= home) & (at > 0))
+                def _():
+                    act(down)
+
+                for copy in over:
+                    act(copy)
+
+    def advance(n, carry):
+        s, p = n // pieces, lax.rem(n, pieces)
+        below, above = at - s, at + s
+
+        @pl.when(below >= 0)
+        def _():
+            @pl.when(s > 0)
+            def _():
+                up_copy(below, p).wait_recv()
+
+            @pl.when(at + 1 < line)
+            def _():
+                up_copy(below, p).start()
+
+        @pl.when(above < line)
+        def _():
+            @pl.when(s > 0)
+            def _():
+                down_copy(above, p).wait_recv()
+
+            @pl.when(at > 0)
+            def _():
+                down_copy(above, p).start()
+
+        if with_ham:
+            for i in range(ratio):
+                home, home_lane = ham_place(i)
+                away = jnp.where(at >= home, at - home, home - at)
+
+                @pl.when((home_lane == g.lane) & (away == s))
+                def _():
+                    @pl.when(s > 0)
+                    def _():
+                        ham_copies(i, p)[0].wait_recv()
+
+                    ham_sends(i, p, lambda copy: copy.start())
+
+        @pl.when(below >= 0)
+        def _():
+            select(below, p)
+
+        @pl.when((above < line) & (s > 0))
+        def _():
+            select(above, p)
+
+        return carry
+
+    def columns(step):
+        for b in range(block_n):
+            slot = chip_slot(step) + b
+            remote(cols_ref.at[b], c_out.at[slot], chip_send.at[step - 1, b], chip_recv.at[step - 1, b], g.other_chip(step)).wait_recv()
+            if g.cores == 2:
+                core_copy(step, b).start()
+
+    lax.fori_loop(0, pieces * (line // 2), advance, 0)
+    for step in range(1, g.chips):
+        columns(step)
+    lax.fori_loop(pieces * (line // 2), pieces * line, advance, 0)
+
+    for slot in range(line):
+        pltpu.make_async_copy(own_buf.at[slot], s_out.at[slot * lanes + g.lane], own_sem.at[2 + slot]).start()
+
+    for slot in range(line):
+        pltpu.make_async_copy(own_buf.at[slot], s_out.at[slot * lanes + g.lane], own_sem.at[2 + slot]).wait()
+    put_cols.wait()
+
+    def finish(n, carry):
+        slot, p = n // pieces, lax.rem(n, pieces)
+
+        @pl.when((slot <= at) & (at + 1 < line))
+        def _():
+            up_copy(slot, p).wait_send()
+
+        @pl.when((slot >= at) & (at > 0))
+        def _():
+            down_copy(slot, p).wait_send()
+
+        for step in range(1, lanes):
+            lane_copy(step, slot, p).wait_send()
+            came = slot * lanes + lax.rem(g.lane - step + lanes, lanes)
+            rows = pl.ds(pl.multiple_of(p * piece, piece), piece)
+            remote(lane_buf.at[step - 1, slot, rows, :], s_out.at[came, rows, :], lane_send.at[step - 1, slot, p],
+                   lane_recv.at[step - 1, slot, p], g.other_lane(step)).wait_recv()
+        return carry
+
+    lax.fori_loop(0, line * pieces, finish, 0)
+    for b in range(block_n):
+        for step in range(1, g.chips):
+            chip_copy(step, b).wait_send()
+        if g.cores == 2:
+            for step in range(g.chips):
+                core_copy(step, b).wait_send()
+                other = lax.rem(g.core + 1, g.cores)
+                slot = (lax.rem(g.chip - step + g.chips, g.chips) * g.cores + other) * block_n + b
+                remote(cols_ref.at[b], c_out.at[slot], core_send.at[step, b], core_recv.at[step, b], g.other_core()).wait_recv()
+    if with_ham:
+        for i in range(ratio):
+            home, home_lane = ham_place(i)
+
+            def settle(p, carry):
+                ham_sends(i, p, lambda copy: copy.wait_send())
+
+                @pl.when(home_lane != g.lane)
+                def _():
+                    ham_copies(i, p)[2][0].wait_recv()
+                return carry
+
+            lax.fori_loop(0, pieces, settle, 0)
+
+
+def exchange(rows, cols, ham, sel, row_n, col_n, ident):
+    hot_count, size, width = rows.shape
+    block_n, height = cols.shape[:2]
     ratio = row_n // col_n
-    side = lax.rem(lax.axis_index("row"), ratio)
-    group = lax.axis_index("row") // ratio
-    dist = lax.rem(group - lax.axis_index("col") + col_n, col_n)
-    bwd = (col_n - 1) // 2
-    fwd = col_n - 1 - bwd
-
-    def device(group, side, col):
-        return ((group % col_n) * ratio + side) * col_n + col
-
-    held = ham
-    for way, count in ((1, fwd), (-1, bwd)):
-        moving = ham
-        for step in range(count):
-            links = [(device(col + way * step, s, col), device(col + way * (step + 1), s, col))
-                     for col in range(col_n) for s in range(ratio)]
-            moving = lax.ppermute(moving, ("row", "col"), links)
-            held = jnp.where(dist == (way * (step + 1)) % col_n, moving, held)
-    pieces = [held]
-    for m in range(1, ratio):
-        links = [(device(g, s, col), device(g, (s + m) % ratio, col))
-                 for g in range(col_n) for col in range(col_n) for s in range(ratio)]
-        pieces.append(lax.ppermute(held, ("row", "col"), links))
-    order = lax.rem(side - jnp.arange(ratio) + ratio, ratio)
-    return jnp.take(jnp.stack(pieces), order, axis=0)
-
-
-def exchange(rows_in, cols_in):
-    rows = lax.all_to_all(rows_in, "row", split_axis=0, concat_axis=0, tiled=True)
-    return rows, lax.all_gather(cols_in, "col")
+    pieces = 4
+    with jax.named_scope("grid"):
+        g = Grid(row_n, col_n)
+    line, lanes, chips = g.line, g.lanes, g.chips
+    dma = pltpu.SemaphoreType.DMA
+    anywhere = pl.BlockSpec(memory_space=pl.ANY)
+    out_shape = [
+        jax.ShapeDtypeStruct((row_n, size, width), jnp.bfloat16),
+        jax.ShapeDtypeStruct((col_n * block_n, height, size), jnp.bfloat16),
+    ]
+    scratch = [
+        pltpu.VMEM((line, hot_count, size, width), jnp.bfloat16),
+        pltpu.VMEM((max(lanes - 1, 1), line, size, width), jnp.bfloat16),
+        pltpu.VMEM((line, size, width), jnp.bfloat16),
+        pltpu.VMEM(cols.shape, jnp.bfloat16),
+        dma((2 + line,)),
+        dma((line, pieces)),
+        dma((line, pieces)),
+        dma((line, pieces)),
+        dma((max(lanes - 1, 1), line, pieces)),
+        dma((max(lanes - 1, 1), line, pieces)),
+        dma((max(chips - 1, 1), block_n)),
+        dma((max(chips - 1, 1), block_n)),
+        dma((chips, block_n)),
+        dma((chips, block_n)),
+    ]
+    args = [sel, rows, cols]
+    if ham is not None:
+        out_shape.append(jax.ShapeDtypeStruct((ratio,) + ham.shape, ham.dtype))
+        scratch += [
+            pltpu.VMEM(ham.shape, ham.dtype),
+            dma((1,)),
+            dma((ratio, pieces)),
+            dma((ratio, pieces)),
+            dma((ratio, pieces)),
+            dma((ratio, max(lanes - 1, 1), pieces)),
+        ]
+        args.append(ham)
+    return pl.pallas_call(
+        functools.partial(exchange_kernel, row_n, col_n, pieces, ham is not None),
+        out_shape=out_shape,
+        in_specs=[pl.BlockSpec(memory_space=pltpu.SMEM)] + [anywhere] * (len(args) - 1),
+        out_specs=[anywhere] * len(out_shape),
+        scratch_shapes=scratch,
+        compiler_params=pltpu.CompilerParams(collective_id=ident, has_side_effects=True, vmem_limit_bytes=VMEM_LIMIT),
+    )(*args)
 
 
 def filter_kernel(source_count, row_chunk, last, place, sel, wa_ref, s_ref, wb_ref, rd_ref, cd_ref, *refs):
@@ -205,23 +511,16 @@
     cd = lax.dynamic_slice_in_dim(diagonal, col_index * width, width)[None, :]
     depth = row_n * size
 
-    def sources(x):
-        rows = gather_rows(x, place, hot, sel, row_n, size)
-        cols = gather_cols(x, place, hot, sel, row_n, ratio, size)
-        return rows, cols
-
-    def joined(rows, cols):
-        return rows.reshape(depth, width), cols.reshape((-1,) + cols.shape[2:])
-
-    rows, cols = exchange(*sources(start_vector))
-    hams = spread_hams(ham_blocks, row_n, col_n)
+    rows, cols = pack(start_vector, place, hot, row_n, ratio, size)
+    s, b, hams = exchange(rows, cols, ham_blocks, sel, row_n, col_n, 0)
+    s = s.reshape(depth, width)
     wa = dense(ham_blocks[None], place[:1], pairs, pair_counts, (height, depth), False)[0]
     mirrors = (col_index * ratio + jnp.arange(ratio)).astype(jnp.int32)
     wb = dense(hams, mirrors, pairs, pair_counts, (depth, width // ratio), True)
-    s, b = joined(rows, cols)
     first = filter_step(place, sel, wa, s, wb, rd, cd, b, start_vector, None, row_n, ratio)
-    s, b = joined(*exchange(*sources(first)))
-    second = filter_step(place, sel, wa, s, wb, rd, cd, b, first, start_vector, row_n, ratio)
+    rows, cols = pack(first, place, hot, row_n, ratio, size)
+    s, b = exchange(rows, cols, None, sel, row_n, col_n, 1)
+    second = filter_step(place, sel, wa, s.reshape(depth, width), wb, rd, cd, b, first, start_vector, row_n, ratio)
     return (first, second)
 
 

time: 500 us -> 367 us (0.73)
  waiting for transfers between devices: 271 us -> 0 us
  Pallas kernels: 114 us -> 355 us
  starting transfers between devices: 78.1 us -> 0 us
  between operations: 14.1 us -> 0.66 us
  other arithmetic: 9.03 us -> 1.1 us
    pallas_call x4, Pallas kernels: 29.2 us -> 268 us  [the longest x2 256 us: exchange(): pl.pallas_call(functools.partial(exchange_kernel, row_n, col_n, pieces, h...]
    ppermute x4 -> x0, waiting for transfers between devices: 138 us -> none  [the longest x3 128 us: spread_hams(): moving = lax.ppermute(moving, ('row', 'col'), links)]
    all_to_all x2 -> x0, waiting for transfers between devices: 81.1 us -> none  [exchange(): lax.all_to_all(rows_in, 'row', split_axis=0, concat_axis=0, tiled=True)]
    all_to_all x2 -> x0, starting transfers between devices: 72.9 us -> none  [exchange(): lax.all_to_all(rows_in, 'row', split_axis=0, concat_axis=0, tiled=True)]
    all_gather x2 -> x0, waiting for transfers between devices: 52.3 us -> none  [exchange(): return (rows, lax.all_gather(cols_in, 'col'))]
    select_n x3 -> x0, other arithmetic: 5.62 us -> none  [the longest x2 3.93 us: spread_hams(): return jnp.take(jnp.stack(pieces), order, axis=0)]
    ppermute x4 -> x0, starting transfers between devices: 5.17 us -> none  [the longest x3 3.88 us: spread_hams(): moving = lax.ppermute(moving, ('row', 'col'), links)]
  transfers between devices with their start and end apart: 8 -> 0, of which waited for: 4 -> 0; matrix products, arithmetic and copies ran while one was open for 3% -> 0% of each run, Pallas kernels for 5% -> 0%
where the time goes in v1:
time: 367 us; the launch traced here: 364 us
  Pallas kernels  355 us (97%)
  local copies, waits for them, and re-layouts  7.36 us (2%)
    pallas_call x2, Pallas kernels, exchange(): pl.pallas_call(functools.partial(exchange_kernel, row_n, col_n, pieces, h...  256 us
    pallas_call x2, Pallas kernels, filter_step(): pl.pallas_call(functools.partial(filter_kernel, row_n, row_chunk, last),...  70.9 us
    pallas_call x2, Pallas kernels, dense(): pl.pallas_call(functools.partial(dense_kernel, transposed), out_shape=jax...  16.8 us
    pallas_call x2, Pallas kernels, pack(): pl.pallas_call(pack_kernel, out_shape=[jax.ShapeDtypeStruct((hot_count, s...  11.2 us

profile of v1, /device:TPU:24, one launch (start us, length us, event | category | flops | bytes accessed | tf_op | source)
XLA Modules:
  0.0 364.4 jit_solution(3168313390489269162)
XLA Ops:
  0.6 0.6 pad_add_fusion.place
  1.3 0.5 iota_add_fusion.tiles
  1.7 1.4 reshape.19.sel
  3.1 0.8 copy.10
  3.8 0.6 reshape.21.hot
  4.4 0.8 dynamic_slice.6
  5.2 1.4 reshape.20.pairs
  6.6 1.3 dynamic_slice.7
  7.9 1.2 broadcast_in_dim.12.rd_ref
  9.1 5.4 %shard_map.86 = bf16[1,1536,1024]{2,1,0:T(8,128)(2,1)} custom-call(s32[1]{0:T(128)} %bitcast.tiles, s32[1536]{0:T(1024)} %reshape.20.pairs, s32[8]{0:T(128)} %counts.3, bf16[1,48,128,128]{3,2,1,0:T(8,128)(2,1)} %bitcast.11), custom_call_target="tpu_custom_call" | custom-call | tf_op jit(solution)/shard_map/pallas_call | solution.py:46
  14.5 5.6 %shard_map.87 = (bf16[2,128,3072]{2,1,0:T(8,128)(2,1)}, bf16[4,1536,128]{2,1,0:T(8,128)(2,1)}) custom-call(s32[2]{0:T(128)} %pad_add_fusion.place, s32[16]{0:T(128)} %reshape.21.hot, f32[1536,3072]{1,0:T(8,128)} %refs_9_.1, f32[1536,3072]{1,0:T(8,128)} %refs_9_.1), custom_call_target="tpu_custom_call" | custom-call | tf_op jit(solution)/shard_map/pallas_call | solution.py:83
  20.1 150.4 %shard_map.88 = (bf16[8,128,3072]{2,1,0:T(8,128)(2,1)}, bf16[16,1536,128]{2,1,0:T(8,128)(2,1)}, bf16[2,48,128,128]{3,2,1,0:T(8,128)(2,1)}) custom-call(s32[64]{0:T(128)} %reshape.19.sel, bf16[2,128,3072]{2,1,0:T(8,128)(2,1)} %get-tuple-element.11.rows_ref, bf16[4,1536,128]{2,1,0:T(8,128)(2,1)} %get-tuple-element.12.cols_ref, bf16[48,128,128]{2,1,0:T(8,128)(2,1)} %refs_0_.1), custom_call_target="tpu_custom_call" | custom-call | tf_op jit(solution)/shard_map/pallas_call | solution.py:430
  170.6 11.3 %shard_map.89.wb_ref = bf16[2,1024,1536]{2,1,0:T(8,128)(2,1)} custom-call(s32[2]{0:T(128)} %iota_add_fusion.tiles, s32[1536]{0:T(1024)} %reshape.20.pairs, s32[8]{0:T(128)} %counts.3, bf16[2,48,128,128]{3,2,1,0:T(8,128)(2,1)} %get-tuple-element.14.ham_ref), custom_call_target="tpu_custom_call" | custom-call | tf_op jit(solution)/shard_map/pallas_call | solution.py:46
  181.9 34.5 %shard_map.90.xr_ref.xc_ref.refs_8_ = f32[1536,3072]{1,0:T(8,128)} custom-call(s32[2]{0:T(128)} %pad_add_fusion.place, s32[64]{0:T(128)} %reshape.19.sel, bf16[1536,1024]{1,0:T(8,128)(2,1)} %bitcast.7, bf16[1024,3072]{1,0:T(8,128)(2,1)} %bitcast.10, bf16[2,1024,1536]{2,1,0:T(8,128)(2,1)} %shard_map.89.wb_ref, f32[1536,1]{1,0:T(8,128)} %broadcast_in_dim.12.rd_ref, ...), custom_call_target="tpu_custom_call" | custom-call | tf_op jit(solution)/shard_map/pallas_call | solution.py:490
  216.4 5.6 %shard_map.91 = (bf16[2,128,3072]{2,1,0:T(8,128)(2,1)}, bf16[4,1536,128]{2,1,0:T(8,128)(2,1)}) custom-call(s32[2]{0:T(128)} %pad_add_fusion.place, s32[16]{0:T(128)} %reshape.21.hot, f32[1536,3072]{1,0:T(8,128)} %shard_map.90.xr_ref.xc_ref.refs_8_, f32[1536,3072]{1,0:T(8,128)} %shard_map.90.xr_ref.xc_ref.refs_8_), custom_call_target="tpu_custom_call" | custom-call | tf_op jit(solution)/shard_map/pallas_call | solution.py:83
  222.0 105.9 %shard_map.92 = (bf16[8,128,3072]{2,1,0:T(8,128)(2,1)}, bf16[16,1536,128]{2,1,0:T(8,128)(2,1)}) custom-call(s32[64]{0:T(128)} %reshape.19.sel, bf16[2,128,3072]{2,1,0:T(8,128)(2,1)} %get-tuple-element.16.rows_ref, bf16[4,1536,128]{2,1,0:T(8,128)(2,1)} %get-tuple-element.17.cols_ref), custom_call_target="tpu_custom_call" | custom-call | tf_op jit(solution)/shard_map/pallas_call | solution.py:430
  328.0 36.4 %shard_map.93 = f32[1536,3072]{1,0:T(8,128)} custom-call(s32[2]{0:T(128)} %pad_add_fusion.place, s32[64]{0:T(128)} %reshape.19.sel, bf16[1536,1024]{1,0:T(8,128)(2,1)} %bitcast.8, bf16[1024,3072]{1,0:T(8,128)(2,1)} %bitcast.9, bf16[2,1024,1536]{2,1,0:T(8,128)(2,1)} %shard_map.89.wb_ref, f32[1536,1]{1,0:T(8,128)} %broadcast_in_dim.12.rd_ref, ...), custom_call_target="tpu_custom_call" | custom-call | tf_op jit(solution)/shard_map/pallas_call | solution.py:490

commit v2 on v1

--- a/solution.py
+++ b/solution.py
@@ -90,14 +90,17 @@
     )(place, hot, x, x)
 
 
+def layout(row_n, col_n):
+    line = 1
+    while 4 * line * line <= 2 * row_n:
+        line *= 2
+    cores = 2 if col_n % 2 == 0 else 1
+    return line, row_n // line, col_n // cores, cores
+
+
 class Grid:
     def __init__(self, row_n, col_n):
-        line = 1
-        while 4 * line * line <= 2 * row_n:
-            line *= 2
-        self.line, self.lanes = line, row_n // line
-        self.cores = 2 if col_n % 2 == 0 else 1
-        self.chips = col_n // self.cores
+        self.line, self.lanes, self.chips, self.cores = layout(row_n, col_n)
         self.row_n, self.col_n = row_n, col_n
         row, col = lax.axis_index("row"), lax.axis_index("col")
         self.row, self.col = row, col
@@ -148,8 +151,12 @@
     pl.semaphore_wait(barrier, fixed + up.astype(jnp.int32) + down.astype(jnp.int32))
 
 
-def exchange_kernel(row_n, col_n, pieces, with_ham, sel, rows_ref, cols_ref, *refs):
+def exchange_kernel(row_n, col_n, pieces, with_ham, ahead, sel, rows_ref, cols_ref, *refs):
     g = Grid(row_n, col_n)
+    first_step = 2 if ahead else 1
+    if ahead:
+        below_ref, above_ref, chip_ref = refs[:3]
+        refs = refs[3:]
     if with_ham:
         ham_ref, s_out, c_out, h_out = refs[:4]
         refs = refs[4:]
@@ -162,6 +169,8 @@
         ham_buf, ham_sem, ham_recv, ham_up, ham_down, ham_lane = refs[14:]
         ratio = row_n // col_n
         ham_rows = ham_ref.shape[0] // pieces
+    if ahead:
+        ahead_buf, ahead_sem = refs[14:]
     hot_count, size = rows_ref.shape[0], rows_ref.shape[1]
     piece = size // pieces
     block_n = cols_ref.shape[0]
@@ -171,6 +180,18 @@
     take_cols = pltpu.make_async_copy(cols_ref, col_buf, own_sem.at[1])
     take.start()
     take_cols.start()
+    if ahead:
+        take_chip = pltpu.make_async_copy(chip_ref, ahead_buf, ahead_sem.at[2])
+        take_chip.start()
+
+        @pl.when(at > 0)
+        def _():
+            pltpu.make_async_copy(below_ref, held.at[at - 1], ahead_sem.at[0]).start()
+
+        @pl.when(at + 1 < line)
+        def _():
+            pltpu.make_async_copy(above_ref, held.at[at + 1], ahead_sem.at[1]).start()
+
     if with_ham:
         take_ham = pltpu.make_async_copy(ham_ref, ham_buf, ham_sem.at[0])
         take_ham.start()
@@ -188,17 +209,31 @@
             src, slot = cols_ref.at[b], g.col * block_n + b
         else:
             slot = chip_slot(step) + b
-            src = c_out.at[slot]
+            src = chip_ref.at[b] if ahead and step == 1 else c_out.at[slot]
         return remote(src, c_out.at[slot], core_send.at[step, b], core_recv.at[step, b], g.other_core())
 
     for b in range(block_n):
-        for step in range(1, g.chips):
+        for step in range(first_step, g.chips):
             chip_copy(step, b).start()
     if g.cores == 2:
-        for b in range(block_n):
-            core_copy(0, b).start()
+        for step in range(first_step):
+            for b in range(block_n):
+                core_copy(step, b).start()
     take.wait()
     take_cols.wait()
+    if ahead:
+        take_chip.wait()
+        put_chip = pltpu.make_async_copy(ahead_buf, c_out.at[pl.ds(chip_slot(1), block_n)], ahead_sem.at[2])
+        put_chip.start()
+
+        @pl.when(at > 0)
+        def _():
+            pltpu.make_async_copy(below_ref, held.at[at - 1], ahead_sem.at[0]).wait()
+
+        @pl.when(at + 1 < line)
+        def _():
+            pltpu.make_async_copy(above_ref, held.at[at + 1], ahead_sem.at[1]).wait()
+
     put_cols = pltpu.make_async_copy(col_buf, c_out.at[pl.ds(g.col * block_n, block_n)], own_sem.at[1])
     put_cols.start()
 
@@ -281,21 +316,21 @@
 
         @pl.when(below >= 0)
         def _():
-            @pl.when(s > 0)
+            @pl.when(s >= first_step)
             def _():
                 up_copy(below, p).wait_recv()
 
-            @pl.when(at + 1 < line)
+            @pl.when((at + 1 < line) & (s >= first_step - 1))
             def _():
                 up_copy(below, p).start()
 
         @pl.when(above < line)
         def _():
-            @pl.when(s > 0)
+            @pl.when(s >= first_step)
             def _():
                 down_copy(above, p).wait_recv()
 
-            @pl.when(at > 0)
+            @pl.when((at > 0) & (s >= first_step - 1))
             def _():
                 down_copy(above, p).start()
 
@@ -330,7 +365,7 @@
                 core_copy(step, b).start()
 
     lax.fori_loop(0, pieces * (line // 2), advance, 0)
-    for step in range(1, g.chips):
+    for step in range(first_step, g.chips):
         columns(step)
     lax.fori_loop(pieces * (line // 2), pieces * line, advance, 0)
 
@@ -340,15 +375,17 @@
     for slot in range(line):
         pltpu.make_async_copy(own_buf.at[slot], s_out.at[slot * lanes + g.lane], own_sem.at[2 + slot]).wait()
     put_cols.wait()
+    if ahead:
+        put_chip.wait()
 
     def finish(n, carry):
         slot, p = n // pieces, lax.rem(n, pieces)
 
-        @pl.when((slot <= at) & (at + 1 < line))
+        @pl.when((slot <= at + 1 - first_step) & (at + 1 < line))
         def _():
             up_copy(slot, p).wait_send()
 
-        @pl.when((slot >= at) & (at > 0))
+        @pl.when((slot >= at - 1 + first_step) & (at > 0))
         def _():
             down_copy(slot, p).wait_send()
 
@@ -362,7 +399,7 @@
 
     lax.fori_loop(0, line * pieces, finish, 0)
     for b in range(block_n):
-        for step in range(1, g.chips):
+        for step in range(first_step, g.chips):
             chip_copy(step, b).wait_send()
         if g.cores == 2:
             for step in range(g.chips):
@@ -385,14 +422,12 @@
             lax.fori_loop(0, pieces, settle, 0)
 
 
-def exchange(rows, cols, ham, sel, row_n, col_n, ident):
+def exchange(rows, cols, ham, ahead, sel, row_n, col_n, ident):
     hot_count, size, width = rows.shape
     block_n, height = cols.shape[:2]
     ratio = row_n // col_n
     pieces = 4
-    with jax.named_scope("grid"):
-        g = Grid(row_n, col_n)
-    line, lanes, chips = g.line, g.lanes, g.chips
+    line, lanes, chips, _ = layout(row_n, col_n)
     dma = pltpu.SemaphoreType.DMA
     anywhere = pl.BlockSpec(memory_space=pl.ANY)
     out_shape = [
@@ -416,6 +451,9 @@
         dma((chips, block_n)),
     ]
     args = [sel, rows, cols]
+    if ahead is not None:
+        scratch += [pltpu.VMEM(cols.shape, jnp.bfloat16), dma((3,))]
+        args += ahead
     if ham is not None:
         out_shape.append(jax.ShapeDtypeStruct((ratio,) + ham.shape, ham.dtype))
         scratch += [
@@ -428,13 +466,120 @@
         ]
         args.append(ham)
     return pl.pallas_call(
-        functools.partial(exchange_kernel, row_n, col_n, pieces, ham is not None),
+        functools.partial(exchange_kernel, row_n, col_n, pieces, ham is not None, ahead is not None),
         out_shape=out_shape,
         in_specs=[pl.BlockSpec(memory_space=pltpu.SMEM)] + [anywhere] * (len(args) - 1),
         out_specs=[anywhere] * len(out_shape),
         scratch_shapes=scratch,
         compiler_params=pltpu.CompilerParams(collective_id=ident, has_side_effects=True, vmem_limit_bytes=VMEM_LIMIT),
     )(*args)
+
+
+def hot_kernel(row_n, hot_count, place, hot, sel, *refs):
+    refs = list(refs)
+
+    def some(count):
+        taken = refs[:count]
+        del refs[:count]
+        return taken
+
+    wide = lambda blocks: jnp.concatenate(blocks, axis=1)
+    wa_hot, x_rows, rd_hot = some(hot_count), some(hot_count), some(hot_count)
+    b_hot = [some(row_n) for _ in range(hot_count)]
+    s_ref, wb_ref, cd_ref = some(3)
+    wa_ref, rd_ref = some(2)
+    b_refs = some(row_n)
+    s_hot, wb_hot, x_cols, cd_hot = some(hot_count), some(hot_count), some(hot_count), some(hot_count)
+    rows_ref, cols_ref = refs
+    scale = 1.0 / half_width
+
+    def dot(a, b):
+        return jnp.dot(a, b, preferred_element_type=jnp.float32)
+
+    size = rows_ref.shape[1]
+    acc = dot(jnp.concatenate([w[...] for w in wa_hot], axis=0), s_ref[...])
+    beta = jnp.concatenate([wide([b[0] for b in blocks]) for blocks in b_hot], axis=0)
+    acc = acc + dot(beta, wb_ref[0])
+    for h in range(hot_count):
+        value = acc[h * size:(h + 1) * size] + (rd_hot[h][...] + cd_ref[...] - center) * x_rows[h][...]
+        rows_ref[h] = (value * scale).astype(rows_ref.dtype)
+    acc = dot(wa_ref[...], wide([s[...] for s in s_hot]))
+    acc = acc + dot(wide([b[0] for b in b_refs]), wide([w[0] for w in wb_hot]))
+    for h in range(hot_count):
+        value = acc[:, h * size:(h + 1) * size] + (rd_ref[...] + cd_hot[h][...] - center) * x_cols[h][...]
+        cols_ref[h] = (value * scale).astype(cols_ref.dtype)
+
+
+def hot_step(place, hot, sel, wa, s, wb, rd, cd, cols, x, row_n, ratio):
+    height, width = x.shape
+    size = cols.shape[-1]
+    hot_count = hot.shape[0] // row_n
+    tile_width = width // ratio
+    stripe = 256 if tile_width % 256 == 0 else size
+    per_tile = tile_width // stripe
+    blocks = tile_width // size
+    depth = s.shape[0]
+
+    def tile(n):
+        return jnp.minimum(n // per_tile, ratio - 1)
+
+    def hot_row(h, place, hot):
+        return hot[place[0] * hot_count + h]
+
+    def hot_col(h, n, place, hot):
+        return hot[(place[1] * ratio + tile(n)) * hot_count + h]
+
+    def source(q, n, place, sel):
+        return q * hot_count + sel[(place[1] * ratio + tile(n)) * row_n + q]
+
+    spec = pl.BlockSpec
+    each = range(hot_count)
+    in_specs = [spec((size, depth), lambda n, place, hot, sel, h=h: (hot_row(h, place, hot), 0)) for h in each]
+    in_specs += [spec((size, stripe), lambda n, place, hot, sel, h=h: (hot_row(h, place, hot), n)) for h in each]
+    in_specs += [spec((size, 1), lambda n, place, hot, sel, h=h: (hot_row(h, place, hot), 0)) for h in each]
+    in_specs += [spec((1, size, size), lambda n, place, hot, sel, h=h, q=q: (source(q, n, place, sel), hot_row(h, place, hot), 0))
+                 for h in each for q in range(row_n)]
+    in_specs += [
+        spec((depth, stripe), lambda n, *_: (0, n)),
+        spec((1, depth, stripe), lambda n, *_: (n // per_tile, 0, n % per_tile)),
+        spec((1, stripe), lambda n, *_: (0, n)),
+        spec((stripe, depth), lambda n, *_: (n % per_tile, 0)),
+        spec((stripe, 1), lambda n, *_: (n % per_tile, 0)),
+    ]
+    in_specs += [spec((1, stripe, size), lambda n, place, hot, sel, q=q: (source(q, n, place, sel), n % per_tile, 0)) for q in range(row_n)]
+    in_specs += [spec((depth, size), lambda n, place, hot, sel, h=h: (0, tile(n) * blocks + hot_col(h, n, place, hot))) for h in each]
+    in_specs += [spec((1, depth, size), lambda n, place, hot, sel, h=h: (tile(n), 0, hot_col(h, n, place, hot))) for h in each]
+    in_specs += [spec((stripe, size), lambda n, place, hot, sel, h=h: (n % per_tile, tile(n) * blocks + hot_col(h, n, place, hot))) for h in each]
+    in_specs += [spec((1, size), lambda n, place, hot, sel, h=h: (0, tile(n) * blocks + hot_col(h, n, place, hot))) for h in each]
+    args = [wa] * hot_count + [x] * hot_count + [rd] * hot_count + [cols] * (hot_count * row_n)
+    args += [s, wb, cd, wa, rd] + [cols] * row_n + [s] * hot_count + [wb] * hot_count + [x] * hot_count + [cd] * hot_count
+    grid_spec = pltpu.PrefetchScalarGridSpec(
+        num_scalar_prefetch=3,
+        grid=(width // stripe,),
+        in_specs=in_specs,
+        out_specs=[
+            spec((hot_count, size, stripe), lambda n, *_: (0, 0, n)),
+            spec((hot_count, stripe, size), lambda n, *_: (n // per_tile, n % per_tile, 0)),
+        ],
+    )
+    return pl.pallas_call(
+        functools.partial(hot_kernel, row_n, hot_count),
+        out_shape=[
+            jax.ShapeDtypeStruct((hot_count, size, width), jnp.bfloat16),
+            jax.ShapeDtypeStruct((ratio * hot_count, height, size), jnp.bfloat16),
+        ],
+        grid_spec=grid_spec,
+        compiler_params=pltpu.CompilerParams(vmem_limit_bytes=VMEM_LIMIT),
+    )(place, hot, sel, *args)
+
+
+def first_hops(rows, cols, row_n, col_n):
+    line, lanes, chips, cores = layout(row_n, col_n)
+    upward = [(r, r + lanes) for r in range(row_n - lanes)]
+    below = lax.ppermute(rows, "row", upward)
+    above = lax.ppermute(rows, "row", [(b, a) for a, b in upward])
+    turn = [(c, (c // cores + 1) % chips * cores + c % cores) for c in range(col_n)]
+    return [below, above, lax.ppermute(cols, "col", turn)]
 
 
 def filter_kernel(source_count, row_chunk, last, place, sel, wa_ref, s_ref, wb_ref, rd_ref, cd_ref, *refs):
@@ -491,6 +636,8 @@
         functools.partial(filter_kernel, row_n, row_chunk, last),
         out_shape=jax.ShapeDtypeStruct(x.shape, jnp.float32),
         grid_spec=grid_spec,
+        cost_estimate=pl.CostEstimate(
+            flops=4 * height * width * s.shape[0], bytes_accessed=4 * 3 * height * width, transcendentals=0),
         compiler_params=pltpu.CompilerParams(vmem_limit_bytes=VMEM_LIMIT),
     )(place, sel, *args)
 
@@ -512,14 +659,16 @@
     depth = row_n * size
 
     rows, cols = pack(start_vector, place, hot, row_n, ratio, size)
-    s, b, hams = exchange(rows, cols, ham_blocks, sel, row_n, col_n, 0)
+    s, b, hams = exchange(rows, cols, ham_blocks, None, sel, row_n, col_n, 0)
     s = s.reshape(depth, width)
     wa = dense(ham_blocks[None], place[:1], pairs, pair_counts, (height, depth), False)[0]
     mirrors = (col_index * ratio + jnp.arange(ratio)).astype(jnp.int32)
     wb = dense(hams, mirrors, pairs, pair_counts, (depth, width // ratio), True)
+    rows, cols = hot_step(place, hot, sel, wa, s, wb, rd, cd, b, start_vector, row_n, ratio)
+    ahead = first_hops(rows, cols, row_n, col_n)
+    s, _ = lax.optimization_barrier((s, rows))
     first = filter_step(place, sel, wa, s, wb, rd, cd, b, start_vector, None, row_n, ratio)
-    rows, cols = pack(first, place, hot, row_n, ratio, size)
-    s, b = exchange(rows, cols, None, sel, row_n, col_n, 1)
+    s, b = exchange(rows, cols, None, ahead, sel, row_n, col_n, 1)
     second = filter_step(place, sel, wa, s.reshape(depth, width), wb, rd, cd, b, first, start_vector, row_n, ratio)
     return (first, second)
 

time: 367 us -> 365 us (level)
  Pallas kernels: 355 us -> 345 us
    pallas_call x2, Pallas kernels: 256 us -> 229 us  [exchange(): pl.pallas_call(functools.partial(exchange_kernel, row_n, col_n, pieces, h...]
    pallas_call x0 -> x1, Pallas kernels: none -> 23.7 us  [hot_step(): pl.pallas_call(functools.partial(hot_kernel, row_n, hot_count), out_shape...]
    pallas_call x2 -> x1, Pallas kernels: 11.2 us -> 5.61 us  [pack(): pl.pallas_call(pack_kernel, out_shape=[jax.ShapeDtypeStruct((hot_count, s...]
  transfers between devices with their start and end apart: 0 -> 3, of which waited for: 0 -> 0; matrix products, arithmetic and copies ran while one was open for 0% -> 0% of each run, Pallas kernels for 0% -> 10%
where the time goes in v2:
time: 365 us; the launch traced here: 359 us
  Pallas kernels  345 us (95%)
  local copies, waits for them, and re-layouts  9.59 us (3%)
    pallas_call x2, Pallas kernels, exchange(): pl.pallas_call(functools.partial(exchange_kernel, row_n, col_n, pieces, h...  229 us
    pallas_call x2, Pallas kernels, filter_step(): pl.pallas_call(functools.partial(filter_kernel, row_n, row_chunk, last),...  70.4 us
    pallas_call x1, Pallas kernels, hot_step(): pl.pallas_call(functools.partial(hot_kernel, row_n, hot_count), out_shape...  23.7 us
    pallas_call x2, Pallas kernels, dense(): pl.pallas_call(functools.partial(dense_kernel, transposed), out_shape=jax...  15.4 us
  transfers between devices with their start and end apart: 3, of which 0 were waited for; matrix products, arithmetic and copies ran while one was open for 0% of the time, Pallas kernels for 10%

profile of v2, /device:TPU:24, one launch (start us, length us, event | category | flops | bytes accessed | tf_op | source)
XLA Modules:
  0.0 358.8 jit_solution(1850504515530301287)
XLA Ops:
  0.6 0.6 iota_add_fusion.tiles
  1.2 1.2 reshape.19.sel
  2.5 0.8 copy.10
  3.2 0.6 reshape.21.hot
  3.9 1.4 reshape.20.pairs
  5.2 0.8 dynamic_slice.6
  6.0 1.3 dynamic_slice.7
  7.3 1.2 broadcast_in_dim.12.refs_4_.refs_5_.refs_26_.rd_ref
  8.5 0.6 pad_add_fusion.place
  9.1 5.1 %shard_map.86 = bf16[1,1536,1024]{2,1,0:T(8,128)(2,1)} custom-call(s32[1]{0:T(128)} %bitcast.tiles, s32[1536]{0:T(1024)} %reshape.20.pairs, s32[8]{0:T(128)} %counts.3, bf16[1,48,128,128]{3,2,1,0:T(8,128)(2,1)} %bitcast.17), custom_call_target="tpu_custom_call" | custom-call | tf_op jit(solution)/shard_map/pallas_call | solution.py:46
  14.2 5.6 %shard_map.87 = (bf16[2,128,3072]{2,1,0:T(8,128)(2,1)}, bf16[4,1536,128]{2,1,0:T(8,128)(2,1)}) custom-call(s32[2]{0:T(128)} %pad_add_fusion.place, s32[16]{0:T(128)} %reshape.21.hot, f32[1536,3072]{1,0:T(8,128)} %refs_9_.1, f32[1536,3072]{1,0:T(8,128)} %refs_9_.1), custom_call_target="tpu_custom_call" | custom-call | tf_op jit(solution)/shard_map/pallas_call | solution.py:83
  19.8 150.5 %shard_map.88 = (bf16[8,128,3072]{2,1,0:T(8,128)(2,1)}, bf16[16,1536,128]{2,1,0:T(8,128)(2,1)}, bf16[2,48,128,128]{3,2,1,0:T(8,128)(2,1)}) custom-call(s32[64]{0:T(128)} %reshape.19.sel, bf16[2,128,3072]{2,1,0:T(8,128)(2,1)} %get-tuple-element.12.rows_ref, bf16[4,1536,128]{2,1,0:T(8,128)(2,1)} %get-tuple-element.13.cols_ref, bf16[48,128,128]{2,1,0:T(8,128)(2,1)} %refs_0_.1), custom_call_target="tpu_custom_call" | custom-call | tf_op jit(solution)/shard_map/pallas_call | solution.py:468
  170.3 10.3 %shard_map.89.refs_23_.refs_37_.refs_38_.wb_ref = bf16[2,1024,1536]{2,1,0:T(8,128)(2,1)} custom-call(s32[2]{0:T(128)} %iota_add_fusion.tiles, s32[1536]{0:T(1024)} %reshape.20.pairs, s32[8]{0:T(128)} %counts.3, bf16[2,48,128,128]{3,2,1,0:T(8,128)(2,1)} %get-tuple-element.16.ham_ref), custom_call_target="tpu_custom_call" | custom-call | tf_op jit(solution)/shard_map/pallas_call | solution.py:46
  180.7 23.7 %shard_map.90 = (bf16[2,128,3072]{2,1,0:T(8,128)(2,1)}, bf16[4,1536,128]{2,1,0:T(8,128)(2,1)}) custom-call(s32[2]{0:T(128)} %pad_add_fusion.place, s32[16]{0:T(128)} %reshape.21.hot, s32[64]{0:T(128)} %reshape.19.sel, bf16[1536,1024]{1,0:T(8,128)(2,1)} %bitcast.7, bf16[1536,1024]{1,0:T(8,128)(2,1)} %bitcast.8, f32[1536,3072]{1,0:T(8,128)} %refs_9_.1, ...), custom_call_target="tpu_custom_call" | custom-call | tf_op jit(solution)/shard_map/pallas_call | solution.py:565
  204.3 1.4 collective-permute-start.1
  205.7 1.3 collective-permute-start
  207.0 0.1 collective-permute-start.2
  207.1 34.2 %shard_map.91.refs_8_ = f32[1536,3072]{1,0:T(8,128)} custom-call(s32[2]{0:T(128)} %pad_add_fusion.place, s32[64]{0:T(128)} %reshape.19.sel, bf16[1536,1024]{1,0:T(8,128)(2,1)} %bitcast.10, bf16[1024,3072]{1,0:T(8,128)(2,1)} %bitcast.15, bf16[2,1024,1536]{2,1,0:T(8,128)(2,1)} %shard_map.89.refs_23_.refs_37_.refs_38_.wb_ref, ...), custom_call_target="tpu_custom_call" | custom-call | flops 19327352832 | bytes 56623104 | tf_op jit(solution)/shard_map/pallas_call | solution.py:635
  241.3 0.0 collective-permute-done.2.refs_2_
  241.3 0.0 collective-permute-done.1.refs_1_
  241.3 0.0 copy-start
  241.4 0.0 collective-permute-done.refs_0_
  241.4 1.1 copy-done
  242.5 0.0 copy-start.1
  242.5 1.2 copy-done.1
  243.7 78.9 %shard_map.92 = (bf16[8,128,3072]{2,1,0:T(8,128)(2,1)}, bf16[16,1536,128]{2,1,0:T(8,128)(2,1)}) custom-call(s32[64]{0:T(128)} %reshape.19.sel, bf16[2,128,3072]{2,1,0:T(8,128)(2,1)} %get-tuple-element.17.rows_ref, bf16[4,1536,128]{2,1,0:T(8,128)(2,1)} %get-tuple-element.19.cols_ref, bf16[2,128,3072]{2,1,0:T(8,128)(2,1)} %copy-done.1, ...), custom_call_target="tpu_custom_call" | custom-call | tf_op jit(solution)/shard_map/pallas_call | solution.py:468
  322.6 36.2 %shard_map.93 = f32[1536,3072]{1,0:T(8,128)} custom-call(s32[2]{0:T(128)} %pad_add_fusion.place, s32[64]{0:T(128)} %reshape.19.sel, bf16[1536,1024]{1,0:T(8,128)(2,1)} %bitcast.11, bf16[1024,3072]{1,0:T(8,128)(2,1)} %bitcast.16, bf16[2,1024,1536]{2,1,0:T(8,128)(2,1)} %shard_map.89.refs_23_.refs_37_.refs_38_.wb_ref, ...), custom_call_target="tpu_custom_call" | custom-call | flops 19327352832 | bytes 56623104 | tf_op jit(solution)/shard_map/pallas_call | solution.py:635
Async XLA Ops:
  204.3 37.0 %collective-permute-start.1 = (bf16[2,128,3072]{2,1,0:T(8,128)(2,1)}, bf16[2,128,3072]{2,1,0:T(8,128)(2,1)S(1)}, u32[]{:S(2)}, u32[]{:S(2)}) collective-permute-start(bf16[2,128,3072]{2,1,0:T(8,128)(2,1)} %get-tuple-element.17.rows_ref), channel_id=1, source_target_pairs={{8,0},{12,4},{16,8},{20,12},{24,16},{28,20},{9,1},{13,5},{17,9},{2... | collective-permute-start | bytes 4718600 | tf_op jit(solution)/shard_map/ppermute | solution.py:580
  205.7 35.6 %collective-permute-start = (bf16[2,128,3072]{2,1,0:T(8,128)(2,1)}, bf16[2,128,3072]{2,1,0:T(8,128)(2,1)S(1)}, u32[]{:S(2)}, u32[]{:S(2)}) collective-permute-start(bf16[2,128,3072]{2,1,0:T(8,128)(2,1)} %get-tuple-element.17.rows_ref), channel_id=1, source_target_pairs={{0,8},{4,12},{8,16},{12,20},{16,24},{20,28},{1,9},{5,13},{9,17},{1... | collective-permute-start | bytes 4718600 | tf_op jit(solution)/shard_map/ppermute | solution.py:579
  207.0 34.3 %collective-permute-start.2 = (bf16[4,1536,128]{2,1,0:T(8,128)(2,1)}, bf16[4,1536,128]{2,1,0:T(8,128)(2,1)}, u32[]{:S(2)}, u32[]{:S(2)}) collective-permute-start(bf16[4,1536,128]{2,1,0:T(8,128)(2,1)} %get-tuple-element.19.cols_ref), channel_id=1, source_target_pairs={{0,2},{1,3},{2,0},{3,1},{4,6},{5,7},{6,4},{7,5},{8,10},{9,11},{10,... | collective-permute-start | bytes 4718600 | tf_op jit(solution)/shard_map/ppermute | solution.py:582
  241.3 1.1 copy-start
  242.5 1.2 copy-start.1

commit v3 on v2

--- a/solution.py
+++ b/solution.py
@@ -153,28 +153,41 @@
 
 def exchange_kernel(row_n, col_n, pieces, with_ham, ahead, sel, rows_ref, cols_ref, *refs):
     g = Grid(row_n, col_n)
+    refs = list(refs)
+
+    def some(count):
+        taken = refs[:count]
+        del refs[:count]
+        return taken
+
     first_step = 2 if ahead else 1
     if ahead:
-        below_ref, above_ref, chip_ref = refs[:3]
-        refs = refs[3:]
+        below_ref, above_ref, chip_ref = some(3)
     if with_ham:
-        ham_ref, s_out, c_out, h_out = refs[:4]
-        refs = refs[4:]
-    else:
-        s_out, c_out = refs[:2]
-        refs = refs[2:]
-    held, lane_buf, own_buf, col_buf, own_sem, line_recv, up_send, down_send, lane_send, lane_recv = refs[:10]
-    chip_send, chip_recv, core_send, core_recv = refs[10:14]
+        (ham_ref,) = some(1)
+    s_out, c_out = some(2)
     if with_ham:
-        ham_buf, ham_sem, ham_recv, ham_up, ham_down, ham_lane = refs[14:]
-        ratio = row_n // col_n
+        (h_out,) = some(1)
+    held, lane_buf, own_buf, col_buf, pair_buf, turn_buf, got, turned = some(8)
+    own_sem, line_recv, up_send, down_send, lane_send, lane_recv = some(6)
+    chip_send, chip_recv, core_send, core_recv, pair_sem, got_send, got_recv = some(7)
+    if ahead:
+        ahead_buf, ahead_sem = some(2)
+    if with_ham:
+        ham_buf, far_buf, ham_sem, ham_recv, ham_up, ham_down, ham_lane, far_recv, far_send, far_chip = some(10)
         ham_rows = ham_ref.shape[0] // pieces
-    if ahead:
-        ahead_buf, ahead_sem = refs[14:]
+    ratio = row_n // col_n
     hot_count, size = rows_ref.shape[0], rows_ref.shape[1]
+    height = cols_ref.shape[1]
     piece = size // pieces
     block_n = cols_ref.shape[0]
     line, lanes, at = g.line, g.lanes, g.at
+
+    home = (g.col * ratio) // lanes
+    diag = at == home
+    up_ok = (at + 1 < line) & ((home != line - 1) | (at + 1 != line - 1))
+    down_ok = (at > 0) & ((home != 0) | (at - 1 != 0))
+    deaf = diag & ((at == 0) | (at == line - 1))
 
     take = pltpu.make_async_copy(rows_ref, held.at[at], own_sem.at[0])
     take_cols = pltpu.make_async_copy(cols_ref, col_buf, own_sem.at[1])
@@ -252,40 +265,91 @@
             lane_buf.at[step - 1, slot, rows, :], s_out.at[slot * lanes + g.lane, rows, :],
             lane_send.at[step - 1, slot, p], lane_recv.at[step - 1, slot, p], g.other_lane(step))
 
-    def choose(target, source, slot, p, out):
-        rows = pl.ds(pl.multiple_of(p * piece, piece), piece)
+    def pick(target, source, blocks):
         which = sel[target * row_n + source]
-        value = held[slot, 0, rows, :]
+        value = blocks[0]
         for h in range(1, hot_count):
-            value = jnp.where(which == h, held[slot, h, rows, :], value)
-        out[slot, rows, :] = value
+            value = jnp.where(which == h, blocks[h], value)
+        return value
 
     def select(slot, p):
         source = slot * lanes + g.lane
+        rows = pl.ds(pl.multiple_of(p * piece, piece), piece)
+        blocks = [held[slot, h, rows, :] for h in range(hot_count)]
         for step in range(1, lanes):
-            choose(at * lanes + lax.rem(g.lane + step, lanes), source, slot, p, lane_buf.at[step - 1])
+            target = at * lanes + lax.rem(g.lane + step, lanes)
+            lane_buf[step - 1, slot, rows, :] = pick(target, source, blocks)
             lane_copy(step, slot, p).start()
-        choose(g.row, source, slot, p, own_buf)
-
+        own_buf[slot, rows, :] = pick(g.row, source, blocks)
+
+    def tile_place(col, i):
+        tile = col * ratio + i
+        return tile // lanes, lax.rem(tile, lanes)
+
+    detour = g.chips % 2 == 0 and g.chips > 1
+    across = g.chips // 2
+    end = jnp.where(2 * home < line, line - 1, 0)
     if with_ham:
         def ham_part(ref, p):
             return ref.at[pl.ds(pl.multiple_of(p * ham_rows, ham_rows), ham_rows)]
 
         def ham_copies(i, p):
-            part_of = ham_part(h_out.at[i], p)
-            up = remote(part_of, part_of, ham_up.at[i, p], ham_recv.at[i, p], g.on_line(at + 1))
-            down = remote(part_of, part_of, ham_down.at[i, p], ham_recv.at[i, p], g.on_line(at - 1))
-            over = [remote(part_of, part_of, ham_lane.at[i, step - 1, p], ham_recv.at[i, p], g.other_lane(step))
+            here = ham_part(h_out.at[i], p)
+            up = remote(here, here, ham_up.at[i, p], ham_recv.at[i, p], g.on_line(at + 1))
+            down = remote(here, here, ham_down.at[i, p], ham_recv.at[i, p], g.on_line(at - 1))
+            over = [remote(here, here, ham_lane.at[i, step - 1, p], ham_recv.at[i, p], g.other_lane(step))
                     for step in range(1, lanes)]
             return up, down, over
 
-        def ham_place(i):
-            tile = g.col * ratio + i
-            return tile // lanes, lax.rem(tile, lanes)
+        def ham_sends(i, p, act):
+            _, home_lane = tile_place(g.col, i)
+            up, down, over = ham_copies(i, p)
+            skip = end if detour else line
+
+            @pl.when(home_lane == g.lane)
+            def _():
+                @pl.when((at >= home) & (at + 1 < line) & (at + 1 != skip))
+                def _():
+                    act(up)
+
+                @pl.when((at <= home) & (at > 0) & (at - 1 != skip))
+                def _():
+                    act(down)
+
+                for copy in over:
+                    act(copy)
+
+        if detour:
+            far_col = lax.rem(g.chip + across, g.chips) * g.cores + g.core
+            far_home = (far_col * ratio) // lanes
+            far_end = jnp.where(2 * far_home < line, line - 1, 0)
+            rising = far_end > far_home
+            far_away = jnp.where(rising, at - far_home, far_home - at)
+
+            def far_copies(i, p):
+                here = ham_part(far_buf, p)
+                way = jnp.where(rising, at + 1, at - 1)
+                on = remote(here, here, far_send.at[p], far_recv.at[p], g.on_line(way))
+                chip = remote(here, ham_part(h_out.at[i], p), far_chip.at[p], ham_recv.at[i, p], g.other_chip(across))
+                return on, chip
+
+            def far_sends(i, p, act):
+                _, far_lane = tile_place(far_col, i)
+                on, chip = far_copies(i, p)
+
+                @pl.when((far_lane == g.lane) & (far_away >= 0))
+                def _():
+                    @pl.when(at != far_end)
+                    def _():
+                        act(on)
+
+                    @pl.when(at == far_end)
+                    def _():
+                        act(chip)
 
         take_ham.wait()
         for i in range(ratio):
-            home, home_lane = ham_place(i)
+            _, home_lane = tile_place(g.col, i)
 
             @pl.when((home == at) & (home_lane == g.lane))
             def _():
@@ -293,50 +357,18 @@
                 put.start()
                 put.wait()
 
-        def ham_sends(i, p, act):
-            home, home_lane = ham_place(i)
-            up, down, over = ham_copies(i, p)
-
-            @pl.when(home_lane == g.lane)
-            def _():
-                @pl.when((at >= home) & (at + 1 < line))
+            if detour:
+                _, far_lane = tile_place(far_col, i)
+
+                @pl.when((far_home == at) & (far_lane == g.lane))
                 def _():
-                    act(up)
-
-                @pl.when((at <= home) & (at > 0))
-                def _():
-                    act(down)
-
-                for copy in over:
-                    act(copy)
-
-    def advance(n, carry):
-        s, p = n // pieces, lax.rem(n, pieces)
-        below, above = at - s, at + s
-
-        @pl.when(below >= 0)
-        def _():
-            @pl.when(s >= first_step)
-            def _():
-                up_copy(below, p).wait_recv()
-
-            @pl.when((at + 1 < line) & (s >= first_step - 1))
-            def _():
-                up_copy(below, p).start()
-
-        @pl.when(above < line)
-        def _():
-            @pl.when(s >= first_step)
-            def _():
-                down_copy(above, p).wait_recv()
-
-            @pl.when((at > 0) & (s >= first_step - 1))
-            def _():
-                down_copy(above, p).start()
-
-        if with_ham:
+                    put = pltpu.make_async_copy(ham_ref, far_buf, ham_sem.at[0])
+                    put.start()
+                    put.wait()
+
+        def ham_step(s, p):
             for i in range(ratio):
-                home, home_lane = ham_place(i)
+                _, home_lane = tile_place(g.col, i)
                 away = jnp.where(at >= home, at - home, home - at)
 
                 @pl.when((home_lane == g.lane) & (away == s))
@@ -347,11 +379,59 @@
 
                     ham_sends(i, p, lambda copy: copy.start())
 
-        @pl.when(below >= 0)
+                if detour:
+                    _, far_lane = tile_place(far_col, i)
+
+                    @pl.when((far_lane == g.lane) & (far_away == s))
+                    def _():
+                        @pl.when(s > 0)
+                        def _():
+                            far_copies(i, p)[0].wait_recv()
+
+                        far_sends(i, p, lambda copy: copy.start())
+
+        def ham_start(p, carry):
+            ham_step(0, p)
+            return carry
+
+        lax.fori_loop(0, pieces, ham_start, 0)
+
+    def advance(n, carry):
+        s, p = n // pieces, lax.rem(n, pieces)
+        below, above = at - s, at + s
+        hears_below = (below >= 0) & ((s == 0) | (deaf == False))
+        hears_above = (above < line) & ((s == 0) | (deaf == False))
+
+        @pl.when(hears_below)
+        def _():
+            @pl.when(s >= first_step)
+            def _():
+                up_copy(below, p).wait_recv()
+
+            @pl.when(up_ok & (s >= first_step - 1))
+            def _():
+                up_copy(below, p).start()
+
+        @pl.when(hears_above)
+        def _():
+            @pl.when(s >= first_step)
+            def _():
+                down_copy(above, p).wait_recv()
+
+            @pl.when(down_ok & (s >= first_step - 1))
+            def _():
+                down_copy(above, p).start()
+
+        if with_ham:
+            @pl.when(s > 0)
+            def _():
+                ham_step(s, p)
+
+        @pl.when(hears_below & (at != home))
         def _():
             select(below, p)
 
-        @pl.when((above < line) & (s > 0))
+        @pl.when(hears_above & (s > 0) & (at != home))
         def _():
             select(above, p)
 
@@ -364,37 +444,146 @@
             if g.cores == 2:
                 core_copy(step, b).start()
 
-    lax.fori_loop(0, pieces * (line // 2), advance, 0)
+    def core_came(step, b):
+        other = lax.rem(g.core + 1, g.cores)
+        slot = (lax.rem(g.chip - step + g.chips, g.chips) * g.cores + other) * block_n + b
+        return remote(cols_ref.at[b], c_out.at[slot], core_send.at[step, b], core_recv.at[step, b], g.other_core())
+
+    def pair_copy(q, turn):
+        return pltpu.make_async_copy(c_out.at[pl.ds(q * hot_count, hot_count)], pair_buf.at[turn], pair_sem.at[turn])
+
+    def turn_copy(i, step, q):
+        return remote(turn_buf.at[step - 1, q], got.at[i, q], got_send.at[step - 1, q], got_recv.at[i, q], g.other_lane(step))
+
+    def hand_out(q, carry):
+        turn = lax.rem(q, 2)
+
+        @pl.when(q + 1 < row_n)
+        def _():
+            pair_copy(q + 1, 1 - turn).start()
+
+        pair_copy(q, turn).wait()
+        for i in range(ratio):
+            _, home_lane = tile_place(g.col, i)
+
+            @pl.when(home_lane == g.lane)
+            def _():
+                def rows_of(k, carry):
+                    rows = pl.ds(pl.multiple_of(k * size, size), size)
+                    blocks = [pair_buf[turn, h, rows, :] for h in range(hot_count)]
+                    for step in range(1, lanes):
+                        target = at * lanes + lax.rem(g.lane + step, lanes)
+                        turn_buf[step - 1, q, rows, :] = pick(target, q, blocks)
+                    got[i, q, rows, :] = pick(g.row, q, blocks)
+                    return carry
+
+                lax.fori_loop(0, height // size, rows_of, 0)
+                for step in range(1, lanes):
+                    turn_copy(i, step, q).start()
+        return carry
+
+    def turn_over(i, q):
+        for k in range(height // size):
+            block = got[i, q, k * size:(k + 1) * size, :].astype(jnp.float32)
+            turned[q, :, i * height + k * size:i * height + (k + 1) * size] = block.T.astype(turned.dtype)
+
+    def turn_own(q):
+        for i in range(ratio):
+            _, home_lane = tile_place(g.col, i)
+
+            @pl.when(home_lane == g.lane)
+            def _():
+                turn_over(i, q)
+
+    def turn_come(q, carry):
+        for i in range(ratio):
+            _, home_lane = tile_place(g.col, i)
+
+            @pl.when(home_lane != g.lane)
+            def _():
+                turn_copy(i, 1, q).wait_recv()
+                turn_over(i, q)
+        pltpu.make_async_copy(turned.at[q], s_out.at[q], pair_sem.at[2 + q]).start()
+        return carry
+
+    half = pieces * (line // 2)
+    per_step = -(-row_n // half)
+    lax.fori_loop(0, half, advance, 0)
     for step in range(first_step, g.chips):
         columns(step)
-    lax.fori_loop(pieces * (line // 2), pieces * line, advance, 0)
-
-    for slot in range(line):
-        pltpu.make_async_copy(own_buf.at[slot], s_out.at[slot * lanes + g.lane], own_sem.at[2 + slot]).start()
-
-    for slot in range(line):
-        pltpu.make_async_copy(own_buf.at[slot], s_out.at[slot * lanes + g.lane], own_sem.at[2 + slot]).wait()
+
     put_cols.wait()
     if ahead:
         put_chip.wait()
+    if g.cores == 2:
+        for step in range(g.chips):
+            for b in range(block_n):
+                core_came(step, b).wait_recv()
+
+    @pl.when(diag)
+    def _():
+        pair_copy(0, 0).start()
+        lax.fori_loop(0, row_n, hand_out, 0)
+
+    def advance_late(n, carry):
+        advance(n, carry)
+
+        @pl.when(diag)
+        def _():
+            for u in range(per_step):
+                q = (n - half) * per_step + u
+
+                @pl.when(q < row_n)
+                def _():
+                    turn_own(q)
+        return carry
+
+    lax.fori_loop(half, 2 * half, advance_late, 0)
+
+    @pl.when(diag)
+    def _():
+        lax.fori_loop(0, row_n, turn_come, 0)
+        for q in range(row_n):
+            pltpu.make_async_copy(turned.at[q], s_out.at[q], pair_sem.at[2 + q]).wait()
+
+        def sent(q, carry):
+            for i in range(ratio):
+                _, home_lane = tile_place(g.col, i)
+
+                @pl.when(home_lane == g.lane)
+                def _():
+                    for step in range(1, lanes):
+                        turn_copy(i, step, q).wait_send()
+            return carry
+
+        lax.fori_loop(0, row_n, sent, 0)
+
+    @pl.when(at != home)
+    def _():
+        for slot in range(line):
+            pltpu.make_async_copy(own_buf.at[slot], s_out.at[slot * lanes + g.lane], own_sem.at[2 + slot]).start()
+        for slot in range(line):
+            pltpu.make_async_copy(own_buf.at[slot], s_out.at[slot * lanes + g.lane], own_sem.at[2 + slot]).wait()
 
     def finish(n, carry):
         slot, p = n // pieces, lax.rem(n, pieces)
 
-        @pl.when((slot <= at + 1 - first_step) & (at + 1 < line))
+        @pl.when((slot <= at + 1 - first_step) & up_ok)
         def _():
             up_copy(slot, p).wait_send()
 
-        @pl.when((slot >= at - 1 + first_step) & (at > 0))
+        @pl.when((slot >= at - 1 + first_step) & down_ok)
         def _():
             down_copy(slot, p).wait_send()
 
-        for step in range(1, lanes):
-            lane_copy(step, slot, p).wait_send()
-            came = slot * lanes + lax.rem(g.lane - step + lanes, lanes)
-            rows = pl.ds(pl.multiple_of(p * piece, piece), piece)
-            remote(lane_buf.at[step - 1, slot, rows, :], s_out.at[came, rows, :], lane_send.at[step - 1, slot, p],
-                   lane_recv.at[step - 1, slot, p], g.other_lane(step)).wait_recv()
+        @pl.when(at != home)
+        def _():
+            for step in range(1, lanes):
+                lane_copy(step, slot, p).wait_send()
+                came = slot * lanes + lax.rem(g.lane - step + lanes, lanes)
+                rows = pl.ds(pl.multiple_of(p * piece, piece), piece)
+                remote(lane_buf.at[step - 1, slot, rows, :], s_out.at[came, rows, :], lane_send.at[step - 1, slot, p],
+                       lane_recv.at[step - 1, slot, p], g.other_lane(step)).wait_recv()
         return carry
 
     lax.fori_loop(0, line * pieces, finish, 0)
@@ -404,15 +593,14 @@
         if g.cores == 2:
             for step in range(g.chips):
                 core_copy(step, b).wait_send()
-                other = lax.rem(g.core + 1, g.cores)
-                slot = (lax.rem(g.chip - step + g.chips, g.chips) * g.cores + other) * block_n + b
-                remote(cols_ref.at[b], c_out.at[slot], core_send.at[step, b], core_recv.at[step, b], g.other_core()).wait_recv()
     if with_ham:
         for i in range(ratio):
-            home, home_lane = ham_place(i)
+            _, home_lane = tile_place(g.col, i)
 
             def settle(p, carry):
                 ham_sends(i, p, lambda copy: copy.wait_send())
+                if detour:
+                    far_sends(i, p, lambda copy: copy.wait_send())
 
                 @pl.when(home_lane != g.lane)
                 def _():
@@ -428,41 +616,54 @@
     ratio = row_n // col_n
     pieces = 4
     line, lanes, chips, _ = layout(row_n, col_n)
+    others = max(lanes - 1, 1)
     dma = pltpu.SemaphoreType.DMA
+    vmem = lambda *shape: pltpu.VMEM(shape, jnp.bfloat16)
     anywhere = pl.BlockSpec(memory_space=pl.ANY)
     out_shape = [
         jax.ShapeDtypeStruct((row_n, size, width), jnp.bfloat16),
         jax.ShapeDtypeStruct((col_n * block_n, height, size), jnp.bfloat16),
     ]
     scratch = [
-        pltpu.VMEM((line, hot_count, size, width), jnp.bfloat16),
-        pltpu.VMEM((max(lanes - 1, 1), line, size, width), jnp.bfloat16),
-        pltpu.VMEM((line, size, width), jnp.bfloat16),
-        pltpu.VMEM(cols.shape, jnp.bfloat16),
+        vmem(line, hot_count, size, width),
+        vmem(others, line, size, width),
+        vmem(line, size, width),
+        vmem(*cols.shape),
+        vmem(2, hot_count, height, size),
+        vmem(others, row_n, height, size),
+        vmem(ratio, row_n, height, size),
+        vmem(row_n, size, width),
         dma((2 + line,)),
         dma((line, pieces)),
         dma((line, pieces)),
         dma((line, pieces)),
-        dma((max(lanes - 1, 1), line, pieces)),
-        dma((max(lanes - 1, 1), line, pieces)),
+        dma((others, line, pieces)),
+        dma((others, line, pieces)),
         dma((max(chips - 1, 1), block_n)),
         dma((max(chips - 1, 1), block_n)),
         dma((chips, block_n)),
         dma((chips, block_n)),
+        dma((2 + row_n,)),
+        dma((others, row_n)),
+        dma((ratio, row_n)),
     ]
     args = [sel, rows, cols]
     if ahead is not None:
-        scratch += [pltpu.VMEM(cols.shape, jnp.bfloat16), dma((3,))]
+        scratch += [vmem(*cols.shape), dma((3,))]
         args += ahead
     if ham is not None:
         out_shape.append(jax.ShapeDtypeStruct((ratio,) + ham.shape, ham.dtype))
         scratch += [
             pltpu.VMEM(ham.shape, ham.dtype),
+            pltpu.VMEM(ham.shape, ham.dtype),
             dma((1,)),
             dma((ratio, pieces)),
             dma((ratio, pieces)),
             dma((ratio, pieces)),
-            dma((ratio, max(lanes - 1, 1), pieces)),
+            dma((ratio, others, pieces)),
+            dma((pieces,)),
+            dma((pieces,)),
+            dma((pieces,)),
         ]
         args.append(ham)
     return pl.pallas_call(
@@ -515,7 +716,7 @@
     size = cols.shape[-1]
     hot_count = hot.shape[0] // row_n
     tile_width = width // ratio
-    stripe = 256 if tile_width % 256 == 0 else size
+    stripe = tile_width // 2 if tile_width % 256 == 0 else size
     per_tile = tile_width // stripe
     blocks = tile_width // size
     depth = s.shape[0]
@@ -611,9 +812,9 @@
     size = cols.shape[-1]
     hot_count = cols.shape[0] // row_n
     tile_width = width // ratio
-    stripe = 256 if tile_width % 256 == 0 else size
+    stripe = next(n for n in (512, 384, 256, size) if tile_width % n == 0)
     per_tile = tile_width // stripe
-    row_chunk = height // 3 if height % 384 == 0 else size
+    row_chunk = height // 2 if height % 256 == 0 else height
     last = start is not None
 
     def b_spec(q):

time: 365 us -> 334 us (0.915)
  Pallas kernels: 345 us -> 314 us
    pallas_call x2, Pallas kernels: 229 us -> 212 us  [exchange(): pl.pallas_call(functools.partial(exchange_kernel, row_n, col_n, pieces, h...]
    pallas_call x2, Pallas kernels: 70.4 us -> 63.5 us  [filter_step(): pl.pallas_call(functools.partial(filter_kernel, row_n, row_chunk, last),...]
    pallas_call x1, Pallas kernels: 23.7 us -> 17.9 us  [hot_step(): pl.pallas_call(functools.partial(hot_kernel, row_n, hot_count), out_shape...]
  transfers between devices with their start and end apart: 3 -> 3, of which waited for: 0 -> 1; matrix products, arithmetic and copies ran while one was open for 0% -> 0% of each run, Pallas kernels for 10% -> 9%
where the time goes in v3:
time: 334 us; the launch traced here: 331 us
  Pallas kernels  314 us (94%)
  local copies, waits for them, and re-layouts  8.47 us (3%)
  starting transfers between devices  4.84 us (1%)
    pallas_call x2, Pallas kernels, exchange(): pl.pallas_call(functools.partial(exchange_kernel, row_n, col_n, pieces, h...  212 us
    pallas_call x2, Pallas kernels, filter_step(): pl.pallas_call(functools.partial(filter_kernel, row_n, row_chunk, last),...  63.5 us
    pallas_call x1, Pallas kernels, hot_step(): pl.pallas_call(functools.partial(hot_kernel, row_n, hot_count), out_shape...  17.9 us
    pallas_call x2, Pallas kernels, dense(): pl.pallas_call(functools.partial(dense_kernel, transposed), out_shape=jax...  14.8 us
  transfers between devices with their start and end apart: 3, of which 1 were waited for; matrix products, arithmetic and copies ran while one was open for 0% of the time, Pallas kernels for 9%

profile of v3, /device:TPU:24, one launch (start us, length us, event | category | flops | bytes accessed | tf_op | source)
XLA Modules:
  0.0 331.4 jit_solution(14747826407053310431)
XLA Ops:
  0.6 0.6 iota_add_fusion.tiles
  1.2 1.2 reshape.19.sel
  2.5 0.8 copy.10
  3.2 0.6 reshape.21.hot
  3.9 1.4 reshape.20.pairs
  5.2 0.8 dynamic_slice.6
  6.0 1.3 dynamic_slice.7
  7.3 1.2 broadcast_in_dim.12.refs_4_.refs_5_.refs_26_.rd_ref
  8.5 0.6 pad_add_fusion.place
  9.1 5.5 %shard_map.86 = bf16[1,1536,1024]{2,1,0:T(8,128)(2,1)} custom-call(s32[1]{0:T(128)} %bitcast.tiles, s32[1536]{0:T(1024)} %reshape.20.pairs, s32[8]{0:T(128)} %counts.3, bf16[1,48,128,128]{3,2,1,0:T(8,128)(2,1)} %bitcast.17), custom_call_target="tpu_custom_call" | custom-call | tf_op jit(solution)/shard_map/pallas_call | solution.py:46
  14.6 5.6 %shard_map.87 = (bf16[2,128,3072]{2,1,0:T(8,128)(2,1)}, bf16[4,1536,128]{2,1,0:T(8,128)(2,1)}) custom-call(s32[2]{0:T(128)} %pad_add_fusion.place, s32[16]{0:T(128)} %reshape.21.hot, f32[1536,3072]{1,0:T(8,128)} %refs_9_.1, f32[1536,3072]{1,0:T(8,128)} %refs_9_.1), custom_call_target="tpu_custom_call" | custom-call | tf_op jit(solution)/shard_map/pallas_call | solution.py:83
  20.2 131.0 %shard_map.88 = (bf16[8,128,3072]{2,1,0:T(8,128)(2,1)}, bf16[16,1536,128]{2,1,0:T(8,128)(2,1)}, bf16[2,48,128,128]{3,2,1,0:T(8,128)(2,1)}) custom-call(s32[64]{0:T(128)} %reshape.19.sel, bf16[2,128,3072]{2,1,0:T(8,128)(2,1)} %get-tuple-element.12.rows_ref, bf16[4,1536,128]{2,1,0:T(8,128)(2,1)} %get-tuple-element.13.cols_ref, bf16[48,128,128]{2,1,0:T(8,128)(2,1)} %refs_0_.1), custom_call_target="tpu_custom_call" | custom-call | tf_op jit(solution)/shard_map/pallas_call | solution.py:669
  151.2 9.3 %shard_map.89.refs_23_.refs_37_.refs_38_.wb_ref = bf16[2,1024,1536]{2,1,0:T(8,128)(2,1)} custom-call(s32[2]{0:T(128)} %iota_add_fusion.tiles, s32[1536]{0:T(1024)} %reshape.20.pairs, s32[8]{0:T(128)} %counts.3, bf16[2,48,128,128]{3,2,1,0:T(8,128)(2,1)} %get-tuple-element.16.ham_ref), custom_call_target="tpu_custom_call" | custom-call | tf_op jit(solution)/shard_map/pallas_call | solution.py:46
  160.5 17.9 %shard_map.90 = (bf16[2,128,3072]{2,1,0:T(8,128)(2,1)}, bf16[4,1536,128]{2,1,0:T(8,128)(2,1)}) custom-call(s32[2]{0:T(128)} %pad_add_fusion.place, s32[16]{0:T(128)} %reshape.21.hot, s32[64]{0:T(128)} %reshape.19.sel, bf16[1536,1024]{1,0:T(8,128)(2,1)} %bitcast.7, bf16[1536,1024]{1,0:T(8,128)(2,1)} %bitcast.8, f32[1536,3072]{1,0:T(8,128)} %refs_9_.1, ...), custom_call_target="tpu_custom_call" | custom-call | tf_op jit(solution)/shard_map/pallas_call | solution.py:766
  178.4 1.4 collective-permute-start.1
  179.8 1.3 collective-permute-start
  181.1 2.2 collective-permute-start.2
  183.3 30.3 %shard_map.91.refs_8_ = f32[1536,3072]{1,0:T(8,128)} custom-call(s32[2]{0:T(128)} %pad_add_fusion.place, s32[64]{0:T(128)} %reshape.19.sel, bf16[1536,1024]{1,0:T(8,128)(2,1)} %bitcast.10, bf16[1024,3072]{1,0:T(8,128)(2,1)} %bitcast.15, bf16[2,1024,1536]{2,1,0:T(8,128)(2,1)} %shard_map.89.refs_23_.refs_37_.refs_38_.wb_ref, ...), custom_call_target="tpu_custom_call" | custom-call | flops 19327352832 | bytes 56623104 | tf_op jit(solution)/shard_map/pallas_call | solution.py:836
  213.6 0.0 collective-permute-done.2.refs_2_
  213.6 0.0 collective-permute-done.1.refs_1_
  213.6 0.0 copy-start
  213.6 2.5 collective-permute-done.refs_0_
  216.1 0.0 copy-done
  216.1 0.0 copy-start.1
  216.1 1.2 copy-done.1
  217.3 80.9 %shard_map.92 = (bf16[8,128,3072]{2,1,0:T(8,128)(2,1)}, bf16[16,1536,128]{2,1,0:T(8,128)(2,1)}) custom-call(s32[64]{0:T(128)} %reshape.19.sel, bf16[2,128,3072]{2,1,0:T(8,128)(2,1)} %get-tuple-element.17.rows_ref, bf16[4,1536,128]{2,1,0:T(8,128)(2,1)} %get-tuple-element.19.cols_ref, bf16[2,128,3072]{2,1,0:T(8,128)(2,1)} %copy-done.1, ...), custom_call_target="tpu_custom_call" | custom-call | tf_op jit(solution)/shard_map/pallas_call | solution.py:669
  298.2 33.2 %shard_map.93 = f32[1536,3072]{1,0:T(8,128)} custom-call(s32[2]{0:T(128)} %pad_add_fusion.place, s32[64]{0:T(128)} %reshape.19.sel, bf16[1536,1024]{1,0:T(8,128)(2,1)} %bitcast.11, bf16[1024,3072]{1,0:T(8,128)(2,1)} %bitcast.16, bf16[2,1024,1536]{2,1,0:T(8,128)(2,1)} %shard_map.89.refs_23_.refs_37_.refs_38_.wb_ref, ...), custom_call_target="tpu_custom_call" | custom-call | flops 19327352832 | bytes 56623104 | tf_op jit(solution)/shard_map/pallas_call | solution.py:836
Async XLA Ops:
  178.4 35.2 %collective-permute-start.1 = (bf16[2,128,3072]{2,1,0:T(8,128)(2,1)}, bf16[2,128,3072]{2,1,0:T(8,128)(2,1)S(1)}, u32[]{:S(2)}, u32[]{:S(2)}) collective-permute-start(bf16[2,128,3072]{2,1,0:T(8,128)(2,1)} %get-tuple-element.17.rows_ref), channel_id=1, source_target_pairs={{8,0},{12,4},{16,8},{20,12},{24,16},{28,20},{9,1},{13,5},{17,9},{2... | collective-permute-start | bytes 4718600 | tf_op jit(solution)/shard_map/ppermute | solution.py:781
  179.8 36.2 %collective-permute-start = (bf16[2,128,3072]{2,1,0:T(8,128)(2,1)}, bf16[2,128,3072]{2,1,0:T(8,128)(2,1)S(1)}, u32[]{:S(2)}, u32[]{:S(2)}) collective-permute-start(bf16[2,128,3072]{2,1,0:T(8,128)(2,1)} %get-tuple-element.17.rows_ref), channel_id=1, source_target_pairs={{0,8},{4,12},{8,16},{12,20},{16,24},{20,28},{1,9},{5,13},{9,17},{1... | collective-permute-start | bytes 4718600 | tf_op jit(solution)/shard_map/ppermute | solution.py:780
  181.1 32.4 %collective-permute-start.2 = (bf16[4,1536,128]{2,1,0:T(8,128)(2,1)}, bf16[4,1536,128]{2,1,0:T(8,128)(2,1)}, u32[]{:S(2)}, u32[]{:S(2)}) collective-permute-start(bf16[4,1536,128]{2,1,0:T(8,128)(2,1)} %get-tuple-element.19.cols_ref), channel_id=1, source_target_pairs={{0,2},{1,3},{2,0},{3,1},{4,6},{5,7},{6,4},{7,5},{8,10},{9,11},{10,... | collective-permute-start | bytes 4718600 | tf_op jit(solution)/shard_map/ppermute | solution.py:783
  213.6 2.5 copy-start
  216.1 1.2 copy-start.1

commit v4 on v3

--- a/solution.py
+++ b/solution.py
@@ -10,6 +10,7 @@
 center = 0.25
 half_width = 2.5
 VMEM_LIMIT = 60 * 1024 * 1024
+VMEM_MOST = 67043328
 MESH = pl.DeviceIdType.MESH
 
 
@@ -151,7 +152,11 @@
     pl.semaphore_wait(barrier, fixed + up.astype(jnp.int32) + down.astype(jnp.int32))
 
 
-def exchange_kernel(row_n, col_n, pieces, with_ham, ahead, sel, rows_ref, cols_ref, *refs):
+def late_slot(at, line):
+    return jnp.where(2 * at < line, line - 1, 0)
+
+
+def exchange_kernel(row_n, col_n, pieces, with_ham, fused, sel, rows_ref, cols_ref, *refs):
     g = Grid(row_n, col_n)
     refs = list(refs)
 
@@ -160,25 +165,23 @@
         del refs[:count]
         return taken
 
-    first_step = 2 if ahead else 1
-    if ahead:
-        below_ref, above_ref, chip_ref = some(3)
-    if with_ham:
-        (ham_ref,) = some(1)
-    s_out, c_out = some(2)
-    if with_ham:
-        (h_out,) = some(1)
-    held, lane_buf, own_buf, col_buf, pair_buf, turn_buf, got, turned = some(8)
+    first_step = 2 if fused else 1
+    if fused:
+        below_ref, above_ref, chip_ref, wa_hbm, wb_hbm, rd_ref, cd_ref, x_hbm, start_hbm, s_out, acc_out = some(11)
+    else:
+        ham_ref, s_out, c_out, h_out = some(4)
+    held, lane_buf, turn_buf, s_all, c_all = some(5)
     own_sem, line_recv, up_send, down_send, lane_send, lane_recv = some(6)
-    chip_send, chip_recv, core_send, core_recv, pair_sem, got_send, got_recv = some(7)
-    if ahead:
-        ahead_buf, ahead_sem = some(2)
-    if with_ham:
+    chip_send, chip_recv, core_send, core_recv, turn_send, turn_recv = some(6)
+    if fused:
+        acc, wa, wb, x_buf, start_buf, load_sem, x_sem, start_sem, acc_sem = some(9)
+    else:
         ham_buf, far_buf, ham_sem, ham_recv, ham_up, ham_down, ham_lane, far_recv, far_send, far_chip = some(10)
         ham_rows = ham_ref.shape[0] // pieces
     ratio = row_n // col_n
     hot_count, size = rows_ref.shape[0], rows_ref.shape[1]
     height = cols_ref.shape[1]
+    width = rows_ref.shape[2]
     piece = size // pieces
     block_n = cols_ref.shape[0]
     line, lanes, at = g.line, g.lanes, g.at
@@ -189,41 +192,40 @@
     down_ok = (at > 0) & ((home != 0) | (at - 1 != 0))
     deaf = diag & ((at == 0) | (at == line - 1))
 
+    def chip_slot(step):
+        return (lax.rem(g.chip - step + g.chips, g.chips) * g.cores + g.core) * block_n
+
+    own_slot = g.col * block_n
     take = pltpu.make_async_copy(rows_ref, held.at[at], own_sem.at[0])
-    take_cols = pltpu.make_async_copy(cols_ref, col_buf, own_sem.at[1])
+    take_cols = pltpu.make_async_copy(cols_ref, c_all.at[pl.ds(own_slot, block_n)], own_sem.at[1])
     take.start()
     take_cols.start()
-    if ahead:
-        take_chip = pltpu.make_async_copy(chip_ref, ahead_buf, ahead_sem.at[2])
+    if fused:
+        take_chip = pltpu.make_async_copy(chip_ref, c_all.at[pl.ds(chip_slot(1), block_n)], own_sem.at[2])
         take_chip.start()
 
         @pl.when(at > 0)
         def _():
-            pltpu.make_async_copy(below_ref, held.at[at - 1], ahead_sem.at[0]).start()
+            pltpu.make_async_copy(below_ref, held.at[at - 1], own_sem.at[3]).start()
 
         @pl.when(at + 1 < line)
         def _():
-            pltpu.make_async_copy(above_ref, held.at[at + 1], ahead_sem.at[1]).start()
-
-    if with_ham:
+            pltpu.make_async_copy(above_ref, held.at[at + 1], own_sem.at[4]).start()
+    else:
         take_ham = pltpu.make_async_copy(ham_ref, ham_buf, ham_sem.at[0])
         take_ham.start()
     greet(g)
 
     def chip_copy(step, b):
-        slot = g.col * block_n + b
-        return remote(cols_ref.at[b], c_out.at[slot], chip_send.at[step - 1, b], chip_recv.at[step - 1, b], g.other_chip(step))
-
-    def chip_slot(step):
-        return (lax.rem(g.chip - step + g.chips, g.chips) * g.cores + g.core) * block_n
+        return remote(cols_ref.at[b], c_all.at[own_slot + b], chip_send.at[step - 1, b], chip_recv.at[step - 1, b], g.other_chip(step))
 
     def core_copy(step, b):
         if step == 0:
-            src, slot = cols_ref.at[b], g.col * block_n + b
+            src, slot = cols_ref.at[b], own_slot + b
         else:
             slot = chip_slot(step) + b
-            src = chip_ref.at[b] if ahead and step == 1 else c_out.at[slot]
-        return remote(src, c_out.at[slot], core_send.at[step, b], core_recv.at[step, b], g.other_core())
+            src = chip_ref.at[b] if fused and step == 1 else c_all.at[slot]
+        return remote(src, c_all.at[slot], core_send.at[step, b], core_recv.at[step, b], g.other_core())
 
     for b in range(block_n):
         for step in range(first_step, g.chips):
@@ -233,22 +235,14 @@
             for b in range(block_n):
                 core_copy(step, b).start()
     take.wait()
-    take_cols.wait()
-    if ahead:
-        take_chip.wait()
-        put_chip = pltpu.make_async_copy(ahead_buf, c_out.at[pl.ds(chip_slot(1), block_n)], ahead_sem.at[2])
-        put_chip.start()
-
+    if fused:
         @pl.when(at > 0)
         def _():
-            pltpu.make_async_copy(below_ref, held.at[at - 1], ahead_sem.at[0]).wait()
+            pltpu.make_async_copy(below_ref, held.at[at - 1], own_sem.at[3]).wait()
 
         @pl.when(at + 1 < line)
         def _():
-            pltpu.make_async_copy(above_ref, held.at[at + 1], ahead_sem.at[1]).wait()
-
-    put_cols = pltpu.make_async_copy(col_buf, c_out.at[pl.ds(g.col * block_n, block_n)], own_sem.at[1])
-    put_cols.start()
+            pltpu.make_async_copy(above_ref, held.at[at + 1], own_sem.at[4]).wait()
 
     def part(slot, p):
         return held.at[slot, :, pl.ds(pl.multiple_of(p * piece, piece), piece), :]
@@ -258,11 +252,21 @@
 
     def down_copy(slot, p):
         return remote(part(slot, p), part(slot, p), down_send.at[slot, p], line_recv.at[slot, p], g.on_line(at - 1))
+
+    def s_rows(source, p):
+        return pl.ds(pl.multiple_of(source * size + p * piece, piece), piece)
 
     def lane_copy(step, slot, p):
         rows = pl.ds(pl.multiple_of(p * piece, piece), piece)
         return remote(
-            lane_buf.at[step - 1, slot, rows, :], s_out.at[slot * lanes + g.lane, rows, :],
+            lane_buf.at[step - 1, slot, rows, :], s_all.at[s_rows(slot * lanes + g.lane, p), :],
+            lane_send.at[step - 1, slot, p], lane_recv.at[step - 1, slot, p], g.other_lane(step))
+
+    def lane_came(step, slot, p):
+        rows = pl.ds(pl.multiple_of(p * piece, piece), piece)
+        came = slot * lanes + lax.rem(g.lane - step + lanes, lanes)
+        return remote(
+            lane_buf.at[step - 1, slot, rows, :], s_all.at[s_rows(came, p), :],
             lane_send.at[step - 1, slot, p], lane_recv.at[step - 1, slot, p], g.other_lane(step))
 
     def pick(target, source, blocks):
@@ -280,7 +284,7 @@
             target = at * lanes + lax.rem(g.lane + step, lanes)
             lane_buf[step - 1, slot, rows, :] = pick(target, source, blocks)
             lane_copy(step, slot, p).start()
-        own_buf[slot, rows, :] = pick(g.row, source, blocks)
+        s_all[s_rows(source, p), :] = pick(g.row, source, blocks)
 
     def tile_place(col, i):
         tile = col * ratio + i
@@ -289,7 +293,7 @@
     detour = g.chips % 2 == 0 and g.chips > 1
     across = g.chips // 2
     end = jnp.where(2 * home < line, line - 1, 0)
-    if with_ham:
+    if not fused:
         def ham_part(ref, p):
             return ref.at[pl.ds(pl.multiple_of(p * ham_rows, ham_rows), ham_rows)]
 
@@ -396,174 +400,258 @@
 
         lax.fori_loop(0, pieces, ham_start, 0)
 
-    def advance(n, carry):
+    def hears(s):
+        quiet = (s == 0) | (deaf == False)
+        return (at - s >= 0) & quiet, (at + s < line) & quiet
+
+    def relay(n, carry):
         s, p = n // pieces, lax.rem(n, pieces)
-        below, above = at - s, at + s
-        hears_below = (below >= 0) & ((s == 0) | (deaf == False))
-        hears_above = (above < line) & ((s == 0) | (deaf == False))
+        hears_below, hears_above = hears(s)
 
         @pl.when(hears_below)
         def _():
             @pl.when(s >= first_step)
             def _():
-                up_copy(below, p).wait_recv()
+                up_copy(at - s, p).wait_recv()
 
             @pl.when(up_ok & (s >= first_step - 1))
             def _():
-                up_copy(below, p).start()
+                up_copy(at - s, p).start()
 
         @pl.when(hears_above)
         def _():
             @pl.when(s >= first_step)
             def _():
-                down_copy(above, p).wait_recv()
+                down_copy(at + s, p).wait_recv()
 
             @pl.when(down_ok & (s >= first_step - 1))
             def _():
-                down_copy(above, p).start()
-
-        if with_ham:
+                down_copy(at + s, p).start()
+        return carry
+
+    def digest(n, carry):
+        s, p = n // pieces, lax.rem(n, pieces)
+        hears_below, hears_above = hears(s)
+
+        @pl.when(hears_below & (at != home))
+        def _():
+            select(at - s, p)
+
+        @pl.when(hears_above & (s > 0) & (at != home))
+        def _():
+            select(at + s, p)
+        return carry
+
+    def advance(n, carry):
+        relay(n, carry)
+        if not fused:
+            s, p = n // pieces, lax.rem(n, pieces)
+
             @pl.when(s > 0)
             def _():
                 ham_step(s, p)
-
-        @pl.when(hears_below & (at != home))
-        def _():
-            select(below, p)
-
-        @pl.when(hears_above & (s > 0) & (at != home))
-        def _():
-            select(above, p)
-
-        return carry
-
-    def columns(step):
-        for b in range(block_n):
-            slot = chip_slot(step) + b
-            remote(cols_ref.at[b], c_out.at[slot], chip_send.at[step - 1, b], chip_recv.at[step - 1, b], g.other_chip(step)).wait_recv()
-            if g.cores == 2:
-                core_copy(step, b).start()
+        return digest(n, carry)
 
     def core_came(step, b):
         other = lax.rem(g.core + 1, g.cores)
         slot = (lax.rem(g.chip - step + g.chips, g.chips) * g.cores + other) * block_n + b
-        return remote(cols_ref.at[b], c_out.at[slot], core_send.at[step, b], core_recv.at[step, b], g.other_core())
-
-    def pair_copy(q, turn):
-        return pltpu.make_async_copy(c_out.at[pl.ds(q * hot_count, hot_count)], pair_buf.at[turn], pair_sem.at[turn])
+        return remote(cols_ref.at[b], c_all.at[slot], core_send.at[step, b], core_recv.at[step, b], g.other_core())
 
     def turn_copy(i, step, q):
-        return remote(turn_buf.at[step - 1, q], got.at[i, q], got_send.at[step - 1, q], got_recv.at[i, q], g.other_lane(step))
-
-    def hand_out(q, carry):
-        turn = lax.rem(q, 2)
-
-        @pl.when(q + 1 < row_n)
-        def _():
-            pair_copy(q + 1, 1 - turn).start()
-
-        pair_copy(q, turn).wait()
+        rows = pl.ds(pl.multiple_of(q * size, size), size)
+        return remote(turn_buf.at[step - 1, q], s_all.at[rows, i * height:(i + 1) * height],
+                      turn_send.at[step - 1, q], turn_recv.at[i, q], g.other_lane(step))
+
+    def turn(q):
+        rows = pl.ds(pl.multiple_of(q * size, size), size)
         for i in range(ratio):
             _, home_lane = tile_place(g.col, i)
 
             @pl.when(home_lane == g.lane)
             def _():
-                def rows_of(k, carry):
-                    rows = pl.ds(pl.multiple_of(k * size, size), size)
-                    blocks = [pair_buf[turn, h, rows, :] for h in range(hot_count)]
+                for k in range(height // size):
+                    strip = slice(k * size, (k + 1) * size)
+                    blocks = [c_all[q * hot_count + h, strip, :] for h in range(hot_count)]
                     for step in range(1, lanes):
                         target = at * lanes + lax.rem(g.lane + step, lanes)
-                        turn_buf[step - 1, q, rows, :] = pick(target, q, blocks)
-                    got[i, q, rows, :] = pick(g.row, q, blocks)
-                    return carry
-
-                lax.fori_loop(0, height // size, rows_of, 0)
+                        value = pick(target, q, blocks).astype(jnp.float32).T
+                        turn_buf[step - 1, q, :, strip] = value.astype(turn_buf.dtype)
+                    value = pick(g.row, q, blocks).astype(jnp.float32).T
+                    s_all[rows, i * height + k * size:i * height + (k + 1) * size] = value.astype(s_all.dtype)
                 for step in range(1, lanes):
                     turn_copy(i, step, q).start()
-        return carry
-
-    def turn_over(i, q):
-        for k in range(height // size):
-            block = got[i, q, k * size:(k + 1) * size, :].astype(jnp.float32)
-            turned[q, :, i * height + k * size:i * height + (k + 1) * size] = block.T.astype(turned.dtype)
-
-    def turn_own(q):
-        for i in range(ratio):
-            _, home_lane = tile_place(g.col, i)
-
-            @pl.when(home_lane == g.lane)
+
+    def turns(act):
+        def one(q, carry):
+            for i in range(ratio):
+                _, home_lane = tile_place(g.col, i)
+                act(i, q, home_lane)
+            return carry
+
+        lax.fori_loop(0, row_n, one, 0)
+
+    def turn_came(i, q, home_lane):
+        @pl.when(home_lane != g.lane)
+        def _():
+            turn_copy(i, 1, q).wait_recv()
+
+    def turn_sent(i, q, home_lane):
+        @pl.when(home_lane == g.lane)
+        def _():
+            for step in range(1, lanes):
+                turn_copy(i, step, q).wait_send()
+
+    if fused:
+        stripe = x_buf.shape[2]
+        stripes = width // stripe
+        per_tile = height // stripe
+        rows_at_once = height // 2
+        share = -(-stripes // pieces)
+        late = late_slot(at, line)
+        take_wa = pltpu.make_async_copy(wa_hbm, wa, load_sem.at[0])
+        take_wb = pltpu.make_async_copy(wb_hbm, wb, load_sem.at[1])
+
+        def band(n):
+            return pl.ds(pl.multiple_of(n * stripe, stripe), stripe)
+
+        def x_copy(n):
+            return pltpu.make_async_copy(x_hbm.at[:, band(n)], x_buf.at[lax.rem(n, 2)], x_sem.at[lax.rem(n, 2)])
+
+        def start_copy(n):
+            return pltpu.make_async_copy(start_hbm.at[:, band(n)], start_buf.at[lax.rem(n, 2)], start_sem.at[lax.rem(n, 2)])
+
+        def acc_copy(n):
+            return pltpu.make_async_copy(acc.at[:, band(n)], acc_out.at[:, band(n)], acc_sem.at[n])
+
+        def beta_side(n, carry):
+            tile, inner = n // per_tile, lax.rem(n, per_tile)
+
+            @pl.when(n + 1 < stripes)
             def _():
-                turn_over(i, q)
-
-    def turn_come(q, carry):
-        for i in range(ratio):
-            _, home_lane = tile_place(g.col, i)
-
-            @pl.when(home_lane != g.lane)
-            def _():
-                turn_copy(i, 1, q).wait_recv()
-                turn_over(i, q)
-        pltpu.make_async_copy(turned.at[q], s_out.at[q], pair_sem.at[2 + q]).start()
-        return carry
+                x_copy(n + 1).start()
+                start_copy(n + 1).start()
+
+            x_copy(n).wait()
+            start_copy(n).wait()
+            slots = [q * hot_count + sel[(g.col * ratio + tile) * row_n + q] for q in range(row_n)]
+            for k in range(2):
+                rows = slice(k * rows_at_once, (k + 1) * rows_at_once)
+                beta = jnp.concatenate([c_all[slots[q], rows, :] for q in range(row_n)], axis=1)
+                value = jnp.dot(beta, wb[tile, :, band(inner)], preferred_element_type=jnp.float32)
+                value = value + (rd_ref[rows, :] + cd_ref[:, band(n)] - center) * x_buf[lax.rem(n, 2), rows, :]
+                acc[rows, band(n)] = value - start_buf[lax.rem(n, 2), rows, :] * (half_width / 2.0)
+            return carry
+
+        def alpha_side(n, carry):
+            for k in range(2):
+                rows = slice(k * rows_at_once, (k + 1) * rows_at_once)
+                value = acc[rows, band(n)]
+                for other in range(1, line):
+                    slot = lax.rem(late + other, line)
+                    depth = pl.ds(pl.multiple_of(slot * lanes * size, size), lanes * size)
+                    value = value + jnp.dot(wa[rows, depth], s_all[depth, band(n)], preferred_element_type=jnp.float32)
+                acc[rows, band(n)] = value
+            acc_copy(n).start()
+            return carry
+
+        def some_stripes(work, turn_n):
+            lax.fori_loop(turn_n * share, jnp.minimum(turn_n * share + share, stripes), work, 0)
 
     half = pieces * (line // 2)
-    per_step = -(-row_n // half)
-    lax.fori_loop(0, half, advance, 0)
+    per_step = -(-row_n // pieces)
+    if fused:
+        lax.fori_loop(pieces, half, relay, 0)
+        take_wa.start()
+        take_wb.start()
+        x_copy(0).start()
+        start_copy(0).start()
+        lax.fori_loop(0, half, digest, 0)
+    else:
+        lax.fori_loop(0, half, advance, 0)
     for step in range(first_step, g.chips):
-        columns(step)
-
-    put_cols.wait()
-    if ahead:
-        put_chip.wait()
+        for b in range(block_n):
+            slot = chip_slot(step) + b
+            remote(cols_ref.at[b], c_all.at[slot], chip_send.at[step - 1, b], chip_recv.at[step - 1, b], g.other_chip(step)).wait_recv()
+            if g.cores == 2:
+                core_copy(step, b).start()
+
+    take_cols.wait()
+    if fused:
+        take_chip.wait()
     if g.cores == 2:
         for step in range(g.chips):
             for b in range(block_n):
                 core_came(step, b).wait_recv()
+    if not fused:
+        put_cols = pltpu.make_async_copy(c_all, c_out, own_sem.at[2])
+        put_cols.start()
+    else:
+        take_wa.wait()
+        take_wb.wait()
+
+    def middle(n, carry):
+        advance(n, carry)
+
+        @pl.when(diag)
+        def _():
+            for u in range(per_step):
+                q = (n - half) * per_step + u
+
+                @pl.when(q < row_n)
+                def _():
+                    turn(q)
+        if fused:
+            some_stripes(beta_side, n - half)
+        return carry
+
+    def lanes_came(slot):
+        def one(p, carry):
+            for step in range(1, lanes):
+                lane_came(step, slot, p).wait_recv()
+            return carry
+
+        @pl.when(at != home)
+        def _():
+            lax.fori_loop(0, pieces, one, 0)
+
+    lax.fori_loop(half, half + pieces, middle, 0)
+    if fused:
+        for other in range(1, line):
+            lanes_came(lax.rem(late + other, line))
+
+        @pl.when(diag)
+        def _():
+            turns(turn_came)
+
+        def ending(n, carry):
+            advance(n, carry)
+            some_stripes(alpha_side, n - half - pieces)
+            return carry
+
+        lax.fori_loop(half + pieces, pieces * line, ending, 0)
+        lanes_came(late)
+        put_s = pltpu.make_async_copy(s_all.at[pl.ds(pl.multiple_of(late * lanes * size, size), lanes * size), :], s_out, own_sem.at[5])
+        put_s.start()
+        put_s.wait()
+        for n in range(stripes):
+            acc_copy(n).wait()
+    else:
+        lax.fori_loop(half + pieces, pieces * line, advance, 0)
+        for slot in range(line):
+            lanes_came(slot)
+
+        @pl.when(diag)
+        def _():
+            turns(turn_came)
+
+        put_s = pltpu.make_async_copy(s_all, s_out, own_sem.at[5])
+        put_s.start()
+        put_s.wait()
+        put_cols.wait()
 
     @pl.when(diag)
     def _():
-        pair_copy(0, 0).start()
-        lax.fori_loop(0, row_n, hand_out, 0)
-
-    def advance_late(n, carry):
-        advance(n, carry)
-
-        @pl.when(diag)
-        def _():
-            for u in range(per_step):
-                q = (n - half) * per_step + u
-
-                @pl.when(q < row_n)
-                def _():
-                    turn_own(q)
-        return carry
-
-    lax.fori_loop(half, 2 * half, advance_late, 0)
-
-    @pl.when(diag)
-    def _():
-        lax.fori_loop(0, row_n, turn_come, 0)
-        for q in range(row_n):
-            pltpu.make_async_copy(turned.at[q], s_out.at[q], pair_sem.at[2 + q]).wait()
-
-        def sent(q, carry):
-            for i in range(ratio):
-                _, home_lane = tile_place(g.col, i)
-
-                @pl.when(home_lane == g.lane)
-                def _():
-                    for step in range(1, lanes):
-                        turn_copy(i, step, q).wait_send()
-            return carry
-
-        lax.fori_loop(0, row_n, sent, 0)
-
-    @pl.when(at != home)
-    def _():
-        for slot in range(line):
-            pltpu.make_async_copy(own_buf.at[slot], s_out.at[slot * lanes + g.lane], own_sem.at[2 + slot]).start()
-        for slot in range(line):
-            pltpu.make_async_copy(own_buf.at[slot], s_out.at[slot * lanes + g.lane], own_sem.at[2 + slot]).wait()
+        turns(turn_sent)
 
     def finish(n, carry):
         slot, p = n // pieces, lax.rem(n, pieces)
@@ -580,10 +668,6 @@
         def _():
             for step in range(1, lanes):
                 lane_copy(step, slot, p).wait_send()
-                came = slot * lanes + lax.rem(g.lane - step + lanes, lanes)
-                rows = pl.ds(pl.multiple_of(p * piece, piece), piece)
-                remote(lane_buf.at[step - 1, slot, rows, :], s_out.at[came, rows, :], lane_send.at[step - 1, slot, p],
-                       lane_recv.at[step - 1, slot, p], g.other_lane(step)).wait_recv()
         return carry
 
     lax.fori_loop(0, line * pieces, finish, 0)
@@ -593,7 +677,7 @@
         if g.cores == 2:
             for step in range(g.chips):
                 core_copy(step, b).wait_send()
-    if with_ham:
+    if not fused:
         for i in range(ratio):
             _, home_lane = tile_place(g.col, i)
 
@@ -610,30 +694,25 @@
             lax.fori_loop(0, pieces, settle, 0)
 
 
-def exchange(rows, cols, ham, ahead, sel, row_n, col_n, ident):
+def exchange(rows, cols, sel, row_n, col_n, ident, ham=None, ahead=None, product=None):
     hot_count, size, width = rows.shape
     block_n, height = cols.shape[:2]
     ratio = row_n // col_n
     pieces = 4
+    fused = product is not None
     line, lanes, chips, _ = layout(row_n, col_n)
     others = max(lanes - 1, 1)
     dma = pltpu.SemaphoreType.DMA
     vmem = lambda *shape: pltpu.VMEM(shape, jnp.bfloat16)
     anywhere = pl.BlockSpec(memory_space=pl.ANY)
-    out_shape = [
-        jax.ShapeDtypeStruct((row_n, size, width), jnp.bfloat16),
-        jax.ShapeDtypeStruct((col_n * block_n, height, size), jnp.bfloat16),
-    ]
+    whole = pl.BlockSpec(memory_space=pltpu.VMEM)
     scratch = [
         vmem(line, hot_count, size, width),
         vmem(others, line, size, width),
-        vmem(line, size, width),
-        vmem(*cols.shape),
-        vmem(2, hot_count, height, size),
-        vmem(others, row_n, height, size),
-        vmem(ratio, row_n, height, size),
-        vmem(row_n, size, width),
-        dma((2 + line,)),
+        vmem(others, row_n, size, height),
+        vmem(row_n * size, width),
+        vmem(col_n * block_n, height, size),
+        dma((6,)),
         dma((line, pieces)),
         dma((line, pieces)),
         dma((line, pieces)),
@@ -643,16 +722,39 @@
         dma((max(chips - 1, 1), block_n)),
         dma((chips, block_n)),
         dma((chips, block_n)),
-        dma((2 + row_n,)),
         dma((others, row_n)),
         dma((ratio, row_n)),
     ]
     args = [sel, rows, cols]
-    if ahead is not None:
-        scratch += [vmem(*cols.shape), dma((3,))]
-        args += ahead
-    if ham is not None:
-        out_shape.append(jax.ShapeDtypeStruct((ratio,) + ham.shape, ham.dtype))
+    in_specs = [pl.BlockSpec(memory_space=pltpu.SMEM), anywhere, anywhere]
+    if fused:
+        wa, wb, rd, cd, x, start = product
+        stripe = 256 if height % 256 == 0 else size
+        args += list(ahead) + [wa, wb, rd, cd, x, start]
+        in_specs += [anywhere] * 5 + [whole] * 2 + [anywhere] * 2
+        out_shape = [
+            jax.ShapeDtypeStruct((lanes * size, width), jnp.bfloat16),
+            jax.ShapeDtypeStruct((height, width), jnp.float32),
+        ]
+        scratch += [
+            pltpu.VMEM((height, width), jnp.float32),
+            vmem(*wa.shape),
+            vmem(*wb.shape),
+            pltpu.VMEM((2, height, stripe), jnp.float32),
+            pltpu.VMEM((2, height, stripe), jnp.float32),
+            dma((2,)),
+            dma((2,)),
+            dma((2,)),
+            dma((width // stripe,)),
+        ]
+    else:
+        args.append(ham)
+        in_specs.append(anywhere)
+        out_shape = [
+            jax.ShapeDtypeStruct((row_n * size, width), jnp.bfloat16),
+            jax.ShapeDtypeStruct((col_n * block_n, height, size), jnp.bfloat16),
+            jax.ShapeDtypeStruct((ratio,) + ham.shape, ham.dtype),
+        ]
         scratch += [
             pltpu.VMEM(ham.shape, ham.dtype),
             pltpu.VMEM(ham.shape, ham.dtype),
@@ -665,15 +767,42 @@
             dma((pieces,)),
             dma((pieces,)),
         ]
-        args.append(ham)
     return pl.pallas_call(
-        functools.partial(exchange_kernel, row_n, col_n, pieces, ham is not None, ahead is not None),
+        functools.partial(exchange_kernel, row_n, col_n, pieces, ham is not None, fused),
         out_shape=out_shape,
-        in_specs=[pl.BlockSpec(memory_space=pltpu.SMEM)] + [anywhere] * (len(args) - 1),
+        in_specs=in_specs,
         out_specs=[anywhere] * len(out_shape),
         scratch_shapes=scratch,
-        compiler_params=pltpu.CompilerParams(collective_id=ident, has_side_effects=True, vmem_limit_bytes=VMEM_LIMIT),
+        compiler_params=pltpu.CompilerParams(collective_id=ident, has_side_effects=True, vmem_limit_bytes=VMEM_MOST),
     )(*args)
+
+
+def last_kernel(place, acc_ref, wa_ref, s_ref, out_ref):
+    acc = acc_ref[...] + jnp.dot(wa_ref[...], s_ref[...], preferred_element_type=jnp.float32)
+    out_ref[...] = acc * (2.0 / half_width)
+
+
+def last_step(place, acc, wa, s, row_n, col_n):
+    height, width = acc.shape
+    depth = s.shape[0]
+    line, lanes, _, _ = layout(row_n, col_n)
+    stripe = 256 if width % 256 == 0 else width
+    grid_spec = pltpu.PrefetchScalarGridSpec(
+        num_scalar_prefetch=1,
+        grid=(width // stripe,),
+        in_specs=[
+            pl.BlockSpec((height, stripe), lambda n, place: (0, n)),
+            pl.BlockSpec((height, depth), lambda n, place: (0, late_slot(place[0] // lanes, line))),
+            pl.BlockSpec((depth, stripe), lambda n, place: (0, n)),
+        ],
+        out_specs=pl.BlockSpec((height, stripe), lambda n, place: (0, n)),
+    )
+    return pl.pallas_call(
+        last_kernel,
+        out_shape=jax.ShapeDtypeStruct(acc.shape, jnp.float32),
+        grid_spec=grid_spec,
+        compiler_params=pltpu.CompilerParams(vmem_limit_bytes=VMEM_LIMIT),
+    )(place, acc, wa, s)
 
 
 def hot_kernel(row_n, hot_count, place, hot, sel, *refs):
@@ -783,31 +912,23 @@
     return [below, above, lax.ppermute(cols, "col", turn)]
 
 
-def filter_kernel(source_count, row_chunk, last, place, sel, wa_ref, s_ref, wb_ref, rd_ref, cd_ref, *refs):
+def filter_kernel(source_count, row_chunk, place, sel, wa_ref, s_ref, wb_ref, rd_ref, cd_ref, *refs):
     b_refs = refs[:source_count]
-    rest = refs[source_count:]
-    if last:
-        x_ref, start_ref, out_ref = rest
-    else:
-        x_ref, out_ref = rest
+    x_ref, out_ref = refs[source_count:]
 
     def chunk(i, carry):
         rows = pl.ds(pl.multiple_of(i * row_chunk, row_chunk), row_chunk)
         beta = jnp.concatenate([b[0, rows, :] for b in b_refs], axis=1)
         acc = jnp.dot(wa_ref[rows, :], s_ref[...], preferred_element_type=jnp.float32)
         acc = acc + jnp.dot(beta, wb_ref[0], preferred_element_type=jnp.float32)
-        x = x_ref[rows, :]
-        acc = acc + (rd_ref[rows, :] + cd_ref[...] - center) * x
-        if last:
-            out_ref[rows, :] = acc * (2.0 / half_width) - start_ref[rows, :]
-        else:
-            out_ref[rows, :] = acc * (1.0 / half_width)
+        acc = acc + (rd_ref[rows, :] + cd_ref[...] - center) * x_ref[rows, :]
+        out_ref[rows, :] = acc * (1.0 / half_width)
         return carry
 
     lax.fori_loop(0, x_ref.shape[0] // row_chunk, chunk, 0)
 
 
-def filter_step(place, sel, wa, s, wb, rd, cd, cols, x, start, row_n, ratio):
+def filter_step(place, sel, wa, s, wb, rd, cd, cols, x, row_n, ratio):
     height, width = x.shape
     size = cols.shape[-1]
     hot_count = cols.shape[0] // row_n
@@ -815,7 +936,6 @@
     stripe = next(n for n in (512, 384, 256, size) if tile_width % n == 0)
     per_tile = tile_width // stripe
     row_chunk = height // 2 if height % 256 == 0 else height
-    last = start is not None
 
     def b_spec(q):
         return pl.BlockSpec(
@@ -829,12 +949,12 @@
         pl.BlockSpec((1, wb.shape[1], stripe), lambda n, *_: (n // per_tile, 0, n % per_tile)),
         pl.BlockSpec((height, 1), lambda n, *_: (0, 0)),
         pl.BlockSpec((1, stripe), lambda n, *_: (0, n)),
-    ] + [b_spec(q) for q in range(row_n)] + [striped] * (2 if last else 1)
-    args = [wa, s, wb, rd, cd] + [cols] * row_n + [x] + ([start] if last else [])
+    ] + [b_spec(q) for q in range(row_n)] + [striped]
+    args = [wa, s, wb, rd, cd] + [cols] * row_n + [x]
     grid_spec = pltpu.PrefetchScalarGridSpec(
         num_scalar_prefetch=2, grid=(width // stripe,), in_specs=in_specs, out_specs=striped)
     return pl.pallas_call(
-        functools.partial(filter_kernel, row_n, row_chunk, last),
+        functools.partial(filter_kernel, row_n, row_chunk),
         out_shape=jax.ShapeDtypeStruct(x.shape, jnp.float32),
         grid_spec=grid_spec,
         cost_estimate=pl.CostEstimate(
@@ -860,18 +980,16 @@
     depth = row_n * size
 
     rows, cols = pack(start_vector, place, hot, row_n, ratio, size)
-    s, b, hams = exchange(rows, cols, ham_blocks, None, sel, row_n, col_n, 0)
-    s = s.reshape(depth, width)
+    s, b, hams = exchange(rows, cols, sel, row_n, col_n, 0, ham=ham_blocks)
     wa = dense(ham_blocks[None], place[:1], pairs, pair_counts, (height, depth), False)[0]
     mirrors = (col_index * ratio + jnp.arange(ratio)).astype(jnp.int32)
     wb = dense(hams, mirrors, pairs, pair_counts, (depth, width // ratio), True)
     rows, cols = hot_step(place, hot, sel, wa, s, wb, rd, cd, b, start_vector, row_n, ratio)
     ahead = first_hops(rows, cols, row_n, col_n)
     s, _ = lax.optimization_barrier((s, rows))
-    first = filter_step(place, sel, wa, s, wb, rd, cd, b, start_vector, None, row_n, ratio)
-    s, b = exchange(rows, cols, None, ahead, sel, row_n, col_n, 1)
-    second = filter_step(place, sel, wa, s.reshape(depth, width), wb, rd, cd, b, first, start_vector, row_n, ratio)
-    return (first, second)
+    first = filter_step(place, sel, wa, s, wb, rd, cd, b, start_vector, row_n, ratio)
+    s, acc = exchange(rows, cols, sel, row_n, col_n, 1, ahead=ahead, product=(wa, wb, rd, cd, first, start_vector))
+    return (first, last_step(place, acc, wa, s, row_n, col_n))
 
 
 def solution(mesh):

time: 334 us -> 330 us (0.988)
  the two profiles are of different devices: /device:TPU:24 before, /device:TPU:11 now
where the time goes in v4:
time: 330 us; the launch traced here: 328 us
  Pallas kernels  308 us (93%)
  starting transfers between devices  7.67 us (2%)
  local copies, waits for them, and re-layouts  7.26 us (2%)
    pallas_call x2, Pallas kernels, exchange(): pl.pallas_call(functools.partial(exchange_kernel, row_n, col_n, pieces, h...  216 us
    pallas_call x1, Pallas kernels, filter_step(): pl.pallas_call(functools.partial(filter_kernel, row_n, row_chunk), out_sh...  30.2 us
    pallas_call x1, Pallas kernels, hot_step(): pl.pallas_call(functools.partial(hot_kernel, row_n, hot_count), out_shape...  20.9 us
    pallas_call x1, Pallas kernels, last_step(): pl.pallas_call(last_kernel, out_shape=jax.ShapeDtypeStruct(acc.shape, jnp...  19.2 us
    pallas_call x2, Pallas kernels, dense(): pl.pallas_call(functools.partial(dense_kernel, transposed), out_shape=jax...  16.2 us
  transfers between devices with their start and end apart: 3, of which 1 were waited for; matrix products, arithmetic and copies ran while one was open for 0% of the time, Pallas kernels for 9%

profile of v4, /device:TPU:11, one launch (start us, length us, event | category | flops | bytes accessed | tf_op | source)
XLA Modules:
  0.0 327.6 jit_solution(10436382183188885320)
XLA Ops:
  0.6 0.5 iota_add_fusion.tiles
  1.2 1.3 reshape.13.sel
  2.5 0.8 copy.10
  3.2 0.6 reshape.15.hot
  3.8 1.4 reshape.14.pairs
  5.2 0.8 dynamic_slice.6
  6.0 1.3 dynamic_slice.7
  7.3 1.2 broadcast_in_dim.12.refs_4_.refs_5_.refs_26_.rd_ref
  8.4 0.6 pad_add_fusion.place
  9.0 5.0 %shard_map.86 = bf16[1,1536,1024]{2,1,0:T(8,128)(2,1)} custom-call(s32[1]{0:T(128)} %bitcast.tiles, s32[1536]{0:T(1024)} %reshape.14.pairs, s32[8]{0:T(128)} %counts.3, bf16[1,48,128,128]{3,2,1,0:T(8,128)(2,1)} %bitcast.11), custom_call_target="tpu_custom_call" | custom-call | tf_op jit(solution)/shard_map/pallas_call | solution.py:47
  14.0 5.6 %shard_map.87 = (bf16[2,128,3072]{2,1,0:T(8,128)(2,1)}, bf16[4,1536,128]{2,1,0:T(8,128)(2,1)}) custom-call(s32[2]{0:T(128)} %pad_add_fusion.place, s32[16]{0:T(128)} %reshape.15.hot, f32[1536,3072]{1,0:T(8,128)} %refs_8_.3, f32[1536,3072]{1,0:T(8,128)} %refs_8_.3), custom_call_target="tpu_custom_call" | custom-call | tf_op jit(solution)/shard_map/pallas_call | solution.py:84
  19.6 126.3 %shard_map.88 = (bf16[1024,3072]{1,0:T(8,128)(2,1)}, bf16[16,1536,128]{2,1,0:T(8,128)(2,1)}, bf16[2,48,128,128]{3,2,1,0:T(8,128)(2,1)}) custom-call(s32[64]{0:T(128)} %reshape.13.sel, bf16[2,128,3072]{2,1,0:T(8,128)(2,1)} %get-tuple-element.12.rows_ref, bf16[4,1536,128]{2,1,0:T(8,128)(2,1)} %get-tuple-element.13.cols_ref, bf16[48,128,128]{2,1,0:T(8,128)(2,1)} %refs_0_.1), custom_call_target="tpu_custom_call" | custom-call | tf_op jit(solution)/shard_map/pallas_call | solution.py:770
  146.0 11.2 %shard_map.89.refs_23_.refs_37_.refs_38_.wb_ref.refs_4_ = bf16[2,1024,1536]{2,1,0:T(8,128)(2,1)} custom-call(s32[2]{0:T(128)} %iota_add_fusion.tiles, s32[1536]{0:T(1024)} %reshape.14.pairs, s32[8]{0:T(128)} %counts.3, bf16[2,48,128,128]{3,2,1,0:T(8,128)(2,1)} %get-tuple-element.16.ham_ref), custom_call_target="tpu_custom_call" | custom-call | tf_op jit(solution)/shard_map/pallas_call | solution.py:47
  157.2 20.9 %shard_map.90 = (bf16[2,128,3072]{2,1,0:T(8,128)(2,1)}, bf16[4,1536,128]{2,1,0:T(8,128)(2,1)}) custom-call(s32[2]{0:T(128)} %pad_add_fusion.place, s32[16]{0:T(128)} %reshape.15.hot, s32[64]{0:T(128)} %reshape.13.sel, bf16[1536,1024]{1,0:T(8,128)(2,1)} %bitcast.5, bf16[1536,1024]{1,0:T(8,128)(2,1)} %bitcast.6, f32[1536,3072]{1,0:T(8,128)} %refs_8_.3, ...), custom_call_target="tpu_custom_call" | custom-call | tf_op jit(solution)/shard_map/pallas_call | solution.py:895
  178.1 1.9 collective-permute-start.1
  180.0 3.4 %collective-permute-start = (bf16[2,128,3072]{2,1,0:T(8,128)(2,1)}, bf16[2,128,3072]{2,1,0:T(8,128)(2,1)}, u32[]{:S(2)}, u32[]{:S(2)}) collective-permute-start(bf16[2,128,3072]{2,1,0:T(8,128)(2,1)} %get-tuple-element.17.rows_ref), channel_id=1, source_target_pairs={{0,8},{4,12},{8,16},{12,20},{16,24},{20,28},{1,9},{5,13},{9,17},{1... | collective-permute-start | bytes 4718600 | tf_op jit(solution)/shard_map/ppermute | solution.py:909
  183.4 2.4 collective-permute-start.2
  185.7 30.2 %shard_map.91.refs_7_ = f32[1536,3072]{1,0:T(8,128)} custom-call(s32[2]{0:T(128)} %pad_add_fusion.place, s32[64]{0:T(128)} %reshape.13.sel, bf16[1536,1024]{1,0:T(8,128)(2,1)} %bitcast.8, bf16[1024,3072]{1,0:T(8,128)(2,1)} %get-tuple-element.18.refs_22_.refs_35_.refs_36_.s_ref, bf16[2,1024,1536]{2,1,0:T(8,128)(2,1)} %shard_map.89.refs_23_.refs_37_.refs_38_.wb_ref.refs_4_, ...), custom_call_target="tpu_custom_call" | custom-call | flops 19327352832 | bytes 56623104 | tf_op jit(solution)/shard_map/pallas_call | solution.py:956
  215.9 3.2 collective-permute-done.2.refs_2_
  219.1 0.0 collective-permute-done.1.refs_1_
  219.1 0.0 collective-permute-done.refs_0_
  219.1 89.3 %shard_map.92 = (bf16[256,3072]{1,0:T(8,128)(2,1)}, f32[1536,3072]{1,0:T(8,128)}) custom-call(s32[64]{0:T(128)} %reshape.13.sel, bf16[2,128,3072]{2,1,0:T(8,128)(2,1)} %get-tuple-element.17.rows_ref, bf16[4,1536,128]{2,1,0:T(8,128)(2,1)} %get-tuple-element.19.cols_ref, bf16[2,128,3072]{2,1,0:T(8,128)(2,1)} %collective-permute-done.refs_0_, ...), custom_call_target="tpu_custom_call" | custom-call | tf_op jit(solution)/shard_map/pallas_call | solution.py:770
  308.4 19.2 %shard_map.93 = f32[1536,3072]{1,0:T(8,128)} custom-call(s32[2]{0:T(128)} %pad_add_fusion.place, f32[1536,3072]{1,0:T(8,128)} %get-tuple-element.20.acc_ref, bf16[1536,1024]{1,0:T(8,128)(2,1)} %bitcast.10, bf16[256,3072]{1,0:T(8,128)(2,1)} %get-tuple-element.21.s_ref), custom_call_target="tpu_custom_call" | custom-call | tf_op jit(solution)/shard_map/pallas_call | solution.py:800
Async XLA Ops:
  178.1 41.1 %collective-permute-start.1 = (bf16[2,128,3072]{2,1,0:T(8,128)(2,1)}, bf16[2,128,3072]{2,1,0:T(8,128)(2,1)}, u32[]{:S(2)}, u32[]{:S(2)}) collective-permute-start(bf16[2,128,3072]{2,1,0:T(8,128)(2,1)} %get-tuple-element.17.rows_ref), channel_id=1, source_target_pairs={{8,0},{12,4},{16,8},{20,12},{24,16},{28,20},{9,1},{13,5},{17,9},{2... | collective-permute-start | bytes 4718600 | tf_op jit(solution)/shard_map/ppermute | solution.py:910
  180.0 39.1 %collective-permute-start = (bf16[2,128,3072]{2,1,0:T(8,128)(2,1)}, bf16[2,128,3072]{2,1,0:T(8,128)(2,1)}, u32[]{:S(2)}, u32[]{:S(2)}) collective-permute-start(bf16[2,128,3072]{2,1,0:T(8,128)(2,1)} %get-tuple-element.17.rows_ref), channel_id=1, source_target_pairs={{0,8},{4,12},{8,16},{12,20},{16,24},{20,28},{1,9},{5,13},{9,17},{1... | collective-permute-start | bytes 4718600 | tf_op jit(solution)/shard_map/ppermute | solution.py:909
  183.4 35.8 %collective-permute-start.2 = (bf16[4,1536,128]{2,1,0:T(8,128)(2,1)}, bf16[4,1536,128]{2,1,0:T(8,128)(2,1)}, u32[]{:S(2)}, u32[]{:S(2)}) collective-permute-start(bf16[4,1536,128]{2,1,0:T(8,128)(2,1)} %get-tuple-element.19.cols_ref), channel_id=1, source_target_pairs={{0,2},{1,3},{2,0},{3,1},{4,6},{5,7},{6,4},{7,5},{8,10},{9,11},{10,... | collective-permute-start | bytes 4718600 | tf_op jit(solution)/shard_map/ppermute | solution.py:912

commit v5 on v4

--- a/solution.py
+++ b/solution.py
@@ -14,29 +14,22 @@
 MESH = pl.DeviceIdType.MESH
 
 
-def dense_kernel(transposed, tiles, pairs, counts, ham_ref, out_ref, acc):
-    tile = tiles[pl.program_id(0)]
-    tile_count = counts.shape[0]
-    slots = pairs.shape[0] // (3 * tile_count)
+def dense_kernel(tile_of, place, pairs, counts, ham_ref, out_ref, acc):
+    tile = tile_of(place, pl.program_id(0))
     size = ham_ref.shape[-1]
     acc[...] = jnp.zeros_like(acc)
 
     def add(slot, carry):
-        at = tile * slots + slot
-        source = pl.multiple_of(pairs[at] * size, size)
-        target = pl.multiple_of(pairs[tile_count * slots + at] * size, size)
-        block = ham_ref[0, pairs[2 * tile_count * slots + at]].astype(jnp.float32)
-        if transposed:
-            acc[pl.ds(source, size), pl.ds(target, size)] += block.T
-        else:
-            acc[pl.ds(target, size), pl.ds(source, size)] += block
+        source = pl.multiple_of(pairs[0, tile, slot] * size, size)
+        target = pl.multiple_of(pairs[1, tile, slot] * size, size)
+        acc[pl.ds(target, size), pl.ds(source, size)] += ham_ref[0, pairs[2, tile, slot]].astype(jnp.float32)
         return carry
 
     lax.fori_loop(0, counts[tile], add, 0)
     out_ref[0] = acc[...].astype(out_ref.dtype)
 
 
-def dense(hams, tiles, pairs, counts, shape, transposed):
+def dense(hams, place, pairs, counts, shape, tile_of):
     grid_spec = pltpu.PrefetchScalarGridSpec(
         num_scalar_prefetch=3,
         grid=(hams.shape[0],),
@@ -45,11 +38,15 @@
         scratch_shapes=[pltpu.VMEM(shape, jnp.float32)],
     )
     return pl.pallas_call(
-        functools.partial(dense_kernel, transposed),
+        functools.partial(dense_kernel, tile_of),
         out_shape=jax.ShapeDtypeStruct((hams.shape[0],) + shape, jnp.bfloat16),
         grid_spec=grid_spec,
         compiler_params=pltpu.CompilerParams(vmem_limit_bytes=VMEM_LIMIT),
-    )(tiles, pairs, counts, hams)
+    )(place, pairs, counts, hams)
+
+
+def dot_t(a, b):
+    return lax.dot_general(a, b, (((1,), (1,)), ((), ())), preferred_element_type=jnp.float32)
 
 
 def pack_kernel(place, hot, xr_ref, xc_ref, rows_ref, cols_ref):
@@ -59,18 +56,18 @@
 
 def pack(x, place, hot, row_count, ratio, size):
     height, width = x.shape
-    hot_count = hot.shape[0] // row_count
+    hot_count = hot.shape[1]
     blocks = width // (ratio * size)
     part = width // ratio
 
     def row_block(n, place, hot):
         n = jnp.minimum(n, ratio * hot_count - 1)
-        return (hot[place[0] * hot_count + n // ratio], n % ratio)
+        return (hot[place[0], n // ratio], n % ratio)
 
     def col_block(n, place, hot):
         n = jnp.minimum(n, ratio * hot_count - 1)
         tile, which = n // hot_count, n % hot_count
-        return (0, tile * blocks + hot[(place[1] * ratio + tile) * hot_count + which])
+        return (0, tile * blocks + hot[place[1] * ratio + tile, which])
 
     grid_spec = pltpu.PrefetchScalarGridSpec(
         num_scalar_prefetch=2,
@@ -169,12 +166,12 @@
     if fused:
         below_ref, above_ref, chip_ref, wa_hbm, wb_hbm, rd_ref, cd_ref, x_hbm, start_hbm, s_out, acc_out = some(11)
     else:
-        ham_ref, s_out, c_out, h_out = some(4)
+        ham_ref, diag_ref, s_out, c_out, h_out, rd_out, cd_out = some(7)
     held, lane_buf, turn_buf, s_all, c_all = some(5)
     own_sem, line_recv, up_send, down_send, lane_send, lane_recv = some(6)
     chip_send, chip_recv, core_send, core_recv, turn_send, turn_recv = some(6)
     if fused:
-        acc, wa, wb, x_buf, start_buf, load_sem, x_sem, start_sem, acc_sem = some(9)
+        acc, wa, wb, x_buf, start_buf, via_buf, load_sem, x_sem, start_sem, acc_sem, via_send, via_recv = some(12)
     else:
         ham_buf, far_buf, ham_sem, ham_recv, ham_up, ham_down, ham_lane, far_recv, far_send, far_chip = some(10)
         ham_rows = ham_ref.shape[0] // pieces
@@ -270,7 +267,7 @@
             lane_send.at[step - 1, slot, p], lane_recv.at[step - 1, slot, p], g.other_lane(step))
 
     def pick(target, source, blocks):
-        which = sel[target * row_n + source]
+        which = sel[target, source]
         value = blocks[0]
         for h in range(1, hot_count):
             value = jnp.where(which == h, blocks[h], value)
@@ -377,8 +374,7 @@
 
                 @pl.when((home_lane == g.lane) & (away == s))
                 def _():
-                    @pl.when(s > 0)
-                    def _():
+                    if s > 0:
                         ham_copies(i, p)[0].wait_recv()
 
                     ham_sends(i, p, lambda copy: copy.start())
@@ -388,8 +384,7 @@
 
                     @pl.when((far_lane == g.lane) & (far_away == s))
                     def _():
-                        @pl.when(s > 0)
-                        def _():
+                        if s > 0:
                             far_copies(i, p)[0].wait_recv()
 
                         far_sends(i, p, lambda copy: copy.start())
@@ -400,6 +395,40 @@
 
         lax.fori_loop(0, pieces, ham_start, 0)
 
+    if fused and detour and line > 2:
+        climbs = end > home
+        before = jnp.where(climbs, end - 1, end + 1)
+        via_slot = jnp.where(climbs, end - 2, end + 2)
+        leaves = at == before
+        far_col = lax.rem(g.chip + across, g.chips) * g.cores + g.core
+        far_home = (far_col * ratio) // lanes
+        far_end = jnp.where(2 * far_home < line, line - 1, 0)
+        far_before = jnp.where(far_end > far_home, far_end - 1, far_end + 1)
+        far_slot = jnp.where(far_end > far_home, far_end - 2, far_end + 2)
+        kept = pieces // 2
+
+        def via_leave(p):
+            return remote(part(via_slot, p), via_buf.at[p - kept], via_send.at[0, p - kept], via_recv.at[0, p - kept], g.other_chip(across))
+
+        def via_pass(p):
+            return remote(via_buf.at[p - kept], via_buf.at[p - kept], via_send.at[1, p - kept], via_recv.at[1, p - kept], g.on_line(far_end))
+
+        def via_land(p):
+            return remote(via_buf.at[p - kept], part(far_slot, p), via_send.at[2, p - kept], line_recv.at[far_slot, p], g.other_chip(across))
+
+        def via_came(stage, p):
+            there = g.other_chip(across) if stage == 0 else g.on_line(far_before)
+            return remote(via_buf.at[p - kept], via_buf.at[p - kept], via_send.at[stage, p - kept], via_recv.at[stage, p - kept], there)
+
+        def via_up(slot, p):
+            return ((leaves & climbs & (slot == via_slot)) == False) | (p < kept)
+
+        def via_down(slot, p):
+            return ((leaves & (climbs == False) & (slot == via_slot)) == False) | (p < kept)
+    else:
+        leaves = None
+        via_up = via_down = lambda slot, p: p >= 0
+
     def hears(s):
         quiet = (s == 0) | (deaf == False)
         return (at - s >= 0) & quiet, (at + s < line) & quiet
@@ -414,7 +443,7 @@
             def _():
                 up_copy(at - s, p).wait_recv()
 
-            @pl.when(up_ok & (s >= first_step - 1))
+            @pl.when(up_ok & (s >= first_step - 1) & via_up(at - s, p))
             def _():
                 up_copy(at - s, p).start()
 
@@ -424,7 +453,7 @@
             def _():
                 down_copy(at + s, p).wait_recv()
 
-            @pl.when(down_ok & (s >= first_step - 1))
+            @pl.when(down_ok & (s >= first_step - 1) & via_down(at + s, p))
             def _():
                 down_copy(at + s, p).start()
         return carry
@@ -445,11 +474,13 @@
     def advance(n, carry):
         relay(n, carry)
         if not fused:
-            s, p = n // pieces, lax.rem(n, pieces)
-
-            @pl.when(s > 0)
-            def _():
-                ham_step(s, p)
+            for s in range(1, line):
+                first = pieces * min(s, 2) + pieces // 2 * max(s - 2, 0)
+
+                @pl.when((n >= first) & (n < first + pieces // 2))
+                def _():
+                    for u in range(2):
+                        ham_step(s, (n - first) * 2 + u)
         return digest(n, carry)
 
     def core_came(step, b):
@@ -533,11 +564,11 @@
 
             x_copy(n).wait()
             start_copy(n).wait()
-            slots = [q * hot_count + sel[(g.col * ratio + tile) * row_n + q] for q in range(row_n)]
+            slots = [q * hot_count + sel[g.col * ratio + tile, q] for q in range(row_n)]
             for k in range(2):
                 rows = slice(k * rows_at_once, (k + 1) * rows_at_once)
                 beta = jnp.concatenate([c_all[slots[q], rows, :] for q in range(row_n)], axis=1)
-                value = jnp.dot(beta, wb[tile, :, band(inner)], preferred_element_type=jnp.float32)
+                value = dot_t(beta, wb[tile, band(inner), :])
                 value = value + (rd_ref[rows, :] + cd_ref[:, band(n)] - center) * x_buf[lax.rem(n, 2), rows, :]
                 acc[rows, band(n)] = value - start_buf[lax.rem(n, 2), rows, :] * (half_width / 2.0)
             return carry
@@ -560,6 +591,12 @@
     half = pieces * (line // 2)
     per_step = -(-row_n // pieces)
     if fused:
+        if leaves is not None:
+            @pl.when(leaves)
+            def _():
+                for p in range(kept, pieces):
+                    via_leave(p).start()
+
         lax.fori_loop(pieces, half, relay, 0)
         take_wa.start()
         take_wb.start()
@@ -583,6 +620,10 @@
             for b in range(block_n):
                 core_came(step, b).wait_recv()
     if not fused:
+        cd_out[...] = diag_ref[:, pl.ds(pl.multiple_of(g.col * width, width), width)]
+        for k in range(height // size):
+            strip = diag_ref[:, pl.ds(pl.multiple_of(g.row * height + k * size, size), size)]
+            rd_out[k * size:(k + 1) * size, :] = jnp.broadcast_to(strip, (size, size)).T[:, :1]
         put_cols = pltpu.make_async_copy(c_all, c_out, own_sem.at[2])
         put_cols.start()
     else:
@@ -590,6 +631,19 @@
         take_wb.wait()
 
     def middle(n, carry):
+        if leaves is not None:
+            @pl.when((n < half + 2) & (at == far_before))
+            def _():
+                p = kept + lax.rem(n - half, 2)
+                via_came(0, p).wait_recv()
+                via_pass(p).start()
+
+            @pl.when((n >= half) & (n < half + 2) & (at == far_end))
+            def _():
+                p = kept + lax.rem(n - half, 2)
+                via_came(1, p).wait_recv()
+                via_land(p).start()
+
         advance(n, carry)
 
         @pl.when(diag)
@@ -656,11 +710,11 @@
     def finish(n, carry):
         slot, p = n // pieces, lax.rem(n, pieces)
 
-        @pl.when((slot <= at + 1 - first_step) & up_ok)
+        @pl.when((slot <= at + 1 - first_step) & up_ok & via_up(slot, p))
         def _():
             up_copy(slot, p).wait_send()
 
-        @pl.when((slot >= at - 1 + first_step) & down_ok)
+        @pl.when((slot >= at - 1 + first_step) & down_ok & via_down(slot, p))
         def _():
             down_copy(slot, p).wait_send()
 
@@ -671,6 +725,19 @@
         return carry
 
     lax.fori_loop(0, line * pieces, finish, 0)
+    if leaves is not None:
+        for p in range(kept, pieces):
+            @pl.when(leaves)
+            def _():
+                via_leave(p).wait_send()
+
+            @pl.when(at == far_before)
+            def _():
+                via_pass(p).wait_send()
+
+            @pl.when(at == far_end)
+            def _():
+                via_land(p).wait_send()
     for b in range(block_n):
         for step in range(first_step, g.chips):
             chip_copy(step, b).wait_send()
@@ -694,7 +761,7 @@
             lax.fori_loop(0, pieces, settle, 0)
 
 
-def exchange(rows, cols, sel, row_n, col_n, ident, ham=None, ahead=None, product=None):
+def exchange(rows, cols, sel, row_n, col_n, ident, ham=None, diagonal=None, ahead=None, product=None):
     hot_count, size, width = rows.shape
     block_n, height = cols.shape[:2]
     ratio = row_n // col_n
@@ -736,25 +803,32 @@
             jax.ShapeDtypeStruct((lanes * size, width), jnp.bfloat16),
             jax.ShapeDtypeStruct((height, width), jnp.float32),
         ]
+        out_specs = [anywhere] * 2
         scratch += [
             pltpu.VMEM((height, width), jnp.float32),
             vmem(*wa.shape),
             vmem(*wb.shape),
             pltpu.VMEM((2, height, stripe), jnp.float32),
             pltpu.VMEM((2, height, stripe), jnp.float32),
+            vmem(pieces - pieces // 2, hot_count, size // pieces, width),
             dma((2,)),
             dma((2,)),
             dma((2,)),
             dma((width // stripe,)),
+            dma((3, pieces)),
+            dma((3, pieces)),
         ]
     else:
-        args.append(ham)
-        in_specs.append(anywhere)
+        args += [ham, diagonal[None, :]]
+        in_specs += [anywhere, whole]
         out_shape = [
             jax.ShapeDtypeStruct((row_n * size, width), jnp.bfloat16),
             jax.ShapeDtypeStruct((col_n * block_n, height, size), jnp.bfloat16),
             jax.ShapeDtypeStruct((ratio,) + ham.shape, ham.dtype),
+            jax.ShapeDtypeStruct((height, 1), jnp.float32),
+            jax.ShapeDtypeStruct((1, width), jnp.float32),
         ]
+        out_specs = [anywhere] * 3 + [whole] * 2
         scratch += [
             pltpu.VMEM(ham.shape, ham.dtype),
             pltpu.VMEM(ham.shape, ham.dtype),
@@ -771,7 +845,7 @@
         functools.partial(exchange_kernel, row_n, col_n, pieces, ham is not None, fused),
         out_shape=out_shape,
         in_specs=in_specs,
-        out_specs=[anywhere] * len(out_shape),
+        out_specs=out_specs,
         scratch_shapes=scratch,
         compiler_params=pltpu.CompilerParams(collective_id=ident, has_side_effects=True, vmem_limit_bytes=VMEM_MOST),
     )(*args)
@@ -786,7 +860,7 @@
     height, width = acc.shape
     depth = s.shape[0]
     line, lanes, _, _ = layout(row_n, col_n)
-    stripe = 256 if width % 256 == 0 else width
+    stripe = next(n for n in (512, 384, 256, width) if width % n == 0)
     grid_spec = pltpu.PrefetchScalarGridSpec(
         num_scalar_prefetch=1,
         grid=(width // stripe,),
@@ -829,12 +903,12 @@
     size = rows_ref.shape[1]
     acc = dot(jnp.concatenate([w[...] for w in wa_hot], axis=0), s_ref[...])
     beta = jnp.concatenate([wide([b[0] for b in blocks]) for blocks in b_hot], axis=0)
-    acc = acc + dot(beta, wb_ref[0])
+    acc = acc + dot_t(beta, wb_ref[0])
     for h in range(hot_count):
         value = acc[h * size:(h + 1) * size] + (rd_hot[h][...] + cd_ref[...] - center) * x_rows[h][...]
         rows_ref[h] = (value * scale).astype(rows_ref.dtype)
     acc = dot(wa_ref[...], wide([s[...] for s in s_hot]))
-    acc = acc + dot(wide([b[0] for b in b_refs]), wide([w[0] for w in wb_hot]))
+    acc = acc + dot_t(wide([b[0] for b in b_refs]), jnp.concatenate([w[0] for w in wb_hot], axis=0))
     for h in range(hot_count):
         value = acc[:, h * size:(h + 1) * size] + (rd_ref[...] + cd_hot[h][...] - center) * x_cols[h][...]
         cols_ref[h] = (value * scale).astype(cols_ref.dtype)
@@ -843,7 +917,7 @@
 def hot_step(place, hot, sel, wa, s, wb, rd, cd, cols, x, row_n, ratio):
     height, width = x.shape
     size = cols.shape[-1]
-    hot_count = hot.shape[0] // row_n
+    hot_count = hot.shape[1]
     tile_width = width // ratio
     stripe = tile_width // 2 if tile_width % 256 == 0 else size
     per_tile = tile_width // stripe
@@ -854,13 +928,13 @@
         return jnp.minimum(n // per_tile, ratio - 1)
 
     def hot_row(h, place, hot):
-        return hot[place[0] * hot_count + h]
+        return hot[place[0], h]
 
     def hot_col(h, n, place, hot):
-        return hot[(place[1] * ratio + tile(n)) * hot_count + h]
+        return hot[place[1] * ratio + tile(n), h]
 
     def source(q, n, place, sel):
-        return q * hot_count + sel[(place[1] * ratio + tile(n)) * row_n + q]
+        return q * hot_count + sel[place[1] * ratio + tile(n), q]
 
     spec = pl.BlockSpec
     each = range(hot_count)
@@ -871,14 +945,14 @@
                  for h in each for q in range(row_n)]
     in_specs += [
         spec((depth, stripe), lambda n, *_: (0, n)),
-        spec((1, depth, stripe), lambda n, *_: (n // per_tile, 0, n % per_tile)),
+        spec((1, stripe, depth), lambda n, *_: (n // per_tile, n % per_tile, 0)),
         spec((1, stripe), lambda n, *_: (0, n)),
         spec((stripe, depth), lambda n, *_: (n % per_tile, 0)),
         spec((stripe, 1), lambda n, *_: (n % per_tile, 0)),
     ]
     in_specs += [spec((1, stripe, size), lambda n, place, hot, sel, q=q: (source(q, n, place, sel), n % per_tile, 0)) for q in range(row_n)]
     in_specs += [spec((depth, size), lambda n, place, hot, sel, h=h: (0, tile(n) * blocks + hot_col(h, n, place, hot))) for h in each]
-    in_specs += [spec((1, depth, size), lambda n, place, hot, sel, h=h: (tile(n), 0, hot_col(h, n, place, hot))) for h in each]
+    in_specs += [spec((1, size, depth), lambda n, place, hot, sel, h=h: (tile(n), hot_col(h, n, place, hot), 0)) for h in each]
     in_specs += [spec((stripe, size), lambda n, place, hot, sel, h=h: (n % per_tile, tile(n) * blocks + hot_col(h, n, place, hot))) for h in each]
     in_specs += [spec((1, size), lambda n, place, hot, sel, h=h: (0, tile(n) * blocks + hot_col(h, n, place, hot))) for h in each]
     args = [wa] * hot_count + [x] * hot_count + [rd] * hot_count + [cols] * (hot_count * row_n)
@@ -920,7 +994,7 @@
         rows = pl.ds(pl.multiple_of(i * row_chunk, row_chunk), row_chunk)
         beta = jnp.concatenate([b[0, rows, :] for b in b_refs], axis=1)
         acc = jnp.dot(wa_ref[rows, :], s_ref[...], preferred_element_type=jnp.float32)
-        acc = acc + jnp.dot(beta, wb_ref[0], preferred_element_type=jnp.float32)
+        acc = acc + dot_t(beta, wb_ref[0])
         acc = acc + (rd_ref[rows, :] + cd_ref[...] - center) * x_ref[rows, :]
         out_ref[rows, :] = acc * (1.0 / half_width)
         return carry
@@ -940,13 +1014,13 @@
     def b_spec(q):
         return pl.BlockSpec(
             (1, height, size),
-            lambda n, place, sel: (q * hot_count + sel[(place[1] * ratio + jnp.minimum(n // per_tile, ratio - 1)) * row_n + q], 0, 0))
+            lambda n, place, sel: (q * hot_count + sel[place[1] * ratio + jnp.minimum(n // per_tile, ratio - 1), q], 0, 0))
 
     striped = pl.BlockSpec((height, stripe), lambda n, *_: (0, n))
     in_specs = [
         pl.BlockSpec(wa.shape, lambda n, *_: (0, 0)),
         pl.BlockSpec((s.shape[0], stripe), lambda n, *_: (0, n)),
-        pl.BlockSpec((1, wb.shape[1], stripe), lambda n, *_: (n // per_tile, 0, n % per_tile)),
+        pl.BlockSpec((1, stripe, wb.shape[2]), lambda n, *_: (n // per_tile, n % per_tile, 0)),
         pl.BlockSpec((height, 1), lambda n, *_: (0, 0)),
         pl.BlockSpec((1, stripe), lambda n, *_: (0, n)),
     ] + [b_spec(q) for q in range(row_n)] + [striped]
@@ -969,26 +1043,17 @@
     ratio = row_n // col_n
     height, width = start_vector.shape
     size = ham_blocks.shape[1]
-    row_index = lax.axis_index("row")
-    col_index = lax.axis_index("col")
-    place = jnp.stack([row_index, col_index]).astype(jnp.int32)
-    pairs = pair_lists.reshape(-1)
-    hot = hot_blocks.reshape(-1)
-    sel = selection.reshape(-1)
-    rd = lax.dynamic_slice_in_dim(diagonal, row_index * height, height)[:, None]
-    cd = lax.dynamic_slice_in_dim(diagonal, col_index * width, width)[None, :]
-    depth = row_n * size
-
-    rows, cols = pack(start_vector, place, hot, row_n, ratio, size)
-    s, b, hams = exchange(rows, cols, sel, row_n, col_n, 0, ham=ham_blocks)
-    wa = dense(ham_blocks[None], place[:1], pairs, pair_counts, (height, depth), False)[0]
-    mirrors = (col_index * ratio + jnp.arange(ratio)).astype(jnp.int32)
-    wb = dense(hams, mirrors, pairs, pair_counts, (depth, width // ratio), True)
-    rows, cols = hot_step(place, hot, sel, wa, s, wb, rd, cd, b, start_vector, row_n, ratio)
+    place = jnp.stack([lax.axis_index("row"), lax.axis_index("col")]).astype(jnp.int32)
+    shape = (height, row_n * size)
+    rows, cols = pack(start_vector, place, hot_blocks, row_n, ratio, size)
+    s, b, hams, rd, cd = exchange(rows, cols, selection, row_n, col_n, 0, ham=ham_blocks, diagonal=diagonal)
+    wa = dense(ham_blocks[None], place, pair_lists, pair_counts, shape, lambda place, i: place[0])[0]
+    wb = dense(hams, place, pair_lists, pair_counts, shape, lambda place, i: place[1] * ratio + i)
+    rows, cols = hot_step(place, hot_blocks, selection, wa, s, wb, rd, cd, b, start_vector, row_n, ratio)
     ahead = first_hops(rows, cols, row_n, col_n)
     s, _ = lax.optimization_barrier((s, rows))
-    first = filter_step(place, sel, wa, s, wb, rd, cd, b, start_vector, row_n, ratio)
-    s, acc = exchange(rows, cols, sel, row_n, col_n, 1, ahead=ahead, product=(wa, wb, rd, cd, first, start_vector))
+    first = filter_step(place, selection, wa, s, wb, rd, cd, b, start_vector, row_n, ratio)
+    s, acc = exchange(rows, cols, selection, row_n, col_n, 1, ahead=ahead, product=(wa, wb, rd, cd, first, start_vector))
     return (first, last_step(place, acc, wa, s, row_n, col_n))
 
 

time: 330 us -> 324 us (0.982)
  the two profiles are of different devices: /device:TPU:11 before, /device:TPU:2 now
where the time goes in v5:
time: 324 us; the launch traced here: 322 us
  Pallas kernels  299 us (92%)
  starting transfers between devices  20.3 us (6%)
    pallas_call x2, Pallas kernels, exchange(): pl.pallas_call(functools.partial(exchange_kernel, row_n, col_n, pieces, h...  214 us
    pallas_call x1, Pallas kernels, filter_step(): pl.pallas_call(functools.partial(filter_kernel, row_n, row_chunk), out_sh...  30.8 us
    pallas_call x1, Pallas kernels, hot_step(): pl.pallas_call(functools.partial(hot_kernel, row_n, hot_count), out_shape...  21.8 us
    pallas_call x1, Pallas kernels, last_step(): pl.pallas_call(last_kernel, out_shape=jax.ShapeDtypeStruct(acc.shape, jnp...  15.8 us
    ppermute x1, starting transfers between devices, first_hops(): return [below, above, lax.ppermute(cols, 'col', turn)]  13.2 us
    pallas_call x2, Pallas kernels, dense(): pl.pallas_call(functools.partial(dense_kernel, tile_of), out_shape=jax.Sh...  11.1 us
  transfers between devices with their start and end apart: 3, of which 0 were waited for; matrix products, arithmetic and copies ran while one was open for 0% of the time, Pallas kernels for 10%

profile of v5, /device:TPU:2, one launch (start us, length us, event | category | flops | bytes accessed | tf_op | source)
XLA Modules:
  0.0 321.7 jit_solution(5595417020682071595)
XLA Ops:
  0.6 1.3 copy.9.hot
  2.0 0.6 pad_add_fusion.place
  2.5 5.7 %shard_map.87 = (bf16[2,128,3072]{2,1,0:T(8,128)(2,1)}, bf16[4,1536,128]{2,1,0:T(8,128)(2,1)}) custom-call(s32[2]{0:T(128)} %pad_add_fusion.place, s32[8,2]{1,0:T(8,128)} %copy.9.hot, f32[1536,3072]{1,0:T(8,128)} %refs_8_.3, f32[1536,3072]{1,0:T(8,128)} %refs_8_.3), custom_call_target="tpu_custom_call" | custom-call | tf_op jit(solution)/shard_map/pallas_call | solution.py:81
  8.2 5.0 %shard_map.86 = bf16[1,1536,1024]{2,1,0:T(8,128)(2,1)} custom-call(s32[2]{0:T(128)} %pad_add_fusion.place, s32[3,8,64]{2,1,0:T(8,128)} %pairs.3, s32[8]{0:T(128)} %counts.3, bf16[1,48,128,128]{3,2,1,0:T(8,128)(2,1)} %bitcast.11), custom_call_target="tpu_custom_call" | custom-call | tf_op jit(solution)/shard_map/pallas_call | solution.py:40
  13.2 111.8 %shard_map.88 = (bf16[1024,3072]{1,0:T(8,128)(2,1)}, bf16[16,1536,128]{2,1,0:T(8,128)(2,1)}, bf16[2,48,128,128]{3,2,1,0:T(8,128)(2,1)}, f32[1536,1]{1,0:T(8,128)}, f32[1,3072]{1,0:T(1,128)}) custom-call(s32[8,8]{1,0:T(8,128)} %sel.7, bf16[2,128,3072]{2,1,0:T(8,128)(2,1)} %get-tuple-element.14.rows_ref, bf16[4,1536,128]{2,1,0:T(8,128)(2,1)} %get-tuple-element.15.cols_ref, ...), custom_call_target="tpu_custom_call" | custom-call | tf_op jit(solution)/shard_map/pallas_call | solution.py:844
  125.0 6.1 %shard_map.89.refs_23_.refs_37_.refs_38_.wb_ref.refs_4_ = bf16[2,1536,1024]{2,1,0:T(8,128)(2,1)} custom-call(s32[2]{0:T(128)} %pad_add_fusion.place, s32[3,8,64]{2,1,0:T(8,128)} %pairs.3, s32[8]{0:T(128)} %counts.3, bf16[2,48,128,128]{3,2,1,0:T(8,128)(2,1)} %get-tuple-element.19.ham_ref), custom_call_target="tpu_custom_call" | custom-call | tf_op jit(solution)/shard_map/pallas_call | solution.py:40
  131.1 21.8 %shard_map.90 = (bf16[2,128,3072]{2,1,0:T(8,128)(2,1)}, bf16[4,1536,128]{2,1,0:T(8,128)(2,1)}) custom-call(s32[2]{0:T(128)} %pad_add_fusion.place, s32[8,2]{1,0:T(8,128)} %copy.9.hot, s32[8,8]{1,0:T(8,128)} %sel.7, bf16[1536,1024]{1,0:T(8,128)(2,1)} %bitcast.5, bf16[1536,1024]{1,0:T(8,128)(2,1)} %bitcast.6, f32[1536,3072]{1,0:T(8,128)} %refs_8_.3, ...), custom_call_target="tpu_custom_call" | custom-call | tf_op jit(solution)/shard_map/pallas_call | solution.py:969
  152.9 1.3 collective-permute-start.1
  154.2 5.8 %collective-permute-start = (bf16[2,128,3072]{2,1,0:T(8,128)(2,1)}, bf16[2,128,3072]{2,1,0:T(8,128)(2,1)}, u32[]{:S(2)}, u32[]{:S(2)}) collective-permute-start(bf16[2,128,3072]{2,1,0:T(8,128)(2,1)} %get-tuple-element.21.rows_ref), channel_id=1, source_target_pairs={{0,8},{4,12},{8,16},{12,20},{16,24},{20,28},{1,9},{5,13},{9,17},{1... | collective-permute-start | bytes 4718600 | tf_op jit(solution)/shard_map/ppermute | solution.py:983
  160.0 13.2 %collective-permute-start.2 = (bf16[4,1536,128]{2,1,0:T(8,128)(2,1)}, bf16[4,1536,128]{2,1,0:T(8,128)(2,1)}, u32[]{:S(2)}, u32[]{:S(2)}) collective-permute-start(bf16[4,1536,128]{2,1,0:T(8,128)(2,1)} %get-tuple-element.23.cols_ref), channel_id=1, source_target_pairs={{0,2},{1,3},{2,0},{3,1},{4,6},{5,7},{6,4},{7,5},{8,10},{9,11},{10,... | collective-permute-start | bytes 4718600 | tf_op jit(solution)/shard_map/ppermute | solution.py:986
  173.1 30.8 %shard_map.91.refs_7_ = f32[1536,3072]{1,0:T(8,128)} custom-call(s32[2]{0:T(128)} %pad_add_fusion.place, s32[8,8]{1,0:T(8,128)} %sel.7, bf16[1536,1024]{1,0:T(8,128)(2,1)} %bitcast.8, bf16[1024,3072]{1,0:T(8,128)(2,1)} %get-tuple-element.22.refs_22_.refs_35_.refs_36_.s_ref, bf16[2,1536,1024]{2,1,0:T(8,128)(2,1)} %shard_map.89.refs_23_.refs_37_.refs_38_.wb_ref.refs_4_, ...), custom_call_target="tpu_custom_call" | custom-call | flops 19327352832 | bytes 56623104 | tf_op jit(solution)/shard_map/pallas_call | solution.py:1030
  204.0 0.0 collective-permute-done.2.refs_2_
  204.0 0.0 collective-permute-done.1.refs_1_
  204.0 0.0 collective-permute-done.refs_0_
  204.0 101.9 %shard_map.92 = (bf16[256,3072]{1,0:T(8,128)(2,1)}, f32[1536,3072]{1,0:T(8,128)}) custom-call(s32[8,8]{1,0:T(8,128)} %sel.7, bf16[2,128,3072]{2,1,0:T(8,128)(2,1)} %get-tuple-element.21.rows_ref, bf16[4,1536,128]{2,1,0:T(8,128)(2,1)} %get-tuple-element.23.cols_ref, bf16[2,128,3072]{2,1,0:T(8,128)(2,1)} %collective-permute-done.refs_0_, ...), custom_call_target="tpu_custom_call" | custom-call | tf_op jit(solution)/shard_map/pallas_call | solution.py:844
  305.9 15.8 %shard_map.93 = f32[1536,3072]{1,0:T(8,128)} custom-call(s32[2]{0:T(128)} %pad_add_fusion.place, f32[1536,3072]{1,0:T(8,128)} %get-tuple-element.24.acc_ref, bf16[1536,1024]{1,0:T(8,128)(2,1)} %bitcast.10, bf16[256,3072]{1,0:T(8,128)(2,1)} %get-tuple-element.25.s_ref), custom_call_target="tpu_custom_call" | custom-call | tf_op jit(solution)/shard_map/pallas_call | solution.py:874
Async XLA Ops:
  152.9 51.1 %collective-permute-start.1 = (bf16[2,128,3072]{2,1,0:T(8,128)(2,1)}, bf16[2,128,3072]{2,1,0:T(8,128)(2,1)}, u32[]{:S(2)}, u32[]{:S(2)}) collective-permute-start(bf16[2,128,3072]{2,1,0:T(8,128)(2,1)} %get-tuple-element.21.rows_ref), channel_id=1, source_target_pairs={{8,0},{12,4},{16,8},{20,12},{24,16},{28,20},{9,1},{13,5},{17,9},{2... | collective-permute-start | bytes 4718600 | tf_op jit(solution)/shard_map/ppermute | solution.py:984
  154.2 49.8 %collective-permute-start = (bf16[2,128,3072]{2,1,0:T(8,128)(2,1)}, bf16[2,128,3072]{2,1,0:T(8,128)(2,1)}, u32[]{:S(2)}, u32[]{:S(2)}) collective-permute-start(bf16[2,128,3072]{2,1,0:T(8,128)(2,1)} %get-tuple-element.21.rows_ref), channel_id=1, source_target_pairs={{0,8},{4,12},{8,16},{12,20},{16,24},{20,28},{1,9},{5,13},{9,17},{1... | collective-permute-start | bytes 4718600 | tf_op jit(solution)/shard_map/ppermute | solution.py:983
  160.0 44.0 %collective-permute-start.2 = (bf16[4,1536,128]{2,1,0:T(8,128)(2,1)}, bf16[4,1536,128]{2,1,0:T(8,128)(2,1)}, u32[]{:S(2)}, u32[]{:S(2)}) collective-permute-start(bf16[4,1536,128]{2,1,0:T(8,128)(2,1)} %get-tuple-element.23.cols_ref), channel_id=1, source_target_pairs={{0,2},{1,3},{2,0},{3,1},{4,6},{5,7},{6,4},{7,5},{8,10},{9,11},{10,... | collective-permute-start | bytes 4718600 | tf_op jit(solution)/shard_map/ppermute | solution.py:986

commit v6 on v5

--- a/solution.py
+++ b/solution.py
@@ -149,6 +149,12 @@
     pl.semaphore_wait(barrier, fixed + up.astype(jnp.int32) + down.astype(jnp.int32))
 
 
+def got_slots(row_n, col_n):
+    _, lanes, _, _ = layout(row_n, col_n)
+    ratio = row_n // col_n
+    return ratio if lanes > ratio > 1 else 1
+
+
 def late_slot(at, line):
     return jnp.where(2 * at < line, line - 1, 0)
 
@@ -171,7 +177,7 @@
     own_sem, line_recv, up_send, down_send, lane_send, lane_recv = some(6)
     chip_send, chip_recv, core_send, core_recv, turn_send, turn_recv = some(6)
     if fused:
-        acc, wa, wb, x_buf, start_buf, via_buf, load_sem, x_sem, start_sem, acc_sem, via_send, via_recv = some(12)
+        acc, wa, wb_buf, x_buf, start_buf, via_buf, beta, st_buf, got, load_sem, wb_sem, x_sem, start_sem, acc_sem, via_send, via_recv = some(16)
     else:
         ham_buf, far_buf, ham_sem, ham_recv, ham_up, ham_down, ham_lane, far_recv, far_send, far_chip = some(10)
         ham_rows = ham_ref.shape[0] // pieces
@@ -367,7 +373,7 @@
                     put.start()
                     put.wait()
 
-        def ham_step(s, p):
+        def near_step(s, p):
             for i in range(ratio):
                 _, home_lane = tile_place(g.col, i)
                 away = jnp.where(at >= home, at - home, home - at)
@@ -379,18 +385,39 @@
 
                     ham_sends(i, p, lambda copy: copy.start())
 
-                if detour:
-                    _, far_lane = tile_place(far_col, i)
-
-                    @pl.when((far_lane == g.lane) & (far_away == s))
-                    def _():
-                        if s > 0:
-                            far_copies(i, p)[0].wait_recv()
-
-                        far_sends(i, p, lambda copy: copy.start())
+        def far_step(s, p):
+            for i in range(ratio if detour else 0):
+                _, far_lane = tile_place(far_col, i)
+
+                @pl.when((far_lane == g.lane) & (far_away == s))
+                def _():
+                    if s > 0:
+                        far_copies(i, p)[0].wait_recv()
+
+                    far_sends(i, p, lambda copy: copy.start())
+
+        def far_steps(s):
+            def one(p, carry):
+                far_step(s, p)
+                return carry
+
+            lax.fori_loop(0, pieces, one, 0)
+
+        if detour:
+            held_back = (far_away > 0) & (at != far_end)
+            up_first = (held_back & rising) == False
+            down_first = (held_back & (rising == False)) == False
+        else:
+            up_first = down_first = at >= 0
 
         def ham_start(p, carry):
-            ham_step(0, p)
+            near_step(0, p)
+            far_step(0, p)
+            return carry
+
+        def ham_next(p, carry):
+            near_step(1, p)
+            far_step(1, p)
             return carry
 
         lax.fori_loop(0, pieces, ham_start, 0)
@@ -429,10 +456,15 @@
         leaves = None
         via_up = via_down = lambda slot, p: p >= 0
 
+    half = pieces * (line // 2)
+
     def hears(s):
         quiet = (s == 0) | (deaf == False)
         return (at - s >= 0) & quiet, (at + s < line) & quiet
 
+    if fused:
+        up_first = down_first = at >= 0
+
     def relay(n, carry):
         s, p = n // pieces, lax.rem(n, pieces)
         hears_below, hears_above = hears(s)
@@ -443,7 +475,7 @@
             def _():
                 up_copy(at - s, p).wait_recv()
 
-            @pl.when(up_ok & (s >= first_step - 1) & via_up(at - s, p))
+            @pl.when(up_ok & (s >= first_step - 1) & via_up(at - s, p) & ((s > 0) | up_first))
             def _():
                 up_copy(at - s, p).start()
 
@@ -453,7 +485,7 @@
             def _():
                 down_copy(at + s, p).wait_recv()
 
-            @pl.when(down_ok & (s >= first_step - 1) & via_down(at + s, p))
+            @pl.when(down_ok & (s >= first_step - 1) & via_down(at + s, p) & ((s > 0) | down_first))
             def _():
                 down_copy(at + s, p).start()
         return carry
@@ -474,13 +506,10 @@
     def advance(n, carry):
         relay(n, carry)
         if not fused:
-            for s in range(1, line):
-                first = pieces * min(s, 2) + pieces // 2 * max(s - 2, 0)
-
-                @pl.when((n >= first) & (n < first + pieces // 2))
-                def _():
-                    for u in range(2):
-                        ham_step(s, (n - first) * 2 + u)
+            @pl.when((n >= half) & (n < half + pieces))
+            def _():
+                for s in range(2, line):
+                    near_step(s, n - half)
         return digest(n, carry)
 
     def core_came(step, b):
@@ -488,10 +517,15 @@
         slot = (lax.rem(g.chip - step + g.chips, g.chips) * g.cores + other) * block_n + b
         return remote(cols_ref.at[b], c_all.at[slot], core_send.at[step, b], core_recv.at[step, b], g.other_core())
 
+    def got_at(i):
+        return i if got_slots(row_n, col_n) > 1 else 0
+
     def turn_copy(i, step, q):
-        rows = pl.ds(pl.multiple_of(q * size, size), size)
-        return remote(turn_buf.at[step - 1, q], s_all.at[rows, i * height:(i + 1) * height],
-                      turn_send.at[step - 1, q], turn_recv.at[i, q], g.other_lane(step))
+        if fused:
+            there = got.at[got_at(i), q]
+        else:
+            there = s_all.at[pl.ds(pl.multiple_of(q * size, size), size), i * height:(i + 1) * height]
+        return remote(turn_buf.at[step - 1, q], there, turn_send.at[step - 1, q], turn_recv.at[i, q], g.other_lane(step))
 
     def turn(q):
         rows = pl.ds(pl.multiple_of(q * size, size), size)
@@ -505,10 +539,13 @@
                     blocks = [c_all[q * hot_count + h, strip, :] for h in range(hot_count)]
                     for step in range(1, lanes):
                         target = at * lanes + lax.rem(g.lane + step, lanes)
-                        value = pick(target, q, blocks).astype(jnp.float32).T
-                        turn_buf[step - 1, q, :, strip] = value.astype(turn_buf.dtype)
-                    value = pick(g.row, q, blocks).astype(jnp.float32).T
-                    s_all[rows, i * height + k * size:i * height + (k + 1) * size] = value.astype(s_all.dtype)
+                        value = pick(target, q, blocks)
+                        if fused:
+                            turn_buf[step - 1, q, strip, :] = value
+                        else:
+                            turn_buf[step - 1, q, :, strip] = value.T
+                    if not fused:
+                        s_all[rows, i * height + k * size:i * height + (k + 1) * size] = pick(g.row, q, blocks).T
                 for step in range(1, lanes):
                     turn_copy(i, step, q).start()
 
@@ -540,55 +577,78 @@
         share = -(-stripes // pieces)
         late = late_slot(at, line)
         take_wa = pltpu.make_async_copy(wa_hbm, wa, load_sem.at[0])
-        take_wb = pltpu.make_async_copy(wb_hbm, wb, load_sem.at[1])
+        early = line - 1
+        first_early = jnp.where(late == 0, 1, 0)
+        depth = pl.ds(pl.multiple_of(first_early * lanes * size, lanes * size), early * lanes * size)
 
         def band(n):
             return pl.ds(pl.multiple_of(n * stripe, stripe), stripe)
 
-        def x_copy(n):
-            return pltpu.make_async_copy(x_hbm.at[:, band(n)], x_buf.at[lax.rem(n, 2)], x_sem.at[lax.rem(n, 2)])
-
-        def start_copy(n):
-            return pltpu.make_async_copy(start_hbm.at[:, band(n)], start_buf.at[lax.rem(n, 2)], start_sem.at[lax.rem(n, 2)])
+        def loads(n):
+            turn_n = lax.rem(n, 2)
+            return [
+                pltpu.make_async_copy(x_hbm.at[:, band(n)], x_buf.at[turn_n], x_sem.at[turn_n]),
+                pltpu.make_async_copy(start_hbm.at[:, band(n)], start_buf.at[turn_n], start_sem.at[turn_n]),
+                pltpu.make_async_copy(wb_hbm.at[n // per_tile, band(lax.rem(n, per_tile)), :], wb_buf.at[turn_n], wb_sem.at[turn_n]),
+            ]
 
         def acc_copy(n):
             return pltpu.make_async_copy(acc.at[:, band(n)], acc_out.at[:, band(n)], acc_sem.at[n])
 
         def beta_side(n, carry):
-            tile, inner = n // per_tile, lax.rem(n, per_tile)
+            tile, turn_n = n // per_tile, lax.rem(n, 2)
 
             @pl.when(n + 1 < stripes)
             def _():
-                x_copy(n + 1).start()
-                start_copy(n + 1).start()
-
-            x_copy(n).wait()
-            start_copy(n).wait()
-            slots = [q * hot_count + sel[g.col * ratio + tile, q] for q in range(row_n)]
+                for copy in loads(n + 1):
+                    copy.start()
+
+            @pl.when(lax.rem(n, per_tile) == 0)
+            def _():
+                for q in range(row_n):
+                    beta[:, q * size:(q + 1) * size] = c_all[q * hot_count + sel[g.col * ratio + tile, q]]
+
+            for copy in loads(n):
+                copy.wait()
             for k in range(2):
                 rows = slice(k * rows_at_once, (k + 1) * rows_at_once)
-                beta = jnp.concatenate([c_all[slots[q], rows, :] for q in range(row_n)], axis=1)
-                value = dot_t(beta, wb[tile, band(inner), :])
-                value = value + (rd_ref[rows, :] + cd_ref[:, band(n)] - center) * x_buf[lax.rem(n, 2), rows, :]
-                acc[rows, band(n)] = value - start_buf[lax.rem(n, 2), rows, :] * (half_width / 2.0)
+                value = dot_t(beta[rows, :], wb_buf[turn_n])
+                value = value + (rd_ref[rows, :] + cd_ref[:, band(n)] - center) * x_buf[turn_n, rows, :]
+                acc[rows, band(n)] = value - start_buf[turn_n, rows, :] * (half_width / 2.0)
             return carry
 
         def alpha_side(n, carry):
-            for k in range(2):
-                rows = slice(k * rows_at_once, (k + 1) * rows_at_once)
-                value = acc[rows, band(n)]
-                for other in range(1, line):
-                    slot = lax.rem(late + other, line)
-                    depth = pl.ds(pl.multiple_of(slot * lanes * size, size), lanes * size)
-                    value = value + jnp.dot(wa[rows, depth], s_all[depth, band(n)], preferred_element_type=jnp.float32)
-                acc[rows, band(n)] = value
+            tile, inner = n // per_tile, lax.rem(n, per_tile)
+
+            @pl.when(at != home)
+            def _():
+                for k in range(2):
+                    rows = slice(k * rows_at_once, (k + 1) * rows_at_once)
+                    acc[rows, band(n)] += jnp.dot(wa[rows, depth], s_all[depth, band(n)], preferred_element_type=jnp.float32)
+
+            @pl.when(diag)
+            def _():
+                _, home_lane = tile_place(g.col, tile)
+
+                @pl.when(home_lane == g.lane)
+                def _():
+                    for q in range(row_n):
+                        st_buf[:, q * size:(q + 1) * size] = c_all[q * hot_count + sel[g.row, q], band(inner), :]
+
+                @pl.when(home_lane != g.lane)
+                def _():
+                    for q in range(row_n):
+                        st_buf[:, q * size:(q + 1) * size] = got[got_at(tile), q, band(inner), :]
+
+                for k in range(2):
+                    rows = slice(k * rows_at_once, (k + 1) * rows_at_once)
+                    acc[rows, band(n)] += dot_t(wa[rows, :], st_buf[...])
             acc_copy(n).start()
             return carry
 
         def some_stripes(work, turn_n):
             lax.fori_loop(turn_n * share, jnp.minimum(turn_n * share + share, stripes), work, 0)
 
-    half = pieces * (line // 2)
     per_step = -(-row_n // pieces)
     if fused:
         if leaves is not None:
@@ -599,12 +659,29 @@
 
         lax.fori_loop(pieces, half, relay, 0)
         take_wa.start()
-        take_wb.start()
-        x_copy(0).start()
-        start_copy(0).start()
+        for copy in loads(0):
+            copy.start()
         lax.fori_loop(0, half, digest, 0)
     else:
-        lax.fori_loop(0, half, advance, 0)
+        def held_rows(p, carry):
+            @pl.when(up_ok & (up_first == False))
+            def _():
+                up_copy(at, p).start()
+
+            @pl.when(down_ok & (down_first == False))
+            def _():
+                down_copy(at, p).start()
+            return carry
+
+        lax.fori_loop(0, pieces, relay, 0)
+        lax.fori_loop(0, pieces, digest, 0)
+        lax.fori_loop(0, pieces, ham_next, 0)
+        if line > 2:
+            far_steps(2)
+        lax.fori_loop(0, pieces, held_rows, 0)
+        lax.fori_loop(pieces, half, advance, 0)
+        for s in range(3, line):
+            far_steps(s)
     for step in range(first_step, g.chips):
         for b in range(block_n):
             slot = chip_slot(step) + b
@@ -628,7 +705,6 @@
         put_cols.start()
     else:
         take_wa.wait()
-        take_wb.wait()
 
     def middle(n, carry):
         if leaves is not None:
@@ -684,6 +760,11 @@
 
         lax.fori_loop(half + pieces, pieces * line, ending, 0)
         lanes_came(late)
+
+        @pl.when(diag)
+        def _():
+            s_all[pl.ds(pl.multiple_of(late * lanes * size, size), lanes * size), :] = jnp.zeros((lanes * size, width), s_all.dtype)
+
         put_s = pltpu.make_async_copy(s_all.at[pl.ds(pl.multiple_of(late * lanes * size, size), lanes * size), :], s_out, own_sem.at[5])
         put_s.start()
         put_s.wait()
@@ -776,7 +857,7 @@
     scratch = [
         vmem(line, hot_count, size, width),
         vmem(others, line, size, width),
-        vmem(others, row_n, size, height),
+        vmem(others, row_n, *((height, size) if fused else (size, height))),
         vmem(row_n * size, width),
         vmem(col_n * block_n, height, size),
         dma((6,)),
@@ -807,10 +888,14 @@
         scratch += [
             pltpu.VMEM((height, width), jnp.float32),
             vmem(*wa.shape),
-            vmem(*wb.shape),
+            vmem(2, stripe, wb.shape[2]),
             pltpu.VMEM((2, height, stripe), jnp.float32),
             pltpu.VMEM((2, height, stripe), jnp.float32),
             vmem(pieces - pieces // 2, hot_count, size // pieces, width),
+            vmem(height, row_n * size),
+            vmem(stripe, row_n * size),
+            vmem(got_slots(row_n, col_n), row_n, height, size),
+            dma((2,)),
             dma((2,)),
             dma((2,)),
             dma((2,)),

time: 324 us -> 335 us (1.034)
  Pallas kernels: 299 us -> 320 us
  starting transfers between devices: 20.3 us -> 7.07 us
  waiting for transfers between devices: 0.01 us -> 4.21 us
    pallas_call x2, Pallas kernels: 214 us -> 237 us  [exchange(): pl.pallas_call(functools.partial(exchange_kernel, row_n, col_n, pieces, h...]
    ppermute x1, starting transfers between devices: 13.2 us -> 0.01 us  [first_hops(): return [below, above, lax.ppermute(cols, 'col', turn)]]
    ppermute x1, waiting for transfers between devices: 0.01 us -> 4.2 us  [first_hops(): return [below, above, lax.ppermute(cols, 'col', turn)]]
  transfers between devices with their start and end apart: 3 -> 3, of which waited for: 0 -> 1; matrix products, arithmetic and copies ran while one was open for 0% -> 0% of each run, Pallas kernels for 10% -> 9%
where the time goes in v6:
time: 335 us; the launch traced here: 334 us
  Pallas kernels  320 us (96%)
  starting transfers between devices  7.07 us (2%)
  waiting for transfers between devices  4.21 us (1%)
    pallas_call x2, Pallas kernels, exchange(): pl.pallas_call(functools.partial(exchange_kernel, row_n, col_n, pieces, h...  237 us
    pallas_call x1, Pallas kernels, filter_step(): pl.pallas_call(functools.partial(filter_kernel, row_n, row_chunk), out_sh...  31.1 us
    pallas_call x1, Pallas kernels, hot_step(): pl.pallas_call(functools.partial(hot_kernel, row_n, hot_count), out_shape...  19.7 us
    pallas_call x1, Pallas kernels, last_step(): pl.pallas_call(last_kernel, out_shape=jax.ShapeDtypeStruct(acc.shape, jnp...  15.8 us
    pallas_call x2, Pallas kernels, dense(): pl.pallas_call(functools.partial(dense_kernel, tile_of), out_shape=jax.Sh...  11.4 us
  transfers between devices with their start and end apart: 3, of which 1 were waited for; matrix products, arithmetic and copies ran while one was open for 0% of the time, Pallas kernels for 9%

profile of v6, /device:TPU:2, one launch (start us, length us, event | category | flops | bytes accessed | tf_op | source)
XLA Modules:
  0.0 334.2 jit_solution(15398987928327871866)
XLA Ops:
  0.6 1.3 copy.9.hot
  2.0 0.6 pad_add_fusion.place
  2.5 5.7 %shard_map.87 = (bf16[2,128,3072]{2,1,0:T(8,128)(2,1)}, bf16[4,1536,128]{2,1,0:T(8,128)(2,1)}) custom-call(s32[2]{0:T(128)} %pad_add_fusion.place, s32[8,2]{1,0:T(8,128)} %copy.9.hot, f32[1536,3072]{1,0:T(8,128)} %refs_8_.3, f32[1536,3072]{1,0:T(8,128)} %refs_8_.3), custom_call_target="tpu_custom_call" | custom-call | tf_op jit(solution)/shard_map/pallas_call | solution.py:81
  8.2 5.2 %shard_map.86 = bf16[1,1536,1024]{2,1,0:T(8,128)(2,1)} custom-call(s32[2]{0:T(128)} %pad_add_fusion.place, s32[3,8,64]{2,1,0:T(8,128)} %pairs.3, s32[8]{0:T(128)} %counts.3, bf16[1,48,128,128]{3,2,1,0:T(8,128)(2,1)} %bitcast.11), custom_call_target="tpu_custom_call" | custom-call | tf_op jit(solution)/shard_map/pallas_call | solution.py:40
  13.4 136.7 %shard_map.88 = (bf16[1024,3072]{1,0:T(8,128)(2,1)}, bf16[16,1536,128]{2,1,0:T(8,128)(2,1)}, bf16[2,48,128,128]{3,2,1,0:T(8,128)(2,1)}, f32[1536,1]{1,0:T(8,128)}, f32[1,3072]{1,0:T(1,128)}) custom-call(s32[8,8]{1,0:T(8,128)} %sel.7, bf16[2,128,3072]{2,1,0:T(8,128)(2,1)} %get-tuple-element.14.rows_ref, bf16[4,1536,128]{2,1,0:T(8,128)(2,1)} %get-tuple-element.15.cols_ref, ...), custom_call_target="tpu_custom_call" | custom-call | tf_op jit(solution)/shard_map/pallas_call | solution.py:929
  150.1 6.2 %shard_map.89.refs_23_.refs_37_.refs_38_.wb_ref.refs_4_ = bf16[2,1536,1024]{2,1,0:T(8,128)(2,1)} custom-call(s32[2]{0:T(128)} %pad_add_fusion.place, s32[3,8,64]{2,1,0:T(8,128)} %pairs.3, s32[8]{0:T(128)} %counts.3, bf16[2,48,128,128]{3,2,1,0:T(8,128)(2,1)} %get-tuple-element.19.ham_ref), custom_call_target="tpu_custom_call" | custom-call | tf_op jit(solution)/shard_map/pallas_call | solution.py:40
  156.3 19.7 %shard_map.90 = (bf16[2,128,3072]{2,1,0:T(8,128)(2,1)}, bf16[4,1536,128]{2,1,0:T(8,128)(2,1)}) custom-call(s32[2]{0:T(128)} %pad_add_fusion.place, s32[8,2]{1,0:T(8,128)} %copy.9.hot, s32[8,8]{1,0:T(8,128)} %sel.7, bf16[1536,1024]{1,0:T(8,128)(2,1)} %bitcast.5, bf16[1536,1024]{1,0:T(8,128)(2,1)} %bitcast.6, f32[1536,3072]{1,0:T(8,128)} %refs_8_.3, ...), custom_call_target="tpu_custom_call" | custom-call | tf_op jit(solution)/shard_map/pallas_call | solution.py:1054
  176.1 1.3 collective-permute-start.1
  177.4 5.8 %collective-permute-start = (bf16[2,128,3072]{2,1,0:T(8,128)(2,1)}, bf16[2,128,3072]{2,1,0:T(8,128)(2,1)}, u32[]{:S(2)}, u32[]{:S(2)}) collective-permute-start(bf16[2,128,3072]{2,1,0:T(8,128)(2,1)} %get-tuple-element.21.rows_ref), channel_id=1, source_target_pairs={{0,8},{4,12},{8,16},{12,20},{16,24},{20,28},{1,9},{5,13},{9,17},{1... | collective-permute-start | bytes 4718600 | tf_op jit(solution)/shard_map/ppermute | solution.py:1068
  183.2 0.0 collective-permute-start.2
  183.2 31.1 %shard_map.91.refs_7_ = f32[1536,3072]{1,0:T(8,128)} custom-call(s32[2]{0:T(128)} %pad_add_fusion.place, s32[8,8]{1,0:T(8,128)} %sel.7, bf16[1536,1024]{1,0:T(8,128)(2,1)} %bitcast.8, bf16[1024,3072]{1,0:T(8,128)(2,1)} %get-tuple-element.22.refs_22_.refs_35_.refs_36_.s_ref, bf16[2,1536,1024]{2,1,0:T(8,128)(2,1)} %shard_map.89.refs_23_.refs_37_.refs_38_.wb_ref.refs_4_, ...), custom_call_target="tpu_custom_call" | custom-call | flops 19327352832 | bytes 56623104 | tf_op jit(solution)/shard_map/pallas_call | solution.py:1115
  214.2 4.2 %collective-permute-done.2.refs_2_ = bf16[4,1536,128]{2,1,0:T(8,128)(2,1)} collective-permute-done((bf16[4,1536,128]{2,1,0:T(8,128)(2,1)}, bf16[4,1536,128]{2,1,0:T(8,128)(2,1)}, u32[]{:S(2)}, u32[]{:S(2)}) %collective-permute-start.2) | collective-permute-done | bytes 1572896 | tf_op jit(solution)/shard_map/ppermute | solution.py:1071
  218.4 0.0 collective-permute-done.1.refs_1_
  218.4 0.0 collective-permute-done.refs_0_
  218.4 99.9 %shard_map.92 = (bf16[256,3072]{1,0:T(8,128)(2,1)}, f32[1536,3072]{1,0:T(8,128)}) custom-call(s32[8,8]{1,0:T(8,128)} %sel.7, bf16[2,128,3072]{2,1,0:T(8,128)(2,1)} %get-tuple-element.21.rows_ref, bf16[4,1536,128]{2,1,0:T(8,128)(2,1)} %get-tuple-element.23.cols_ref, bf16[2,128,3072]{2,1,0:T(8,128)(2,1)} %collective-permute-done.refs_0_, ...), custom_call_target="tpu_custom_call" | custom-call | tf_op jit(solution)/shard_map/pallas_call | solution.py:929
  318.3 15.8 %shard_map.93 = f32[1536,3072]{1,0:T(8,128)} custom-call(s32[2]{0:T(128)} %pad_add_fusion.place, f32[1536,3072]{1,0:T(8,128)} %get-tuple-element.24.acc_ref, bf16[1536,1024]{1,0:T(8,128)(2,1)} %bitcast.10, bf16[256,3072]{1,0:T(8,128)(2,1)} %get-tuple-element.25.s_ref), custom_call_target="tpu_custom_call" | custom-call | tf_op jit(solution)/shard_map/pallas_call | solution.py:959
Async XLA Ops:
  176.1 42.4 %collective-permute-start.1 = (bf16[2,128,3072]{2,1,0:T(8,128)(2,1)}, bf16[2,128,3072]{2,1,0:T(8,128)(2,1)}, u32[]{:S(2)}, u32[]{:S(2)}) collective-permute-start(bf16[2,128,3072]{2,1,0:T(8,128)(2,1)} %get-tuple-element.21.rows_ref), channel_id=1, source_target_pairs={{8,0},{12,4},{16,8},{20,12},{24,16},{28,20},{9,1},{13,5},{17,9},{2... | collective-permute-start | bytes 4718600 | tf_op jit(solution)/shard_map/ppermute | solution.py:1069
  177.4 41.1 %collective-permute-start = (bf16[2,128,3072]{2,1,0:T(8,128)(2,1)}, bf16[2,128,3072]{2,1,0:T(8,128)(2,1)}, u32[]{:S(2)}, u32[]{:S(2)}) collective-permute-start(bf16[2,128,3072]{2,1,0:T(8,128)(2,1)} %get-tuple-element.21.rows_ref), channel_id=1, source_target_pairs={{0,8},{4,12},{8,16},{12,20},{16,24},{20,28},{1,9},{5,13},{9,17},{1... | collective-permute-start | bytes 4718600 | tf_op jit(solution)/shard_map/ppermute | solution.py:1068
  183.2 35.3 %collective-permute-start.2 = (bf16[4,1536,128]{2,1,0:T(8,128)(2,1)}, bf16[4,1536,128]{2,1,0:T(8,128)(2,1)}, u32[]{:S(2)}, u32[]{:S(2)}) collective-permute-start(bf16[4,1536,128]{2,1,0:T(8,128)(2,1)} %get-tuple-element.23.cols_ref), channel_id=1, source_target_pairs={{0,2},{1,3},{2,0},{3,1},{4,6},{5,7},{6,4},{7,5},{8,10},{9,11},{10,... | collective-permute-start | bytes 4718600 | tf_op jit(solution)/shard_map/ppermute | solution.py:1071

commit v7 on v6

--- a/solution.py
+++ b/solution.py
@@ -170,14 +170,16 @@
 
     first_step = 2 if fused else 1
     if fused:
-        below_ref, above_ref, chip_ref, wa_hbm, wb_hbm, rd_ref, cd_ref, x_hbm, start_hbm, s_out, acc_out = some(11)
+        below_ref, above_ref, chip_ref = some(3)
+        side_refs = some(layout(row_n, col_n)[1] - 1)
+        wa_hbm, wb_hbm, rd_ref, cd_ref, x_hbm, start_hbm, s_out, acc_out = some(8)
     else:
         ham_ref, diag_ref, s_out, c_out, h_out, rd_out, cd_out = some(7)
     held, lane_buf, turn_buf, s_all, c_all = some(5)
     own_sem, line_recv, up_send, down_send, lane_send, lane_recv = some(6)
     chip_send, chip_recv, core_send, core_recv, turn_send, turn_recv = some(6)
     if fused:
-        acc, wa, wb_buf, x_buf, start_buf, via_buf, beta, st_buf, got, load_sem, wb_sem, x_sem, start_sem, acc_sem, via_send, via_recv = some(16)
+        acc, wa, wb_buf, x_buf, start_buf, via_buf, beta, st_buf, got, side_buf, load_sem, wb_sem, x_sem, start_sem, acc_sem, via_send, via_recv = some(17)
     else:
         ham_buf, far_buf, ham_sem, ham_recv, ham_up, ham_down, ham_lane, far_recv, far_send, far_chip = some(10)
         ham_rows = ham_ref.shape[0] // pieces
@@ -190,10 +192,11 @@
     line, lanes, at = g.line, g.lanes, g.at
 
     home = (g.col * ratio) // lanes
-    diag = at == home
     up_ok = (at + 1 < line) & ((home != line - 1) | (at + 1 != line - 1))
     down_ok = (at > 0) & ((home != 0) | (at - 1 != 0))
-    deaf = diag & ((at == 0) | (at == line - 1))
+    deaf = (at == home) & ((at == 0) | (at == line - 1))
+    far_base = jnp.where(at == 0, 2 * lanes, 0) if fused else 0
+    far_count = (line - 2) * lanes if fused else row_n
 
     def chip_slot(step):
         return (lax.rem(g.chip - step + g.chips, g.chips) * g.cores + g.core) * block_n
@@ -283,10 +286,14 @@
         source = slot * lanes + g.lane
         rows = pl.ds(pl.multiple_of(p * piece, piece), piece)
         blocks = [held[slot, h, rows, :] for h in range(hot_count)]
-        for step in range(1, lanes):
-            target = at * lanes + lax.rem(g.lane + step, lanes)
-            lane_buf[step - 1, slot, rows, :] = pick(target, source, blocks)
-            lane_copy(step, slot, p).start()
+
+        @pl.when((slot != at) | (not fused))
+        def _():
+            for step in range(1, lanes):
+                target = at * lanes + lax.rem(g.lane + step, lanes)
+                lane_buf[step - 1, slot, rows, :] = pick(target, source, blocks)
+                lane_copy(step, slot, p).start()
+
         s_all[s_rows(source, p), :] = pick(g.row, source, blocks)
 
     def tile_place(col, i):
@@ -494,11 +501,17 @@
         s, p = n // pieces, lax.rem(n, pieces)
         hears_below, hears_above = hears(s)
 
-        @pl.when(hears_below & (at != home))
+        if fused:
+            hears_below = (at - s >= 0) & ((s < 2) | (deaf == False))
+            hears_above = (at + s < line) & ((s < 2) | (deaf == False))
+        else:
+            hears_below, hears_above = hears_below & (deaf == False), hears_above & (deaf == False)
+
+        @pl.when(hears_below)
         def _():
             select(at - s, p)
 
-        @pl.when(hears_above & (s > 0) & (at != home))
+        @pl.when(hears_above & (s > 0))
         def _():
             select(at + s, p)
         return carry
@@ -543,9 +556,9 @@
                         if fused:
                             turn_buf[step - 1, q, strip, :] = value
                         else:
-                            turn_buf[step - 1, q, :, strip] = value.T
+                            turn_buf[step - 1, q, :, strip] = value.astype(jnp.float32).T.astype(turn_buf.dtype)
                     if not fused:
-                        s_all[rows, i * height + k * size:i * height + (k + 1) * size] = pick(g.row, q, blocks).T
+                        s_all[rows, i * height + k * size:i * height + (k + 1) * size] = pick(g.row, q, blocks).astype(jnp.float32).T.astype(s_all.dtype)
                 for step in range(1, lanes):
                     turn_copy(i, step, q).start()
 
@@ -556,7 +569,7 @@
                 act(i, q, home_lane)
             return carry
 
-        lax.fori_loop(0, row_n, one, 0)
+        lax.fori_loop(far_base, far_base + far_count, one, 0)
 
     def turn_came(i, q, home_lane):
         @pl.when(home_lane != g.lane)
@@ -617,32 +630,47 @@
                 acc[rows, band(n)] = value - start_buf[turn_n, rows, :] * (half_width / 2.0)
             return carry
 
-        def alpha_side(n, carry):
+        near_base = jnp.where(at == 0, 0, (line - 2) * lanes * size)
+        near_depth = pl.ds(pl.multiple_of(near_base, lanes * size), 2 * lanes * size)
+        far_depth = pl.ds(pl.multiple_of(far_base * size, lanes * size), far_count * size)
+
+        def alpha_side(m, carry):
+            n = jnp.where(deaf, lax.rem(m + g.lane * per_tile, stripes), m)
             tile, inner = n // per_tile, lax.rem(n, per_tile)
 
-            @pl.when(at != home)
+            @pl.when(deaf == False)
             def _():
                 for k in range(2):
                     rows = slice(k * rows_at_once, (k + 1) * rows_at_once)
                     acc[rows, band(n)] += jnp.dot(wa[rows, depth], s_all[depth, band(n)], preferred_element_type=jnp.float32)
 
-            @pl.when(diag)
+            @pl.when(deaf)
             def _():
                 _, home_lane = tile_place(g.col, tile)
 
                 @pl.when(home_lane == g.lane)
                 def _():
-                    for q in range(row_n):
-                        st_buf[:, q * size:(q + 1) * size] = c_all[q * hot_count + sel[g.row, q], band(inner), :]
+                    for j in range(far_count):
+                        q = far_base + j
+                        st_buf[:, j * size:(j + 1) * size] = c_all[q * hot_count + sel[g.row, q], band(inner), :]
 
                 @pl.when(home_lane != g.lane)
                 def _():
-                    for q in range(row_n):
-                        st_buf[:, q * size:(q + 1) * size] = got[got_at(tile), q, band(inner), :]
+                    @pl.when(inner == 0)
+                    def _():
+                        def come(q, carry):
+                            turn_copy(tile, 1, q).wait_recv()
+                            return carry
+
+                        lax.fori_loop(far_base, far_base + far_count, come, 0)
+
+                    for j in range(far_count):
+                        st_buf[:, j * size:(j + 1) * size] = got[got_at(tile), far_base + j, band(inner), :]
 
                 for k in range(2):
                     rows = slice(k * rows_at_once, (k + 1) * rows_at_once)
-                    acc[rows, band(n)] += dot_t(wa[rows, :], st_buf[...])
+                    value = jnp.dot(wa[rows, near_depth], s_all[near_depth, band(n)], preferred_element_type=jnp.float32)
+                    acc[rows, band(n)] += value + dot_t(wa[rows, far_depth], st_buf[...])
             acc_copy(n).start()
             return carry
 
@@ -658,10 +686,26 @@
                     via_leave(p).start()
 
         lax.fori_loop(pieces, half, relay, 0)
+        take_sides = [pltpu.make_async_copy(side, side_buf.at[step], load_sem.at[1 + step]) for step, side in enumerate(side_refs)]
+        for copy in take_sides:
+            copy.start()
+        lax.fori_loop(pieces, half, digest, 0)
         take_wa.start()
         for copy in loads(0):
             copy.start()
-        lax.fori_loop(0, half, digest, 0)
+        lax.fori_loop(0, pieces, digest, 0)
+        for copy in take_sides:
+            copy.wait()
+
+        def sides(p, carry):
+            rows = pl.ds(pl.multiple_of(p * piece, piece), piece)
+            for step in range(1, lanes):
+                source = at * lanes + lax.rem(g.lane - step + lanes, lanes)
+                blocks = [side_buf[step - 1, h, rows, :] for h in range(hot_count)]
+                s_all[s_rows(source, p), :] = pick(g.row, source, blocks)
+            return carry
+
+        lax.fori_loop(0, pieces, sides, 0)
     else:
         def held_rows(p, carry):
             @pl.when(up_ok & (up_first == False))
@@ -676,12 +720,10 @@
         lax.fori_loop(0, pieces, relay, 0)
         lax.fori_loop(0, pieces, digest, 0)
         lax.fori_loop(0, pieces, ham_next, 0)
-        if line > 2:
-            far_steps(2)
+        for s in range(2, line):
+            far_steps(s)
         lax.fori_loop(0, pieces, held_rows, 0)
         lax.fori_loop(pieces, half, advance, 0)
-        for s in range(3, line):
-            far_steps(s)
     for step in range(first_step, g.chips):
         for b in range(block_n):
             slot = chip_slot(step) + b
@@ -706,6 +748,14 @@
     else:
         take_wa.wait()
 
+        @pl.when(deaf)
+        def _():
+            def turn_on(q, carry):
+                turn(q)
+                return carry
+
+            lax.fori_loop(far_base, far_base + far_count, turn_on, 0)
+
     def middle(n, carry):
         if leaves is not None:
             @pl.when((n < half + 2) & (at == far_before))
@@ -721,15 +771,15 @@
                 via_land(p).start()
 
         advance(n, carry)
-
-        @pl.when(diag)
-        def _():
-            for u in range(per_step):
-                q = (n - half) * per_step + u
-
-                @pl.when(q < row_n)
-                def _():
-                    turn(q)
+        if not fused:
+            @pl.when(deaf)
+            def _():
+                for u in range(per_step):
+                    q = (n - half) * per_step + u
+
+                    @pl.when(q < row_n)
+                    def _():
+                        turn(q)
         if fused:
             some_stripes(beta_side, n - half)
         return carry
@@ -740,7 +790,10 @@
                 lane_came(step, slot, p).wait_recv()
             return carry
 
-        @pl.when(at != home)
+        near = (slot - at <= 1) & (at - slot <= 1) if fused else False
+        away = slot != at if fused else True
+
+        @pl.when(((deaf == False) | near) & away)
         def _():
             lax.fori_loop(0, pieces, one, 0)
 
@@ -749,10 +802,6 @@
         for other in range(1, line):
             lanes_came(lax.rem(late + other, line))
 
-        @pl.when(diag)
-        def _():
-            turns(turn_came)
-
         def ending(n, carry):
             advance(n, carry)
             some_stripes(alpha_side, n - half - pieces)
@@ -761,7 +810,7 @@
         lax.fori_loop(half + pieces, pieces * line, ending, 0)
         lanes_came(late)
 
-        @pl.when(diag)
+        @pl.when(deaf)
         def _():
             s_all[pl.ds(pl.multiple_of(late * lanes * size, size), lanes * size), :] = jnp.zeros((lanes * size, width), s_all.dtype)
 
@@ -775,7 +824,7 @@
         for slot in range(line):
             lanes_came(slot)
 
-        @pl.when(diag)
+        @pl.when(deaf)
         def _():
             turns(turn_came)
 
@@ -784,7 +833,7 @@
         put_s.wait()
         put_cols.wait()
 
-    @pl.when(diag)
+    @pl.when(deaf)
     def _():
         turns(turn_sent)
 
@@ -799,7 +848,10 @@
         def _():
             down_copy(slot, p).wait_send()
 
-        @pl.when(at != home)
+        near = (slot - at <= 1) & (at - slot <= 1) if fused else False
+        away = slot != at if fused else True
+
+        @pl.when(((deaf == False) | near) & away)
         def _():
             for step in range(1, lanes):
                 lane_copy(step, slot, p).wait_send()
@@ -879,7 +931,7 @@
         wa, wb, rd, cd, x, start = product
         stripe = 256 if height % 256 == 0 else size
         args += list(ahead) + [wa, wb, rd, cd, x, start]
-        in_specs += [anywhere] * 5 + [whole] * 2 + [anywhere] * 2
+        in_specs += [anywhere] * (len(ahead) + 2) + [whole] * 2 + [anywhere] * 2
         out_shape = [
             jax.ShapeDtypeStruct((lanes * size, width), jnp.bfloat16),
             jax.ShapeDtypeStruct((height, width), jnp.float32),
@@ -893,9 +945,10 @@
             pltpu.VMEM((2, height, stripe), jnp.float32),
             vmem(pieces - pieces // 2, hot_count, size // pieces, width),
             vmem(height, row_n * size),
-            vmem(stripe, row_n * size),
+            vmem(stripe, (line - 2) * lanes * size),
             vmem(got_slots(row_n, col_n), row_n, height, size),
-            dma((2,)),
+            vmem(others, hot_count, size, width),
+            dma((1 + others,)),
             dma((2,)),
             dma((2,)),
             dma((2,)),
@@ -1068,7 +1121,10 @@
     below = lax.ppermute(rows, "row", upward)
     above = lax.ppermute(rows, "row", [(b, a) for a, b in upward])
     turn = [(c, (c // cores + 1) % chips * cores + c % cores) for c in range(col_n)]
-    return [below, above, lax.ppermute(cols, "col", turn)]
+    ahead = [below, above, lax.ppermute(cols, "col", turn)]
+    for step in range(1, lanes):
+        ahead.append(lax.ppermute(rows, "row", [(r, r // lanes * lanes + (r + step) % lanes) for r in range(row_n)]))
+    return ahead
 
 
 def filter_kernel(source_count, row_chunk, place, sel, wa_ref, s_ref, wb_ref, rd_ref, cd_ref, *refs):

time: 335 us -> 305 us (0.910)
  the two profiles are of different devices: /device:TPU:2 before, /device:TPU:24 now
where the time goes in v7:
time: 305 us; the launch traced here: 304 us
  Pallas kernels  288 us (94%)
  waiting for transfers between devices  6.76 us (2%)
  starting transfers between devices  6.33 us (2%)
    pallas_call x2, Pallas kernels, exchange(): pl.pallas_call(functools.partial(exchange_kernel, row_n, col_n, pieces, h...  205 us
    pallas_call x1, Pallas kernels, filter_step(): pl.pallas_call(functools.partial(filter_kernel, row_n, row_chunk), out_sh...  30.7 us
    pallas_call x1, Pallas kernels, hot_step(): pl.pallas_call(functools.partial(hot_kernel, row_n, hot_count), out_shape...  18.7 us
    pallas_call x1, Pallas kernels, last_step(): pl.pallas_call(last_kernel, out_shape=jax.ShapeDtypeStruct(acc.shape, jnp...  15.9 us
    pallas_call x2, Pallas kernels, dense(): pl.pallas_call(functools.partial(dense_kernel, tile_of), out_shape=jax.Sh...  11.6 us
  transfers between devices with their start and end apart: 4, of which 3 were waited for; matrix products, arithmetic and copies ran while one was open for 0% of the time, Pallas kernels for 10%

profile of v7, /device:TPU:24, one launch (start us, length us, event | category | flops | bytes accessed | tf_op | source)
XLA Modules:
  0.0 303.6 jit_solution(14512703072172067337)
XLA Ops:
  0.6 1.3 copy.9.hot
  2.0 0.7 pad_add_fusion.place
  2.6 5.7 %shard_map.87 = (bf16[2,128,3072]{2,1,0:T(8,128)(2,1)}, bf16[4,1536,128]{2,1,0:T(8,128)(2,1)}) custom-call(s32[2]{0:T(128)} %pad_add_fusion.place, s32[8,2]{1,0:T(8,128)} %copy.9.hot, f32[1536,3072]{1,0:T(8,128)} %refs_9_.1, f32[1536,3072]{1,0:T(8,128)} %refs_9_.1), custom_call_target="tpu_custom_call" | custom-call | tf_op jit(solution)/shard_map/pallas_call | solution.py:81
  8.3 5.0 %shard_map.86 = bf16[1,1536,1024]{2,1,0:T(8,128)(2,1)} custom-call(s32[2]{0:T(128)} %pad_add_fusion.place, s32[3,8,64]{2,1,0:T(8,128)} %pairs.3, s32[8]{0:T(128)} %counts.3, bf16[1,48,128,128]{3,2,1,0:T(8,128)(2,1)} %bitcast.11), custom_call_target="tpu_custom_call" | custom-call | tf_op jit(solution)/shard_map/pallas_call | solution.py:40
  13.3 128.9 %shard_map.88 = (bf16[1024,3072]{1,0:T(8,128)(2,1)}, bf16[16,1536,128]{2,1,0:T(8,128)(2,1)}, bf16[2,48,128,128]{3,2,1,0:T(8,128)(2,1)}, f32[1536,1]{1,0:T(8,128)}, f32[1,3072]{1,0:T(1,128)}) custom-call(s32[8,8]{1,0:T(8,128)} %sel.7, bf16[2,128,3072]{2,1,0:T(8,128)(2,1)} %get-tuple-element.14.rows_ref, bf16[4,1536,128]{2,1,0:T(8,128)(2,1)} %get-tuple-element.15.cols_ref, ...), custom_call_target="tpu_custom_call" | custom-call | tf_op jit(solution)/shard_map/pallas_call | solution.py:982
  142.2 6.5 %shard_map.89.refs_23_.refs_37_.refs_38_.wb_ref.refs_5_ = bf16[2,1536,1024]{2,1,0:T(8,128)(2,1)} custom-call(s32[2]{0:T(128)} %pad_add_fusion.place, s32[3,8,64]{2,1,0:T(8,128)} %pairs.3, s32[8]{0:T(128)} %counts.3, bf16[2,48,128,128]{3,2,1,0:T(8,128)(2,1)} %get-tuple-element.19.ham_ref), custom_call_target="tpu_custom_call" | custom-call | tf_op jit(solution)/shard_map/pallas_call | solution.py:40
  148.8 18.7 %shard_map.90 = (bf16[2,128,3072]{2,1,0:T(8,128)(2,1)}, bf16[4,1536,128]{2,1,0:T(8,128)(2,1)}) custom-call(s32[2]{0:T(128)} %pad_add_fusion.place, s32[8,2]{1,0:T(8,128)} %copy.9.hot, s32[8,8]{1,0:T(8,128)} %sel.7, bf16[1536,1024]{1,0:T(8,128)(2,1)} %bitcast.5, bf16[1536,1024]{1,0:T(8,128)(2,1)} %bitcast.6, f32[1536,3072]{1,0:T(8,128)} %refs_9_.1, ...), custom_call_target="tpu_custom_call" | custom-call | tf_op jit(solution)/shard_map/pallas_call | solution.py:1107
  167.5 2.5 collective-permute-start.3
  170.0 2.4 collective-permute-start.1
  172.4 1.3 collective-permute-start
  173.7 0.1 collective-permute-start.2
  173.8 30.7 %shard_map.91.refs_8_ = f32[1536,3072]{1,0:T(8,128)} custom-call(s32[2]{0:T(128)} %pad_add_fusion.place, s32[8,8]{1,0:T(8,128)} %sel.7, bf16[1536,1024]{1,0:T(8,128)(2,1)} %bitcast.8, bf16[1024,3072]{1,0:T(8,128)(2,1)} %get-tuple-element.22.refs_22_.refs_35_.refs_36_.s_ref, bf16[2,1536,1024]{2,1,0:T(8,128)(2,1)} %shard_map.89.refs_23_.refs_37_.refs_38_.wb_ref.refs_5_, ...), custom_call_target="tpu_custom_call" | custom-call | flops 19327352832 | bytes 56623104 | tf_op jit(solution)/shard_map/pallas_call | solution.py:1171
  204.5 0.0 collective-permute-done.2.refs_2_
  204.5 1.0 collective-permute-done.3.refs_3_
  205.5 0.5 collective-permute-done.1.refs_1_
  206.0 5.2 %collective-permute-done.refs_0_ = bf16[2,128,3072]{2,1,0:T(8,128)(2,1)} collective-permute-done((bf16[2,128,3072]{2,1,0:T(8,128)(2,1)}, bf16[2,128,3072]{2,1,0:T(8,128)(2,1)}, u32[]{:S(2)}, u32[]{:S(2)}) %collective-permute-start) | collective-permute-done | bytes 1572896 | tf_op jit(solution)/shard_map/ppermute | solution.py:1121
  211.2 76.5 %shard_map.92 = (bf16[256,3072]{1,0:T(8,128)(2,1)}, f32[1536,3072]{1,0:T(8,128)}) custom-call(s32[8,8]{1,0:T(8,128)} %sel.7, bf16[2,128,3072]{2,1,0:T(8,128)(2,1)} %get-tuple-element.21.rows_ref, bf16[4,1536,128]{2,1,0:T(8,128)(2,1)} %get-tuple-element.23.cols_ref, bf16[2,128,3072]{2,1,0:T(8,128)(2,1)} %collective-permute-done.refs_0_, ...), custom_call_target="tpu_custom_call" | custom-call | tf_op jit(solution)/shard_map/pallas_call | solution.py:982
  287.8 15.9 %shard_map.93 = f32[1536,3072]{1,0:T(8,128)} custom-call(s32[2]{0:T(128)} %pad_add_fusion.place, f32[1536,3072]{1,0:T(8,128)} %get-tuple-element.24.acc_ref, bf16[1536,1024]{1,0:T(8,128)(2,1)} %bitcast.10, bf16[256,3072]{1,0:T(8,128)(2,1)} %get-tuple-element.25.s_ref), custom_call_target="tpu_custom_call" | custom-call | tf_op jit(solution)/shard_map/pallas_call | solution.py:1012
Async XLA Ops:
  167.5 38.0 %collective-permute-start.3 = (bf16[2,128,3072]{2,1,0:T(8,128)(2,1)}, bf16[2,128,3072]{2,1,0:T(8,128)(2,1)}, u32[]{:S(2)}, u32[]{:S(2)}) collective-permute-start(bf16[2,128,3072]{2,1,0:T(8,128)(2,1)} %get-tuple-element.21.rows_ref), channel_id=1, source_target_pairs={{0,4},{4,0},{8,12},{12,8},{16,20},{20,16},{24,28},{28,24},{1,5},{5... | collective-permute-start | bytes 4718600 | tf_op jit(solution)/shard_map/ppermute | solution.py:1126
  170.0 36.0 %collective-permute-start.1 = (bf16[2,128,3072]{2,1,0:T(8,128)(2,1)}, bf16[2,128,3072]{2,1,0:T(8,128)(2,1)}, u32[]{:S(2)}, u32[]{:S(2)}) collective-permute-start(bf16[2,128,3072]{2,1,0:T(8,128)(2,1)} %get-tuple-element.21.rows_ref), channel_id=1, source_target_pairs={{8,0},{12,4},{16,8},{20,12},{24,16},{28,20},{9,1},{13,5},{17,9},{2... | collective-permute-start | bytes 4718600 | tf_op jit(solution)/shard_map/ppermute | solution.py:1122
  172.4 38.8 %collective-permute-start = (bf16[2,128,3072]{2,1,0:T(8,128)(2,1)}, bf16[2,128,3072]{2,1,0:T(8,128)(2,1)}, u32[]{:S(2)}, u32[]{:S(2)}) collective-permute-start(bf16[2,128,3072]{2,1,0:T(8,128)(2,1)} %get-tuple-element.21.rows_ref), channel_id=1, source_target_pairs={{0,8},{4,12},{8,16},{12,20},{16,24},{20,28},{1,9},{5,13},{9,17},{1... | collective-permute-start | bytes 4718600 | tf_op jit(solution)/shard_map/ppermute | solution.py:1121
  173.7 30.7 %collective-permute-start.2 = (bf16[4,1536,128]{2,1,0:T(8,128)(2,1)}, bf16[4,1536,128]{2,1,0:T(8,128)(2,1)}, u32[]{:S(2)}, u32[]{:S(2)}) collective-permute-start(bf16[4,1536,128]{2,1,0:T(8,128)(2,1)} %get-tuple-element.23.cols_ref), channel_id=1, source_target_pairs={{0,2},{1,3},{2,0},{3,1},{4,6},{5,7},{6,4},{7,5},{8,10},{9,11},{10,... | collective-permute-start | bytes 4718600 | tf_op jit(solution)/shard_map/ppermute | solution.py:1124

commit v8 on v7

--- a/solution.py
+++ b/solution.py
@@ -195,13 +195,14 @@
     up_ok = (at + 1 < line) & ((home != line - 1) | (at + 1 != line - 1))
     down_ok = (at > 0) & ((home != 0) | (at - 1 != 0))
     deaf = (at == home) & ((at == 0) | (at == line - 1))
-    far_base = jnp.where(at == 0, 2 * lanes, 0) if fused else 0
-    far_count = (line - 2) * lanes if fused else row_n
+    far_base = jnp.where(at == 0, first_step * lanes, 0)
+    far_count = (line - first_step) * lanes
 
     def chip_slot(step):
         return (lax.rem(g.chip - step + g.chips, g.chips) * g.cores + g.core) * block_n
 
     own_slot = g.col * block_n
+    own_chip = g.chip * g.cores * ratio
     take = pltpu.make_async_copy(rows_ref, held.at[at], own_sem.at[0])
     take_cols = pltpu.make_async_copy(cols_ref, c_all.at[pl.ds(own_slot, block_n)], own_sem.at[1])
     take.start()
@@ -499,13 +500,8 @@
 
     def digest(n, carry):
         s, p = n // pieces, lax.rem(n, pieces)
-        hears_below, hears_above = hears(s)
-
-        if fused:
-            hears_below = (at - s >= 0) & ((s < 2) | (deaf == False))
-            hears_above = (at + s < line) & ((s < 2) | (deaf == False))
-        else:
-            hears_below, hears_above = hears_below & (deaf == False), hears_above & (deaf == False)
+        hears_below = (at - s >= 0) & ((s < first_step) | (deaf == False))
+        hears_above = (at + s < line) & ((s < first_step) | (deaf == False))
 
         @pl.when(hears_below)
         def _():
@@ -677,7 +673,6 @@
         def some_stripes(work, turn_n):
             lax.fori_loop(turn_n * share, jnp.minimum(turn_n * share + share, stripes), work, 0)
 
-    per_step = -(-row_n // pieces)
     if fused:
         if leaves is not None:
             @pl.when(leaves)
@@ -719,6 +714,21 @@
 
         lax.fori_loop(0, pieces, relay, 0)
         lax.fori_loop(0, pieces, digest, 0)
+        take_cols.wait()
+        if g.cores == 2:
+            for b in range(block_n):
+                core_came(0, b).wait_recv()
+
+        @pl.when(deaf)
+        def _():
+            def turn_early(q, carry):
+                @pl.when(q // lanes != at)
+                def _():
+                    turn(q)
+                return carry
+
+            lax.fori_loop(own_chip, own_chip + g.cores * ratio, turn_early, 0)
+
         lax.fori_loop(0, pieces, ham_next, 0)
         for s in range(2, line):
             far_steps(s)
@@ -731,14 +741,24 @@
             if g.cores == 2:
                 core_copy(step, b).start()
 
-    take_cols.wait()
     if fused:
+        take_cols.wait()
         take_chip.wait()
     if g.cores == 2:
-        for step in range(g.chips):
+        for step in range(0 if fused else 1, g.chips):
             for b in range(block_n):
                 core_came(step, b).wait_recv()
     if not fused:
+        @pl.when(deaf)
+        def _():
+            def turn_rest(q, carry):
+                @pl.when(q // (g.cores * ratio) != g.chip)
+                def _():
+                    turn(q)
+                return carry
+
+            lax.fori_loop(far_base, far_base + far_count, turn_rest, 0)
+
         cd_out[...] = diag_ref[:, pl.ds(pl.multiple_of(g.col * width, width), width)]
         for k in range(height // size):
             strip = diag_ref[:, pl.ds(pl.multiple_of(g.row * height + k * size, size), size)]
@@ -771,15 +791,6 @@
                 via_land(p).start()
 
         advance(n, carry)
-        if not fused:
-            @pl.when(deaf)
-            def _():
-                for u in range(per_step):
-                    q = (n - half) * per_step + u
-
-                    @pl.when(q < row_n)
-                    def _():
-                        turn(q)
         if fused:
             some_stripes(beta_side, n - half)
         return carry
@@ -790,7 +801,7 @@
                 lane_came(step, slot, p).wait_recv()
             return carry
 
-        near = (slot - at <= 1) & (at - slot <= 1) if fused else False
+        near = (slot - at < first_step) & (at - slot < first_step)
         away = slot != at if fused else True
 
         @pl.when(((deaf == False) | near) & away)
@@ -848,7 +859,7 @@
         def _():
             down_copy(slot, p).wait_send()
 
-        near = (slot - at <= 1) & (at - slot <= 1) if fused else False
+        near = (slot - at < first_step) & (at - slot < first_step)
         away = slot != at if fused else True
 
         @pl.when(((deaf == False) | near) & away)

time: 305 us -> 301 us (0.987)
    ppermute x1, waiting for transfers between devices: 5.25 us -> 0.52 us  [first_hops(): below = lax.ppermute(rows, 'row', upward)]
    ppermute x1, waiting for transfers between devices: 0.01 us -> 3.84 us  [first_hops(): ahead = [below, above, lax.ppermute(cols, 'col', turn)]]
    pallas_call x2, Pallas kernels: 205 us -> 202 us  [exchange(): pl.pallas_call(functools.partial(exchange_kernel, row_n, col_n, pieces, h...]
  transfers between devices with their start and end apart: 4 -> 4, of which waited for: 3 -> 2; matrix products, arithmetic and copies ran while one was open for 0% -> 0% of each run, Pallas kernels for 10% -> 10%
where the time goes in v8:
time: 301 us; the launch traced here: 299 us
  Pallas kernels  288 us (96%)
  waiting for transfers between devices  4.37 us (1%)
  starting transfers between devices  3.87 us (1%)
    pallas_call x2, Pallas kernels, exchange(): pl.pallas_call(functools.partial(exchange_kernel, row_n, col_n, pieces, h...  202 us
    pallas_call x1, Pallas kernels, filter_step(): pl.pallas_call(functools.partial(filter_kernel, row_n, row_chunk), out_sh...  30.9 us
    pallas_call x1, Pallas kernels, hot_step(): pl.pallas_call(functools.partial(hot_kernel, row_n, hot_count), out_shape...  21.4 us
    pallas_call x1, Pallas kernels, last_step(): pl.pallas_call(last_kernel, out_shape=jax.ShapeDtypeStruct(acc.shape, jnp...  15.8 us
    pallas_call x2, Pallas kernels, dense(): pl.pallas_call(functools.partial(dense_kernel, tile_of), out_shape=jax.Sh...  12.5 us
  transfers between devices with their start and end apart: 4, of which 2 were waited for; matrix products, arithmetic and copies ran while one was open for 0% of the time, Pallas kernels for 10%

profile of v8, /device:TPU:24, one launch (start us, length us, event | category | flops | bytes accessed | tf_op | source)
XLA Modules:
  0.0 299.2 jit_solution(882923488010767246)
XLA Ops:
  0.6 1.3 copy.9.hot
  2.0 0.7 pad_add_fusion.place
  2.6 5.7 %shard_map.87 = (bf16[2,128,3072]{2,1,0:T(8,128)(2,1)}, bf16[4,1536,128]{2,1,0:T(8,128)(2,1)}) custom-call(s32[2]{0:T(128)} %pad_add_fusion.place, s32[8,2]{1,0:T(8,128)} %copy.9.hot, f32[1536,3072]{1,0:T(8,128)} %refs_9_.1, f32[1536,3072]{1,0:T(8,128)} %refs_9_.1), custom_call_target="tpu_custom_call" | custom-call | tf_op jit(solution)/shard_map/pallas_call | solution.py:81
  8.3 5.3 %shard_map.86 = bf16[1,1536,1024]{2,1,0:T(8,128)(2,1)} custom-call(s32[2]{0:T(128)} %pad_add_fusion.place, s32[3,8,64]{2,1,0:T(8,128)} %pairs.3, s32[8]{0:T(128)} %counts.3, bf16[1,48,128,128]{3,2,1,0:T(8,128)(2,1)} %bitcast.11), custom_call_target="tpu_custom_call" | custom-call | tf_op jit(solution)/shard_map/pallas_call | solution.py:40
  13.6 128.3 %shard_map.88 = (bf16[1024,3072]{1,0:T(8,128)(2,1)}, bf16[16,1536,128]{2,1,0:T(8,128)(2,1)}, bf16[2,48,128,128]{3,2,1,0:T(8,128)(2,1)}, f32[1536,1]{1,0:T(8,128)}, f32[1,3072]{1,0:T(1,128)}) custom-call(s32[8,8]{1,0:T(8,128)} %sel.7, bf16[2,128,3072]{2,1,0:T(8,128)(2,1)} %get-tuple-element.14.rows_ref, bf16[4,1536,128]{2,1,0:T(8,128)(2,1)} %get-tuple-element.15.cols_ref, ...), custom_call_target="tpu_custom_call" | custom-call | tf_op jit(solution)/shard_map/pallas_call | solution.py:993
  141.9 7.2 %shard_map.89.refs_23_.refs_37_.refs_38_.wb_ref.refs_5_ = bf16[2,1536,1024]{2,1,0:T(8,128)(2,1)} custom-call(s32[2]{0:T(128)} %pad_add_fusion.place, s32[3,8,64]{2,1,0:T(8,128)} %pairs.3, s32[8]{0:T(128)} %counts.3, bf16[2,48,128,128]{3,2,1,0:T(8,128)(2,1)} %get-tuple-element.19.ham_ref), custom_call_target="tpu_custom_call" | custom-call | tf_op jit(solution)/shard_map/pallas_call | solution.py:40
  149.1 21.4 %shard_map.90 = (bf16[2,128,3072]{2,1,0:T(8,128)(2,1)}, bf16[4,1536,128]{2,1,0:T(8,128)(2,1)}) custom-call(s32[2]{0:T(128)} %pad_add_fusion.place, s32[8,2]{1,0:T(8,128)} %copy.9.hot, s32[8,8]{1,0:T(8,128)} %sel.7, bf16[1536,1024]{1,0:T(8,128)(2,1)} %bitcast.5, bf16[1536,1024]{1,0:T(8,128)(2,1)} %bitcast.6, f32[1536,3072]{1,0:T(8,128)} %refs_9_.1, ...), custom_call_target="tpu_custom_call" | custom-call | tf_op jit(solution)/shard_map/pallas_call | solution.py:1118
  170.5 0.1 collective-permute-start.3
  170.6 2.4 collective-permute-start.1
  173.0 1.3 collective-permute-start
  174.3 0.1 collective-permute-start.2
  174.4 30.9 %shard_map.91.refs_8_ = f32[1536,3072]{1,0:T(8,128)} custom-call(s32[2]{0:T(128)} %pad_add_fusion.place, s32[8,8]{1,0:T(8,128)} %sel.7, bf16[1536,1024]{1,0:T(8,128)(2,1)} %bitcast.8, bf16[1024,3072]{1,0:T(8,128)(2,1)} %get-tuple-element.22.refs_22_.refs_35_.refs_36_.s_ref, bf16[2,1536,1024]{2,1,0:T(8,128)(2,1)} %shard_map.89.refs_23_.refs_37_.refs_38_.wb_ref.refs_5_, ...), custom_call_target="tpu_custom_call" | custom-call | flops 19327352832 | bytes 56623104 | tf_op jit(solution)/shard_map/pallas_call | solution.py:1182
  205.3 3.8 %collective-permute-done.2.refs_2_ = bf16[4,1536,128]{2,1,0:T(8,128)(2,1)} collective-permute-done((bf16[4,1536,128]{2,1,0:T(8,128)(2,1)}, bf16[4,1536,128]{2,1,0:T(8,128)(2,1)}, u32[]{:S(2)}, u32[]{:S(2)}) %collective-permute-start.2) | collective-permute-done | bytes 1572896 | tf_op jit(solution)/shard_map/ppermute | solution.py:1135
  209.1 0.0 collective-permute-done.3.refs_3_
  209.1 0.0 collective-permute-done.1.refs_1_
  209.1 0.5 collective-permute-done.refs_0_
  209.6 73.7 %shard_map.92 = (bf16[256,3072]{1,0:T(8,128)(2,1)}, f32[1536,3072]{1,0:T(8,128)}) custom-call(s32[8,8]{1,0:T(8,128)} %sel.7, bf16[2,128,3072]{2,1,0:T(8,128)(2,1)} %get-tuple-element.21.rows_ref, bf16[4,1536,128]{2,1,0:T(8,128)(2,1)} %get-tuple-element.23.cols_ref, bf16[2,128,3072]{2,1,0:T(8,128)(2,1)} %collective-permute-done.refs_0_, ...), custom_call_target="tpu_custom_call" | custom-call | tf_op jit(solution)/shard_map/pallas_call | solution.py:993
  283.4 15.8 %shard_map.93 = f32[1536,3072]{1,0:T(8,128)} custom-call(s32[2]{0:T(128)} %pad_add_fusion.place, f32[1536,3072]{1,0:T(8,128)} %get-tuple-element.24.acc_ref, bf16[1536,1024]{1,0:T(8,128)(2,1)} %bitcast.10, bf16[256,3072]{1,0:T(8,128)(2,1)} %get-tuple-element.25.s_ref), custom_call_target="tpu_custom_call" | custom-call | tf_op jit(solution)/shard_map/pallas_call | solution.py:1023
Async XLA Ops:
  170.5 38.6 %collective-permute-start.3 = (bf16[2,128,3072]{2,1,0:T(8,128)(2,1)}, bf16[2,128,3072]{2,1,0:T(8,128)(2,1)}, u32[]{:S(2)}, u32[]{:S(2)}) collective-permute-start(bf16[2,128,3072]{2,1,0:T(8,128)(2,1)} %get-tuple-element.21.rows_ref), channel_id=1, source_target_pairs={{0,4},{4,0},{8,12},{12,8},{16,20},{20,16},{24,28},{28,24},{1,5},{5... | collective-permute-start | bytes 4718600 | tf_op jit(solution)/shard_map/ppermute | solution.py:1137
  170.6 38.5 %collective-permute-start.1 = (bf16[2,128,3072]{2,1,0:T(8,128)(2,1)}, bf16[2,128,3072]{2,1,0:T(8,128)(2,1)}, u32[]{:S(2)}, u32[]{:S(2)}) collective-permute-start(bf16[2,128,3072]{2,1,0:T(8,128)(2,1)} %get-tuple-element.21.rows_ref), channel_id=1, source_target_pairs={{8,0},{12,4},{16,8},{20,12},{24,16},{28,20},{9,1},{13,5},{17,9},{2... | collective-permute-start | bytes 4718600 | tf_op jit(solution)/shard_map/ppermute | solution.py:1133
  173.0 36.6 %collective-permute-start = (bf16[2,128,3072]{2,1,0:T(8,128)(2,1)}, bf16[2,128,3072]{2,1,0:T(8,128)(2,1)}, u32[]{:S(2)}, u32[]{:S(2)}) collective-permute-start(bf16[2,128,3072]{2,1,0:T(8,128)(2,1)} %get-tuple-element.21.rows_ref), channel_id=1, source_target_pairs={{0,8},{4,12},{8,16},{12,20},{16,24},{20,28},{1,9},{5,13},{9,17},{1... | collective-permute-start | bytes 4718600 | tf_op jit(solution)/shard_map/ppermute | solution.py:1132
  174.3 34.8 %collective-permute-start.2 = (bf16[4,1536,128]{2,1,0:T(8,128)(2,1)}, bf16[4,1536,128]{2,1,0:T(8,128)(2,1)}, u32[]{:S(2)}, u32[]{:S(2)}) collective-permute-start(bf16[4,1536,128]{2,1,0:T(8,128)(2,1)} %get-tuple-element.23.cols_ref), channel_id=1, source_target_pairs={{0,2},{1,3},{2,0},{3,1},{4,6},{5,7},{6,4},{7,5},{8,10},{9,11},{10,... | collective-permute-start | bytes 4718600 | tf_op jit(solution)/shard_map/ppermute | solution.py:1135

commit v9 on v8

--- a/solution.py
+++ b/solution.py
@@ -440,7 +440,7 @@
         far_end = jnp.where(2 * far_home < line, line - 1, 0)
         far_before = jnp.where(far_end > far_home, far_end - 1, far_end + 1)
         far_slot = jnp.where(far_end > far_home, far_end - 2, far_end + 2)
-        kept = pieces // 2
+        kept = pieces * 3 // 4
 
         def via_leave(p):
             return remote(part(via_slot, p), via_buf.at[p - kept], via_send.at[0, p - kept], via_recv.at[0, p - kept], g.other_chip(across))
@@ -777,23 +777,24 @@
             lax.fori_loop(far_base, far_base + far_count, turn_on, 0)
 
     def middle(n, carry):
+        if fused:
+            some_stripes(beta_side, n - half)
         if leaves is not None:
-            @pl.when((n < half + 2) & (at == far_before))
-            def _():
-                p = kept + lax.rem(n - half, 2)
+            via_p = kept + jnp.minimum(n - half, pieces - kept - 1)
+
+            @pl.when((n < half + pieces - kept) & (at == far_before))
+            def _():
+                p = via_p
                 via_came(0, p).wait_recv()
                 via_pass(p).start()
 
-            @pl.when((n >= half) & (n < half + 2) & (at == far_end))
-            def _():
-                p = kept + lax.rem(n - half, 2)
+            @pl.when((n < half + pieces - kept) & (at == far_end))
+            def _():
+                p = via_p
                 via_came(1, p).wait_recv()
                 via_land(p).start()
 
-        advance(n, carry)
-        if fused:
-            some_stripes(beta_side, n - half)
-        return carry
+        return advance(n, carry)
 
     def lanes_came(slot):
         def one(p, carry):
@@ -814,9 +815,8 @@
             lanes_came(lax.rem(late + other, line))
 
         def ending(n, carry):
-            advance(n, carry)
             some_stripes(alpha_side, n - half - pieces)
-            return carry
+            return advance(n, carry)
 
         lax.fori_loop(half + pieces, pieces * line, ending, 0)
         lanes_came(late)
@@ -909,7 +909,7 @@
     hot_count, size, width = rows.shape
     block_n, height = cols.shape[:2]
     ratio = row_n // col_n
-    pieces = 4
+    pieces = 8
     fused = product is not None
     line, lanes, chips, _ = layout(row_n, col_n)
     others = max(lanes - 1, 1)
@@ -954,7 +954,7 @@
             vmem(2, stripe, wb.shape[2]),
             pltpu.VMEM((2, height, stripe), jnp.float32),
             pltpu.VMEM((2, height, stripe), jnp.float32),
-            vmem(pieces - pieces // 2, hot_count, size // pieces, width),
+            vmem(pieces - pieces * 3 // 4, hot_count, size // pieces, width),
             vmem(height, row_n * size),
             vmem(stripe, (line - 2) * lanes * size),
             vmem(got_slots(row_n, col_n), row_n, height, size),

time: 301 us -> 297 us (0.987)
  Pallas kernels: 288 us -> 282 us
    pallas_call x2, Pallas kernels: 202 us -> 197 us  [exchange(): pl.pallas_call(functools.partial(exchange_kernel, row_n, col_n, pieces, h...]
  transfers between devices with their start and end apart: 4 -> 4, of which waited for: 2 -> 2; matrix products, arithmetic and copies ran while one was open for 0% -> 0% of each run, Pallas kernels for 10% -> 11%
where the time goes in v9:
time: 297 us; the launch traced here: 293 us
  Pallas kernels  282 us (95%)
  starting transfers between devices  5.17 us (2%)
    pallas_call x2, Pallas kernels, exchange(): pl.pallas_call(functools.partial(exchange_kernel, row_n, col_n, pieces, h...  197 us
    pallas_call x1, Pallas kernels, filter_step(): pl.pallas_call(functools.partial(filter_kernel, row_n, row_chunk), out_sh...  30.9 us
    pallas_call x1, Pallas kernels, hot_step(): pl.pallas_call(functools.partial(hot_kernel, row_n, hot_count), out_shape...  21.1 us
    pallas_call x1, Pallas kernels, last_step(): pl.pallas_call(last_kernel, out_shape=jax.ShapeDtypeStruct(acc.shape, jnp...  15.8 us
    pallas_call x2, Pallas kernels, dense(): pl.pallas_call(functools.partial(dense_kernel, tile_of), out_shape=jax.Sh...  11.3 us
  transfers between devices with their start and end apart: 4, of which 2 were waited for; matrix products, arithmetic and copies ran while one was open for 0% of the time, Pallas kernels for 11%

profile of v9, /device:TPU:24, one launch (start us, length us, event | category | flops | bytes accessed | tf_op | source)
XLA Modules:
  0.0 292.8 jit_solution(7307182263390568831)
XLA Ops:
  0.6 1.3 copy.9.hot
  2.0 0.7 pad_add_fusion.place
  2.6 5.7 %shard_map.87 = (bf16[2,128,3072]{2,1,0:T(8,128)(2,1)}, bf16[4,1536,128]{2,1,0:T(8,128)(2,1)}) custom-call(s32[2]{0:T(128)} %pad_add_fusion.place, s32[8,2]{1,0:T(8,128)} %copy.9.hot, f32[1536,3072]{1,0:T(8,128)} %refs_9_.1, f32[1536,3072]{1,0:T(8,128)} %refs_9_.1), custom_call_target="tpu_custom_call" | custom-call | tf_op jit(solution)/shard_map/pallas_call | solution.py:81
  8.3 5.2 %shard_map.86 = bf16[1,1536,1024]{2,1,0:T(8,128)(2,1)} custom-call(s32[2]{0:T(128)} %pad_add_fusion.place, s32[3,8,64]{2,1,0:T(8,128)} %pairs.3, s32[8]{0:T(128)} %counts.3, bf16[1,48,128,128]{3,2,1,0:T(8,128)(2,1)} %bitcast.11), custom_call_target="tpu_custom_call" | custom-call | tf_op jit(solution)/shard_map/pallas_call | solution.py:40
  13.5 124.0 %shard_map.88 = (bf16[1024,3072]{1,0:T(8,128)(2,1)}, bf16[16,1536,128]{2,1,0:T(8,128)(2,1)}, bf16[2,48,128,128]{3,2,1,0:T(8,128)(2,1)}, f32[1536,1]{1,0:T(8,128)}, f32[1,3072]{1,0:T(1,128)}) custom-call(s32[8,8]{1,0:T(8,128)} %sel.7, bf16[2,128,3072]{2,1,0:T(8,128)(2,1)} %get-tuple-element.14.rows_ref, bf16[4,1536,128]{2,1,0:T(8,128)(2,1)} %get-tuple-element.15.cols_ref, ...), custom_call_target="tpu_custom_call" | custom-call | tf_op jit(solution)/shard_map/pallas_call | solution.py:993
  137.5 6.1 %shard_map.89.refs_23_.refs_37_.refs_38_.wb_ref.refs_5_ = bf16[2,1536,1024]{2,1,0:T(8,128)(2,1)} custom-call(s32[2]{0:T(128)} %pad_add_fusion.place, s32[3,8,64]{2,1,0:T(8,128)} %pairs.3, s32[8]{0:T(128)} %counts.3, bf16[2,48,128,128]{3,2,1,0:T(8,128)(2,1)} %get-tuple-element.19.ham_ref), custom_call_target="tpu_custom_call" | custom-call | tf_op jit(solution)/shard_map/pallas_call | solution.py:40
  143.7 21.1 %shard_map.90 = (bf16[2,128,3072]{2,1,0:T(8,128)(2,1)}, bf16[4,1536,128]{2,1,0:T(8,128)(2,1)}) custom-call(s32[2]{0:T(128)} %pad_add_fusion.place, s32[8,2]{1,0:T(8,128)} %copy.9.hot, s32[8,8]{1,0:T(8,128)} %sel.7, bf16[1536,1024]{1,0:T(8,128)(2,1)} %bitcast.5, bf16[1536,1024]{1,0:T(8,128)(2,1)} %bitcast.6, f32[1536,3072]{1,0:T(8,128)} %refs_9_.1, ...), custom_call_target="tpu_custom_call" | custom-call | tf_op jit(solution)/shard_map/pallas_call | solution.py:1118
  164.7 1.4 collective-permute-start.3
  166.1 2.4 collective-permute-start.1
  168.5 1.3 collective-permute-start
  169.8 0.1 collective-permute-start.2
  169.9 30.9 %shard_map.91.refs_8_ = f32[1536,3072]{1,0:T(8,128)} custom-call(s32[2]{0:T(128)} %pad_add_fusion.place, s32[8,8]{1,0:T(8,128)} %sel.7, bf16[1536,1024]{1,0:T(8,128)(2,1)} %bitcast.8, bf16[1024,3072]{1,0:T(8,128)(2,1)} %get-tuple-element.22.refs_22_.refs_35_.refs_36_.s_ref, bf16[2,1536,1024]{2,1,0:T(8,128)(2,1)} %shard_map.89.refs_23_.refs_37_.refs_38_.wb_ref.refs_5_, ...), custom_call_target="tpu_custom_call" | custom-call | flops 19327352832 | bytes 56623104 | tf_op jit(solution)/shard_map/pallas_call | solution.py:1182
  200.8 2.4 collective-permute-done.2.refs_2_
  203.2 0.0 collective-permute-done.3.refs_3_
  203.2 0.0 collective-permute-done.1.refs_1_
  203.2 0.5 collective-permute-done.refs_0_
  203.7 73.2 %shard_map.92 = (bf16[256,3072]{1,0:T(8,128)(2,1)}, f32[1536,3072]{1,0:T(8,128)}) custom-call(s32[8,8]{1,0:T(8,128)} %sel.7, bf16[2,128,3072]{2,1,0:T(8,128)(2,1)} %get-tuple-element.21.rows_ref, bf16[4,1536,128]{2,1,0:T(8,128)(2,1)} %get-tuple-element.23.cols_ref, bf16[2,128,3072]{2,1,0:T(8,128)(2,1)} %collective-permute-done.refs_0_, ...), custom_call_target="tpu_custom_call" | custom-call | tf_op jit(solution)/shard_map/pallas_call | solution.py:993
  277.0 15.8 %shard_map.93 = f32[1536,3072]{1,0:T(8,128)} custom-call(s32[2]{0:T(128)} %pad_add_fusion.place, f32[1536,3072]{1,0:T(8,128)} %get-tuple-element.24.acc_ref, bf16[1536,1024]{1,0:T(8,128)(2,1)} %bitcast.10, bf16[256,3072]{1,0:T(8,128)(2,1)} %get-tuple-element.25.s_ref), custom_call_target="tpu_custom_call" | custom-call | tf_op jit(solution)/shard_map/pallas_call | solution.py:1023
Async XLA Ops:
  164.7 38.5 %collective-permute-start.3 = (bf16[2,128,3072]{2,1,0:T(8,128)(2,1)}, bf16[2,128,3072]{2,1,0:T(8,128)(2,1)}, u32[]{:S(2)}, u32[]{:S(2)}) collective-permute-start(bf16[2,128,3072]{2,1,0:T(8,128)(2,1)} %get-tuple-element.21.rows_ref), channel_id=1, source_target_pairs={{0,4},{4,0},{8,12},{12,8},{16,20},{20,16},{24,28},{28,24},{1,5},{5... | collective-permute-start | bytes 4718600 | tf_op jit(solution)/shard_map/ppermute | solution.py:1137
  166.1 37.1 %collective-permute-start.1 = (bf16[2,128,3072]{2,1,0:T(8,128)(2,1)}, bf16[2,128,3072]{2,1,0:T(8,128)(2,1)}, u32[]{:S(2)}, u32[]{:S(2)}) collective-permute-start(bf16[2,128,3072]{2,1,0:T(8,128)(2,1)} %get-tuple-element.21.rows_ref), channel_id=1, source_target_pairs={{8,0},{12,4},{16,8},{20,12},{24,16},{28,20},{9,1},{13,5},{17,9},{2... | collective-permute-start | bytes 4718600 | tf_op jit(solution)/shard_map/ppermute | solution.py:1133
  168.5 35.2 %collective-permute-start = (bf16[2,128,3072]{2,1,0:T(8,128)(2,1)}, bf16[2,128,3072]{2,1,0:T(8,128)(2,1)}, u32[]{:S(2)}, u32[]{:S(2)}) collective-permute-start(bf16[2,128,3072]{2,1,0:T(8,128)(2,1)} %get-tuple-element.21.rows_ref), channel_id=1, source_target_pairs={{0,8},{4,12},{8,16},{12,20},{16,24},{20,28},{1,9},{5,13},{9,17},{1... | collective-permute-start | bytes 4718600 | tf_op jit(solution)/shard_map/ppermute | solution.py:1132
  169.8 33.3 %collective-permute-start.2 = (bf16[4,1536,128]{2,1,0:T(8,128)(2,1)}, bf16[4,1536,128]{2,1,0:T(8,128)(2,1)}, u32[]{:S(2)}, u32[]{:S(2)}) collective-permute-start(bf16[4,1536,128]{2,1,0:T(8,128)(2,1)} %get-tuple-element.23.cols_ref), channel_id=1, source_target_pairs={{0,2},{1,3},{2,0},{3,1},{4,6},{5,7},{6,4},{7,5},{8,10},{9,11},{10,... | collective-permute-start | bytes 4718600 | tf_op jit(solution)/shard_map/ppermute | solution.py:1135

commit v10 on v9

--- a/solution.py
+++ b/solution.py
@@ -670,7 +670,7 @@
             acc_copy(n).start()
             return carry
 
-        def some_stripes(work, turn_n):
+        def some_stripes(work, turn_n, share=share):
             lax.fori_loop(turn_n * share, jnp.minimum(turn_n * share + share, stripes), work, 0)
 
     if fused:
@@ -814,11 +814,13 @@
         for other in range(1, line):
             lanes_came(lax.rem(late + other, line))
 
-        def ending(n, carry):
-            some_stripes(alpha_side, n - half - pieces)
-            return advance(n, carry)
-
-        lax.fori_loop(half + pieces, pieces * line, ending, 0)
+        def ending(turn_n, carry):
+            for u in range(2):
+                advance(half + pieces + 2 * turn_n + u, carry)
+            some_stripes(alpha_side, turn_n, -(-stripes // (pieces // 2)))
+            return carry
+
+        lax.fori_loop(0, (pieces * line - half - pieces) // 2, ending, 0)
         lanes_came(late)
 
         @pl.when(deaf)
@@ -1068,7 +1070,7 @@
     size = cols.shape[-1]
     hot_count = hot.shape[1]
     tile_width = width // ratio
-    stripe = tile_width // 2 if tile_width % 256 == 0 else size
+    stripe = tile_width
     per_tile = tile_width // stripe
     blocks = tile_width // size
     depth = s.shape[0]

time: 297 us -> 292 us (0.983); the launches traced: 293 us -> 292 us
  Pallas kernels: 282 us -> 278 us
  waiting for transfers between devices: 2.92 us -> 6.47 us
    pallas_call x1, Pallas kernels: 21.1 us -> 16.7 us  [hot_step(): pl.pallas_call(functools.partial(hot_kernel, row_n, hot_count), out_shape...]
    ppermute x1, waiting for transfers between devices: 2.39 us -> 5.94 us  [first_hops(): ahead = [below, above, lax.ppermute(cols, 'col', turn)]]
  transfers between devices with their start and end apart: 4 -> 4, of which waited for: 2 -> 2; matrix products, arithmetic and copies ran while one was open for 0% -> 0% of each run, Pallas kernels for 11% -> 10%
where the time goes in v10:
time: 292 us
  Pallas kernels  278 us (95%)
  waiting for transfers between devices  6.47 us (2%)
  starting transfers between devices  4.62 us (2%)
    pallas_call x2, Pallas kernels, exchange(): pl.pallas_call(functools.partial(exchange_kernel, row_n, col_n, pieces, h...  197 us
    pallas_call x1, Pallas kernels, filter_step(): pl.pallas_call(functools.partial(filter_kernel, row_n, row_chunk), out_sh...  30.7 us
    pallas_call x1, Pallas kernels, hot_step(): pl.pallas_call(functools.partial(hot_kernel, row_n, hot_count), out_shape...  16.7 us
    pallas_call x1, Pallas kernels, last_step(): pl.pallas_call(last_kernel, out_shape=jax.ShapeDtypeStruct(acc.shape, jnp...  15.9 us
    pallas_call x2, Pallas kernels, dense(): pl.pallas_call(functools.partial(dense_kernel, tile_of), out_shape=jax.Sh...  12 us
    ppermute x1, waiting for transfers between devices, first_hops(): ahead = [below, above, lax.ppermute(cols, 'col', turn)]  5.94 us
  transfers between devices with their start and end apart: 4, of which 2 were waited for; matrix products, arithmetic and copies ran while one was open for 0% of the time, Pallas kernels for 10%

profile of v10, /device:TPU:24, one launch (start us, length us, event | category | flops | bytes accessed | tf_op | source)
XLA Modules:
  0.0 292.1 jit_solution(4456213237071145345)
XLA Ops:
  0.6 1.3 copy.9.hot
  2.0 0.7 pad_add_fusion.place
  2.6 5.7 %shard_map.87 = (bf16[2,128,3072]{2,1,0:T(8,128)(2,1)}, bf16[4,1536,128]{2,1,0:T(8,128)(2,1)}) custom-call(s32[2]{0:T(128)} %pad_add_fusion.place, s32[8,2]{1,0:T(8,128)} %copy.9.hot, f32[1536,3072]{1,0:T(8,128)} %refs_9_.1, f32[1536,3072]{1,0:T(8,128)} %refs_9_.1), custom_call_target="tpu_custom_call" | custom-call | tf_op jit(solution)/shard_map/pallas_call | solution.py:81
  8.3 5.0 %shard_map.86 = bf16[1,1536,1024]{2,1,0:T(8,128)(2,1)} custom-call(s32[2]{0:T(128)} %pad_add_fusion.place, s32[3,8,64]{2,1,0:T(8,128)} %pairs.3, s32[8]{0:T(128)} %counts.3, bf16[1,48,128,128]{3,2,1,0:T(8,128)(2,1)} %bitcast.11), custom_call_target="tpu_custom_call" | custom-call | tf_op jit(solution)/shard_map/pallas_call | solution.py:40
  13.3 124.3 %shard_map.88 = (bf16[1024,3072]{1,0:T(8,128)(2,1)}, bf16[16,1536,128]{2,1,0:T(8,128)(2,1)}, bf16[2,48,128,128]{3,2,1,0:T(8,128)(2,1)}, f32[1536,1]{1,0:T(8,128)}, f32[1,3072]{1,0:T(1,128)}) custom-call(s32[8,8]{1,0:T(8,128)} %sel.7, bf16[2,128,3072]{2,1,0:T(8,128)(2,1)} %get-tuple-element.14.rows_ref, bf16[4,1536,128]{2,1,0:T(8,128)(2,1)} %get-tuple-element.15.cols_ref, ...), custom_call_target="tpu_custom_call" | custom-call | tf_op jit(solution)/shard_map/pallas_call | solution.py:995
  137.6 7.0 %shard_map.89.refs_23_.refs_37_.refs_38_.wb_ref.refs_5_ = bf16[2,1536,1024]{2,1,0:T(8,128)(2,1)} custom-call(s32[2]{0:T(128)} %pad_add_fusion.place, s32[3,8,64]{2,1,0:T(8,128)} %pairs.3, s32[8]{0:T(128)} %counts.3, bf16[2,48,128,128]{3,2,1,0:T(8,128)(2,1)} %get-tuple-element.19.ham_ref), custom_call_target="tpu_custom_call" | custom-call | tf_op jit(solution)/shard_map/pallas_call | solution.py:40
  144.6 16.7 %shard_map.90 = (bf16[2,128,3072]{2,1,0:T(8,128)(2,1)}, bf16[4,1536,128]{2,1,0:T(8,128)(2,1)}) custom-call(s32[2]{0:T(128)} %pad_add_fusion.place, s32[8,2]{1,0:T(8,128)} %copy.9.hot, s32[8,8]{1,0:T(8,128)} %sel.7, bf16[1536,1024]{1,0:T(8,128)(2,1)} %bitcast.5, bf16[1536,1024]{1,0:T(8,128)(2,1)} %bitcast.6, f32[1536,3072]{1,0:T(8,128)} %refs_9_.1, ...), custom_call_target="tpu_custom_call" | custom-call | tf_op jit(solution)/shard_map/pallas_call | solution.py:1120
  161.3 0.8 collective-permute-start.3
  162.1 2.4 collective-permute-start.1
  164.5 1.3 collective-permute-start
  165.8 0.1 collective-permute-start.2
  165.9 30.7 %shard_map.91.refs_8_ = f32[1536,3072]{1,0:T(8,128)} custom-call(s32[2]{0:T(128)} %pad_add_fusion.place, s32[8,8]{1,0:T(8,128)} %sel.7, bf16[1536,1024]{1,0:T(8,128)(2,1)} %bitcast.8, bf16[1024,3072]{1,0:T(8,128)(2,1)} %get-tuple-element.22.refs_22_.refs_35_.refs_36_.s_ref, bf16[2,1536,1024]{2,1,0:T(8,128)(2,1)} %shard_map.89.refs_23_.refs_37_.refs_38_.wb_ref.refs_5_, ...), custom_call_target="tpu_custom_call" | custom-call | flops 19327352832 | bytes 56623104 | tf_op jit(solution)/shard_map/pallas_call | solution.py:1184
  196.6 5.9 %collective-permute-done.2.refs_2_ = bf16[4,1536,128]{2,1,0:T(8,128)(2,1)} collective-permute-done((bf16[4,1536,128]{2,1,0:T(8,128)(2,1)}, bf16[4,1536,128]{2,1,0:T(8,128)(2,1)}, u32[]{:S(2)}, u32[]{:S(2)}) %collective-permute-start.2) | collective-permute-done | bytes 1572896 | tf_op jit(solution)/shard_map/ppermute | solution.py:1137
  202.5 0.0 collective-permute-done.3.refs_3_
  202.5 0.0 collective-permute-done.1.refs_1_
  202.5 0.5 collective-permute-done.refs_0_
  203.0 73.1 %shard_map.92 = (bf16[256,3072]{1,0:T(8,128)(2,1)}, f32[1536,3072]{1,0:T(8,128)}) custom-call(s32[8,8]{1,0:T(8,128)} %sel.7, bf16[2,128,3072]{2,1,0:T(8,128)(2,1)} %get-tuple-element.21.rows_ref, bf16[4,1536,128]{2,1,0:T(8,128)(2,1)} %get-tuple-element.23.cols_ref, bf16[2,128,3072]{2,1,0:T(8,128)(2,1)} %collective-permute-done.refs_0_, ...), custom_call_target="tpu_custom_call" | custom-call | tf_op jit(solution)/shard_map/pallas_call | solution.py:995
  276.2 15.9 %shard_map.93 = f32[1536,3072]{1,0:T(8,128)} custom-call(s32[2]{0:T(128)} %pad_add_fusion.place, f32[1536,3072]{1,0:T(8,128)} %get-tuple-element.24.acc_ref, bf16[1536,1024]{1,0:T(8,128)(2,1)} %bitcast.10, bf16[256,3072]{1,0:T(8,128)(2,1)} %get-tuple-element.25.s_ref), custom_call_target="tpu_custom_call" | custom-call | tf_op jit(solution)/shard_map/pallas_call | solution.py:1025
Async XLA Ops:
  161.3 41.2 %collective-permute-start.3 = (bf16[2,128,3072]{2,1,0:T(8,128)(2,1)}, bf16[2,128,3072]{2,1,0:T(8,128)(2,1)}, u32[]{:S(2)}, u32[]{:S(2)}) collective-permute-start(bf16[2,128,3072]{2,1,0:T(8,128)(2,1)} %get-tuple-element.21.rows_ref), channel_id=1, source_target_pairs={{0,4},{4,0},{8,12},{12,8},{16,20},{20,16},{24,28},{28,24},{1,5},{5... | collective-permute-start | bytes 4718600 | tf_op jit(solution)/shard_map/ppermute | solution.py:1139
  162.1 40.4 %collective-permute-start.1 = (bf16[2,128,3072]{2,1,0:T(8,128)(2,1)}, bf16[2,128,3072]{2,1,0:T(8,128)(2,1)}, u32[]{:S(2)}, u32[]{:S(2)}) collective-permute-start(bf16[2,128,3072]{2,1,0:T(8,128)(2,1)} %get-tuple-element.21.rows_ref), channel_id=1, source_target_pairs={{8,0},{12,4},{16,8},{20,12},{24,16},{28,20},{9,1},{13,5},{17,9},{2... | collective-permute-start | bytes 4718600 | tf_op jit(solution)/shard_map/ppermute | solution.py:1135
  164.5 38.5 %collective-permute-start = (bf16[2,128,3072]{2,1,0:T(8,128)(2,1)}, bf16[2,128,3072]{2,1,0:T(8,128)(2,1)}, u32[]{:S(2)}, u32[]{:S(2)}) collective-permute-start(bf16[2,128,3072]{2,1,0:T(8,128)(2,1)} %get-tuple-element.21.rows_ref), channel_id=1, source_target_pairs={{0,8},{4,12},{8,16},{12,20},{16,24},{20,28},{1,9},{5,13},{9,17},{1... | collective-permute-start | bytes 4718600 | tf_op jit(solution)/shard_map/ppermute | solution.py:1134
  165.8 36.7 %collective-permute-start.2 = (bf16[4,1536,128]{2,1,0:T(8,128)(2,1)}, bf16[4,1536,128]{2,1,0:T(8,128)(2,1)}, u32[]{:S(2)}, u32[]{:S(2)}) collective-permute-start(bf16[4,1536,128]{2,1,0:T(8,128)(2,1)} %get-tuple-element.23.cols_ref), channel_id=1, source_target_pairs={{0,2},{1,3},{2,0},{3,1},{4,6},{5,7},{6,4},{7,5},{8,10},{9,11},{10,... | collective-permute-start | bytes 4718600 | tf_op jit(solution)/shard_map/ppermute | solution.py:1137

commit v11 on v10

--- a/solution.py
+++ b/solution.py
@@ -56,18 +56,18 @@
 
 def pack(x, place, hot, row_count, ratio, size):
     height, width = x.shape
-    hot_count = hot.shape[1]
+    hot_count = hot.shape[0]
     blocks = width // (ratio * size)
     part = width // ratio
 
     def row_block(n, place, hot):
         n = jnp.minimum(n, ratio * hot_count - 1)
-        return (hot[place[0], n // ratio], n % ratio)
+        return (hot[n // ratio, place[0]], n % ratio)
 
     def col_block(n, place, hot):
         n = jnp.minimum(n, ratio * hot_count - 1)
         tile, which = n // hot_count, n % hot_count
-        return (0, tile * blocks + hot[place[1] * ratio + tile, which])
+        return (0, tile * blocks + hot[which, place[1] * ratio + tile])
 
     grid_spec = pltpu.PrefetchScalarGridSpec(
         num_scalar_prefetch=2,
@@ -172,7 +172,7 @@
     if fused:
         below_ref, above_ref, chip_ref = some(3)
         side_refs = some(layout(row_n, col_n)[1] - 1)
-        wa_hbm, wb_hbm, rd_ref, cd_ref, x_hbm, start_hbm, s_out, acc_out = some(8)
+        w_hbm, rd_ref, cd_ref, x_hbm, start_hbm, s_out, acc_out = some(7)
     else:
         ham_ref, diag_ref, s_out, c_out, h_out, rd_out, cd_out = some(7)
     held, lane_buf, turn_buf, s_all, c_all = some(5)
@@ -363,6 +363,8 @@
                         act(chip)
 
         take_ham.wait()
+        put_own = pltpu.make_async_copy(ham_buf, h_out.at[ratio], ham_sem.at[1])
+        put_own.start()
         for i in range(ratio):
             _, home_lane = tile_place(g.col, i)
 
@@ -585,7 +587,7 @@
         rows_at_once = height // 2
         share = -(-stripes // pieces)
         late = late_slot(at, line)
-        take_wa = pltpu.make_async_copy(wa_hbm, wa, load_sem.at[0])
+        take_wa = pltpu.make_async_copy(w_hbm.at[ratio], wa, load_sem.at[0])
         early = line - 1
         first_early = jnp.where(late == 0, 1, 0)
         depth = pl.ds(pl.multiple_of(first_early * lanes * size, lanes * size), early * lanes * size)
@@ -598,7 +600,7 @@
             return [
                 pltpu.make_async_copy(x_hbm.at[:, band(n)], x_buf.at[turn_n], x_sem.at[turn_n]),
                 pltpu.make_async_copy(start_hbm.at[:, band(n)], start_buf.at[turn_n], start_sem.at[turn_n]),
-                pltpu.make_async_copy(wb_hbm.at[n // per_tile, band(lax.rem(n, per_tile)), :], wb_buf.at[turn_n], wb_sem.at[turn_n]),
+                pltpu.make_async_copy(w_hbm.at[n // per_tile, band(lax.rem(n, per_tile)), :], wb_buf.at[turn_n], wb_sem.at[turn_n]),
             ]
 
         def acc_copy(n):
@@ -891,6 +893,7 @@
             for step in range(g.chips):
                 core_copy(step, b).wait_send()
     if not fused:
+        put_own.wait()
         for i in range(ratio):
             _, home_lane = tile_place(g.col, i)
 
@@ -941,10 +944,10 @@
     args = [sel, rows, cols]
     in_specs = [pl.BlockSpec(memory_space=pltpu.SMEM), anywhere, anywhere]
     if fused:
-        wa, wb, rd, cd, x, start = product
+        w, rd, cd, x, start = product
         stripe = 256 if height % 256 == 0 else size
-        args += list(ahead) + [wa, wb, rd, cd, x, start]
-        in_specs += [anywhere] * (len(ahead) + 2) + [whole] * 2 + [anywhere] * 2
+        args += list(ahead) + [w, rd, cd, x, start]
+        in_specs += [anywhere] * (len(ahead) + 1) + [whole] * 2 + [anywhere] * 2
         out_shape = [
             jax.ShapeDtypeStruct((lanes * size, width), jnp.bfloat16),
             jax.ShapeDtypeStruct((height, width), jnp.float32),
@@ -952,8 +955,8 @@
         out_specs = [anywhere] * 2
         scratch += [
             pltpu.VMEM((height, width), jnp.float32),
-            vmem(*wa.shape),
-            vmem(2, stripe, wb.shape[2]),
+            vmem(*w.shape[1:]),
+            vmem(2, stripe, w.shape[2]),
             pltpu.VMEM((2, height, stripe), jnp.float32),
             pltpu.VMEM((2, height, stripe), jnp.float32),
             vmem(pieces - pieces * 3 // 4, hot_count, size // pieces, width),
@@ -975,7 +978,7 @@
         out_shape = [
             jax.ShapeDtypeStruct((row_n * size, width), jnp.bfloat16),
             jax.ShapeDtypeStruct((col_n * block_n, height, size), jnp.bfloat16),
-            jax.ShapeDtypeStruct((ratio,) + ham.shape, ham.dtype),
+            jax.ShapeDtypeStruct((ratio + 1,) + ham.shape, ham.dtype),
             jax.ShapeDtypeStruct((height, 1), jnp.float32),
             jax.ShapeDtypeStruct((1, width), jnp.float32),
         ]
@@ -983,7 +986,7 @@
         scratch += [
             pltpu.VMEM(ham.shape, ham.dtype),
             pltpu.VMEM(ham.shape, ham.dtype),
-            dma((1,)),
+            dma((2,)),
             dma((ratio, pieces)),
             dma((ratio, pieces)),
             dma((ratio, pieces)),
@@ -1007,7 +1010,7 @@
     out_ref[...] = acc * (2.0 / half_width)
 
 
-def last_step(place, acc, wa, s, row_n, col_n):
+def last_step(place, acc, w, s, row_n, col_n):
     height, width = acc.shape
     depth = s.shape[0]
     line, lanes, _, _ = layout(row_n, col_n)
@@ -1017,7 +1020,7 @@
         grid=(width // stripe,),
         in_specs=[
             pl.BlockSpec((height, stripe), lambda n, place: (0, n)),
-            pl.BlockSpec((height, depth), lambda n, place: (0, late_slot(place[0] // lanes, line))),
+            pl.BlockSpec((None, height, depth), lambda n, place: (row_n // col_n, 0, late_slot(place[0] // lanes, line))),
             pl.BlockSpec((depth, stripe), lambda n, place: (0, n)),
         ],
         out_specs=pl.BlockSpec((height, stripe), lambda n, place: (0, n)),
@@ -1027,7 +1030,7 @@
         out_shape=jax.ShapeDtypeStruct(acc.shape, jnp.float32),
         grid_spec=grid_spec,
         compiler_params=pltpu.CompilerParams(vmem_limit_bytes=VMEM_LIMIT),
-    )(place, acc, wa, s)
+    )(place, acc, w, s)
 
 
 def hot_kernel(row_n, hot_count, place, hot, sel, *refs):
@@ -1065,10 +1068,10 @@
         cols_ref[h] = (value * scale).astype(cols_ref.dtype)
 
 
-def hot_step(place, hot, sel, wa, s, wb, rd, cd, cols, x, row_n, ratio):
+def hot_step(place, hot, sel, w, s, rd, cd, cols, x, row_n, ratio):
     height, width = x.shape
     size = cols.shape[-1]
-    hot_count = hot.shape[1]
+    hot_count = hot.shape[0]
     tile_width = width // ratio
     stripe = tile_width
     per_tile = tile_width // stripe
@@ -1079,17 +1082,17 @@
         return jnp.minimum(n // per_tile, ratio - 1)
 
     def hot_row(h, place, hot):
-        return hot[place[0], h]
+        return hot[h, place[0]]
 
     def hot_col(h, n, place, hot):
-        return hot[place[1] * ratio + tile(n), h]
+        return hot[h, place[1] * ratio + tile(n)]
 
     def source(q, n, place, sel):
         return q * hot_count + sel[place[1] * ratio + tile(n), q]
 
     spec = pl.BlockSpec
     each = range(hot_count)
-    in_specs = [spec((size, depth), lambda n, place, hot, sel, h=h: (hot_row(h, place, hot), 0)) for h in each]
+    in_specs = [spec((None, size, depth), lambda n, place, hot, sel, h=h: (ratio, hot_row(h, place, hot), 0)) for h in each]
     in_specs += [spec((size, stripe), lambda n, place, hot, sel, h=h: (hot_row(h, place, hot), n)) for h in each]
     in_specs += [spec((size, 1), lambda n, place, hot, sel, h=h: (hot_row(h, place, hot), 0)) for h in each]
     in_specs += [spec((1, size, size), lambda n, place, hot, sel, h=h, q=q: (source(q, n, place, sel), hot_row(h, place, hot), 0))
@@ -1098,7 +1101,7 @@
         spec((depth, stripe), lambda n, *_: (0, n)),
         spec((1, stripe, depth), lambda n, *_: (n // per_tile, n % per_tile, 0)),
         spec((1, stripe), lambda n, *_: (0, n)),
-        spec((stripe, depth), lambda n, *_: (n % per_tile, 0)),
+        spec((None, stripe, depth), lambda n, *_: (ratio, n % per_tile, 0)),
         spec((stripe, 1), lambda n, *_: (n % per_tile, 0)),
     ]
     in_specs += [spec((1, stripe, size), lambda n, place, hot, sel, q=q: (source(q, n, place, sel), n % per_tile, 0)) for q in range(row_n)]
@@ -1106,8 +1109,8 @@
     in_specs += [spec((1, size, depth), lambda n, place, hot, sel, h=h: (tile(n), hot_col(h, n, place, hot), 0)) for h in each]
     in_specs += [spec((stripe, size), lambda n, place, hot, sel, h=h: (n % per_tile, tile(n) * blocks + hot_col(h, n, place, hot))) for h in each]
     in_specs += [spec((1, size), lambda n, place, hot, sel, h=h: (0, tile(n) * blocks + hot_col(h, n, place, hot))) for h in each]
-    args = [wa] * hot_count + [x] * hot_count + [rd] * hot_count + [cols] * (hot_count * row_n)
-    args += [s, wb, cd, wa, rd] + [cols] * row_n + [s] * hot_count + [wb] * hot_count + [x] * hot_count + [cd] * hot_count
+    args = [w] * hot_count + [x] * hot_count + [rd] * hot_count + [cols] * (hot_count * row_n)
+    args += [s, w, cd, w, rd] + [cols] * row_n + [s] * hot_count + [w] * hot_count + [x] * hot_count + [cd] * hot_count
     grid_spec = pltpu.PrefetchScalarGridSpec(
         num_scalar_prefetch=3,
         grid=(width // stripe,),
@@ -1156,7 +1159,7 @@
     lax.fori_loop(0, x_ref.shape[0] // row_chunk, chunk, 0)
 
 
-def filter_step(place, sel, wa, s, wb, rd, cd, cols, x, row_n, ratio):
+def filter_step(place, sel, w, s, rd, cd, cols, x, row_n, ratio):
     height, width = x.shape
     size = cols.shape[-1]
     hot_count = cols.shape[0] // row_n
@@ -1172,13 +1175,13 @@
 
     striped = pl.BlockSpec((height, stripe), lambda n, *_: (0, n))
     in_specs = [
-        pl.BlockSpec(wa.shape, lambda n, *_: (0, 0)),
+        pl.BlockSpec((None,) + w.shape[1:], lambda n, *_: (ratio, 0, 0)),
         pl.BlockSpec((s.shape[0], stripe), lambda n, *_: (0, n)),
-        pl.BlockSpec((1, stripe, wb.shape[2]), lambda n, *_: (n // per_tile, n % per_tile, 0)),
+        pl.BlockSpec((1, stripe, w.shape[2]), lambda n, *_: (n // per_tile, n % per_tile, 0)),
         pl.BlockSpec((height, 1), lambda n, *_: (0, 0)),
         pl.BlockSpec((1, stripe), lambda n, *_: (0, n)),
     ] + [b_spec(q) for q in range(row_n)] + [striped]
-    args = [wa, s, wb, rd, cd] + [cols] * row_n + [x]
+    args = [w, s, w, rd, cd] + [cols] * row_n + [x]
     grid_spec = pltpu.PrefetchScalarGridSpec(
         num_scalar_prefetch=2, grid=(width // stripe,), in_specs=in_specs, out_specs=striped)
     return pl.pallas_call(
@@ -1199,16 +1202,16 @@
     size = ham_blocks.shape[1]
     place = jnp.stack([lax.axis_index("row"), lax.axis_index("col")]).astype(jnp.int32)
     shape = (height, row_n * size)
-    rows, cols = pack(start_vector, place, hot_blocks, row_n, ratio, size)
+    hot = hot_blocks.T
+    rows, cols = pack(start_vector, place, hot, row_n, ratio, size)
     s, b, hams, rd, cd = exchange(rows, cols, selection, row_n, col_n, 0, ham=ham_blocks, diagonal=diagonal)
-    wa = dense(ham_blocks[None], place, pair_lists, pair_counts, shape, lambda place, i: place[0])[0]
-    wb = dense(hams, place, pair_lists, pair_counts, shape, lambda place, i: place[1] * ratio + i)
-    rows, cols = hot_step(place, hot_blocks, selection, wa, s, wb, rd, cd, b, start_vector, row_n, ratio)
+    w = dense(hams, place, pair_lists, pair_counts, shape, lambda place, i: jnp.where(i < ratio, place[1] * ratio + i, place[0]))
+    rows, cols = hot_step(place, hot, selection, w, s, rd, cd, b, start_vector, row_n, ratio)
     ahead = first_hops(rows, cols, row_n, col_n)
     s, _ = lax.optimization_barrier((s, rows))
-    first = filter_step(place, selection, wa, s, wb, rd, cd, b, start_vector, row_n, ratio)
-    s, acc = exchange(rows, cols, selection, row_n, col_n, 1, ahead=ahead, product=(wa, wb, rd, cd, first, start_vector))
-    return (first, last_step(place, acc, wa, s, row_n, col_n))
+    first = filter_step(place, selection, w, s, rd, cd, b, start_vector, row_n, ratio)
+    s, acc = exchange(rows, cols, selection, row_n, col_n, 1, ahead=ahead, product=(w, rd, cd, first, start_vector))
+    return (first, last_step(place, acc, w, s, row_n, col_n))
 
 
 def solution(mesh):

time: 292 us -> 291 us (level)
  starting transfers between devices: 4.62 us -> 7.94 us
  Pallas kernels: 278 us -> 275 us
    ppermute x1, starting transfers between devices: 0.84 us -> 4.15 us  [first_hops(): lax.ppermute(rows, 'row', [(r, r // lanes * lanes + (r + step) % lanes) f...]
    pallas_call x2 -> x1, Pallas kernels: 12 us -> 9.17 us  [dense(): pl.pallas_call(functools.partial(dense_kernel, tile_of), out_shape=jax.Sh...]
  transfers between devices with their start and end apart: 4 -> 4, of which waited for: 2 -> 2; matrix products, arithmetic and copies ran while one was open for 0% -> 0% of each run, Pallas kernels for 10% -> 11%
where the time goes in v11:
time: 291 us; the launch traced here: 290 us
  Pallas kernels  275 us (95%)
  starting transfers between devices  7.94 us (3%)
  waiting for transfers between devices  5.99 us (2%)
    pallas_call x2, Pallas kernels, exchange(): pl.pallas_call(functools.partial(exchange_kernel, row_n, col_n, pieces, h...  196 us
    pallas_call x1, Pallas kernels, filter_step(): pl.pallas_call(functools.partial(filter_kernel, row_n, row_chunk), out_sh...  30.7 us
    pallas_call x1, Pallas kernels, hot_step(): pl.pallas_call(functools.partial(hot_kernel, row_n, hot_count), out_shape...  16.8 us
    pallas_call x1, Pallas kernels, last_step(): pl.pallas_call(last_kernel, out_shape=jax.ShapeDtypeStruct(acc.shape, jnp...  15.8 us
    pallas_call x1, Pallas kernels, dense(): pl.pallas_call(functools.partial(dense_kernel, tile_of), out_shape=jax.Sh...  9.17 us
  transfers between devices with their start and end apart: 4, of which 2 were waited for; matrix products, arithmetic and copies ran while one was open for 0% of the time, Pallas kernels for 11%

profile of v11, /device:TPU:24, one launch (start us, length us, event | category | flops | bytes accessed | tf_op | source)
XLA Modules:
  0.0 289.8 jit_solution(17476247157298428197)
XLA Ops:
  0.6 0.6 pad_add_fusion.place
  1.3 5.6 %shard_map.86 = (bf16[2,128,3072]{2,1,0:T(8,128)(2,1)}, bf16[4,1536,128]{2,1,0:T(8,128)(2,1)}) custom-call(s32[2]{0:T(128)} %pad_add_fusion.place, s32[2,8]{1,0:T(2,128)} %bitcast.5, f32[1536,3072]{1,0:T(8,128)} %refs_8_.3, f32[1536,3072]{1,0:T(8,128)} %refs_8_.3), custom_call_target="tpu_custom_call" | custom-call | tf_op jit(solution)/shard_map/pallas_call | solution.py:81
  6.9 124.0 %shard_map.87 = (bf16[1024,3072]{1,0:T(8,128)(2,1)}, bf16[16,1536,128]{2,1,0:T(8,128)(2,1)}, bf16[3,48,128,128]{3,2,1,0:T(8,128)(2,1)}, f32[1536,1]{1,0:T(8,128)}, f32[1,3072]{1,0:T(1,128)}) custom-call(s32[8,8]{1,0:T(8,128)} %sel.7, bf16[2,128,3072]{2,1,0:T(8,128)(2,1)} %get-tuple-element.14.rows_ref, bf16[4,1536,128]{2,1,0:T(8,128)(2,1)} %get-tuple-element.15.cols_ref, ...), custom_call_target="tpu_custom_call" | custom-call | tf_op jit(solution)/shard_map/pallas_call | solution.py:998
  130.9 9.2 %shard_map.88.refs_0_.refs_1_.refs_23_.refs_25_.refs_37_.refs_38_.wa_ref.wb_ref.refs_4_ = bf16[3,1536,1024]{2,1,0:T(8,128)(2,1)} custom-call(s32[2]{0:T(128)} %pad_add_fusion.place, s32[3,8,64]{2,1,0:T(8,128)} %pairs.1, s32[8]{0:T(128)} %counts.1, bf16[3,48,128,128]{3,2,1,0:T(8,128)(2,1)} %get-tuple-element.16.ham_ref), custom_call_target="tpu_custom_call" | custom-call | tf_op jit(solution)/shard_map/pallas_call | solution.py:40
  140.1 16.8 %shard_map.89 = (bf16[2,128,3072]{2,1,0:T(8,128)(2,1)}, bf16[4,1536,128]{2,1,0:T(8,128)(2,1)}) custom-call(s32[2]{0:T(128)} %pad_add_fusion.place, s32[2,8]{1,0:T(2,128)} %bitcast.6, s32[8,8]{1,0:T(8,128)} %sel.7, bf16[3,1536,1024]{2,1,0:T(8,128)(2,1)} %shard_map.88.refs_0_.refs_1_.refs_23_.refs_25_.refs_37_.refs_38_.wa_ref.wb_ref.refs_4_, ...), custom_call_target="tpu_custom_call" | custom-call | tf_op jit(solution)/shard_map/pallas_call | solution.py:1123
  156.9 4.2 %collective-permute-start.3 = (bf16[2,128,3072]{2,1,0:T(8,128)(2,1)}, bf16[2,128,3072]{2,1,0:T(8,128)(2,1)}, u32[]{:S(2)}, u32[]{:S(2)}) collective-permute-start(bf16[2,128,3072]{2,1,0:T(8,128)(2,1)} %get-tuple-element.21.rows_ref), channel_id=1, source_target_pairs={{0,4},{4,0},{8,12},{12,8},{16,20},{20,16},{24,28},{28,24},{1,5},{5... | collective-permute-start | bytes 4718600 | tf_op jit(solution)/shard_map/ppermute | solution.py:1142
  161.1 2.4 collective-permute-start.1
  163.5 1.3 collective-permute-start
  164.8 0.1 collective-permute-start.2
  164.9 30.7 %shard_map.90.refs_7_ = f32[1536,3072]{1,0:T(8,128)} custom-call(s32[2]{0:T(128)} %pad_add_fusion.place, s32[8,8]{1,0:T(8,128)} %sel.7, bf16[3,1536,1024]{2,1,0:T(8,128)(2,1)} %shard_map.88.refs_0_.refs_1_.refs_23_.refs_25_.refs_37_.refs_38_.wa_ref.wb_ref.refs_4_, bf16[1024,3072]{1,0:T(8,128)(2,1)} %get-tuple-element.22.refs_22_.refs_35_.refs_36_.s_ref, ...), custom_call_target="tpu_custom_call" | custom-call | flops 19327352832 | bytes 56623104 | tf_op jit(solution)/shard_map/pallas_call | solution.py:1187
  195.5 5.5 %collective-permute-done.2.refs_2_ = bf16[4,1536,128]{2,1,0:T(8,128)(2,1)} collective-permute-done((bf16[4,1536,128]{2,1,0:T(8,128)(2,1)}, bf16[4,1536,128]{2,1,0:T(8,128)(2,1)}, u32[]{:S(2)}, u32[]{:S(2)}) %collective-permute-start.2) | collective-permute-done | bytes 1572896 | tf_op jit(solution)/shard_map/ppermute | solution.py:1140
  201.0 0.0 collective-permute-done.3.refs_3_
  201.0 0.0 collective-permute-done.1.refs_1_
  201.0 0.5 collective-permute-done.refs_0_
  201.5 72.5 %shard_map.91 = (bf16[256,3072]{1,0:T(8,128)(2,1)}, f32[1536,3072]{1,0:T(8,128)}) custom-call(s32[8,8]{1,0:T(8,128)} %sel.7, bf16[2,128,3072]{2,1,0:T(8,128)(2,1)} %get-tuple-element.21.rows_ref, bf16[4,1536,128]{2,1,0:T(8,128)(2,1)} %get-tuple-element.23.cols_ref, bf16[2,128,3072]{2,1,0:T(8,128)(2,1)} %collective-permute-done.refs_0_, ...), custom_call_target="tpu_custom_call" | custom-call | tf_op jit(solution)/shard_map/pallas_call | solution.py:998
  274.0 15.8 %shard_map.92 = f32[1536,3072]{1,0:T(8,128)} custom-call(s32[2]{0:T(128)} %pad_add_fusion.place, f32[1536,3072]{1,0:T(8,128)} %get-tuple-element.24.acc_ref, bf16[3,1536,1024]{2,1,0:T(8,128)(2,1)} %shard_map.88.refs_0_.refs_1_.refs_23_.refs_25_.refs_37_.refs_38_.wa_ref.wb_ref.refs_4_, bf16[256,3072]{1,0:T(8,128)(2,1)} %get-tuple-element.25.s_ref), custom_call_target="tpu_custom_call" | custom-call | tf_op jit(solution)/shard_map/pallas_call | solution.py:1028
Async XLA Ops:
  156.9 44.1 %collective-permute-start.3 = (bf16[2,128,3072]{2,1,0:T(8,128)(2,1)}, bf16[2,128,3072]{2,1,0:T(8,128)(2,1)}, u32[]{:S(2)}, u32[]{:S(2)}) collective-permute-start(bf16[2,128,3072]{2,1,0:T(8,128)(2,1)} %get-tuple-element.21.rows_ref), channel_id=1, source_target_pairs={{0,4},{4,0},{8,12},{12,8},{16,20},{20,16},{24,28},{28,24},{1,5},{5... | collective-permute-start | bytes 4718600 | tf_op jit(solution)/shard_map/ppermute | solution.py:1142
  161.1 39.9 %collective-permute-start.1 = (bf16[2,128,3072]{2,1,0:T(8,128)(2,1)}, bf16[2,128,3072]{2,1,0:T(8,128)(2,1)}, u32[]{:S(2)}, u32[]{:S(2)}) collective-permute-start(bf16[2,128,3072]{2,1,0:T(8,128)(2,1)} %get-tuple-element.21.rows_ref), channel_id=1, source_target_pairs={{8,0},{12,4},{16,8},{20,12},{24,16},{28,20},{9,1},{13,5},{17,9},{2... | collective-permute-start | bytes 4718600 | tf_op jit(solution)/shard_map/ppermute | solution.py:1138
  163.5 38.0 %collective-permute-start = (bf16[2,128,3072]{2,1,0:T(8,128)(2,1)}, bf16[2,128,3072]{2,1,0:T(8,128)(2,1)}, u32[]{:S(2)}, u32[]{:S(2)}) collective-permute-start(bf16[2,128,3072]{2,1,0:T(8,128)(2,1)} %get-tuple-element.21.rows_ref), channel_id=1, source_target_pairs={{0,8},{4,12},{8,16},{12,20},{16,24},{20,28},{1,9},{5,13},{9,17},{1... | collective-permute-start | bytes 4718600 | tf_op jit(solution)/shard_map/ppermute | solution.py:1137
  164.8 36.2 %collective-permute-start.2 = (bf16[4,1536,128]{2,1,0:T(8,128)(2,1)}, bf16[4,1536,128]{2,1,0:T(8,128)(2,1)}, u32[]{:S(2)}, u32[]{:S(2)}) collective-permute-start(bf16[4,1536,128]{2,1,0:T(8,128)(2,1)} %get-tuple-element.23.cols_ref), channel_id=1, source_target_pairs={{0,2},{1,3},{2,0},{3,1},{4,6},{5,7},{6,4},{7,5},{8,10},{9,11},{10,... | collective-permute-start | bytes 4718600 | tf_op jit(solution)/shard_map/ppermute | solution.py:1140
